TPU v7x, 128 devices: a whole 4x4x4 slice. The times are simulated.
128 devices in a mesh: row: 16 (over x, z_lo, core), col: 8 (over y, z_hi).
Axes of the slice: x: 4, y: 4, z: 4 (z_hi: 2, z_lo: 2; z = z_hi * 2 + z_lo), core: 2. Of those that a mesh axis runs over, the one named last changes fastest.
Arguments:
- hidden: bfloat16 [8192, 2048], P('col', 'row'), may hold values from -6 to 6
- lengths: int32 [64], replicated, may hold values from 16 to 128, as said below
- square_matrix_shards: float32 [7, 2048, 2048], P(None, ('row', 'col')), may hold values from -0.125 to 0.125
- channel_mix_shards: float32 [2, 2048, 8192], P(None, ('row', 'col')), may hold values from -0.09375 to 0.09375
- lowrank_down: bfloat16 [2, 2048, 96], replicated, may hold values from -0.125 to 0.125
- lowrank_up: bfloat16 [2, 96, 2048], replicated, may hold values from -0.625 to 0.625
- token_shift_weights: float32 [9, 2048], replicated, may hold values from 0 to 1
- attention_coefficients: float32 [6, 2048], replicated, may hold values from -8 to 2, as said below
- norm_parameters: float32 [6, 2048], P(None, 'row'), may hold values from 0.25 to 1.75
Outputs:
- out_hidden: bfloat16 [8192, 2048], P('col', 'row')
- next_rkv: bfloat16 [3, 8192, 2048], P(None, 'row', 'col')
- final_state: float32 [64, 32, 4096], P('row', 'col')
Inputs may be any that keep to these rules, and one draw needn't show every extreme that they name: `lengths`: every prompt length lies between 16 and 128; in every draw at least one prompt has length 128, most are under 41. `attention_coefficients`: row 0 lies in -8 to -1, row 1 in -2 to 2, row 2 in 0.5 to 1.5, row 3 in -1 to 1, row 4 in 0.5 to 1.5, row 5 in -0.5 to 0.5.
All inputs are finite; a program needn't handle non-finite values.
Results may differ from a plain program's by a relative error of at most 0.034.
Values may be sent and summed in bfloat16 or wider, within the bound.
A program may use at most 128 MiB of HBM per device.

v0:
```python
import jax
import jax.numpy as jnp
from jax import lax
from jax.sharding import PartitionSpec as P

MODEL_WIDTH = 2048
ATTENTION_DIM = 64
LMAX = 128
SPAN = 16


def shifted(source):
    grid = source.reshape(-1, LMAX, source.shape[-1])
    before = jnp.concatenate([jnp.zeros_like(grid[:, :1]), grid[:, :-1]], axis=1)
    return before.reshape(source.shape)


def mixed(source, weight):
    wide = source.astype(jnp.float32)
    return (wide + (shifted(wide) - wide) * weight).astype(jnp.bfloat16)


def normed(source, gain, bias):
    totals, squares = lax.psum((jnp.sum(source, axis=-1), jnp.sum(source * source, axis=-1)), "row")
    center = (totals / MODEL_WIDTH)[:, None]
    second = (squares / MODEL_WIDTH)[:, None]
    scaled = (source - center) * lax.rsqrt(second - center * center + 1e-05)
    return (scaled * gain + bias).astype(jnp.bfloat16)


def gather_cols(source):
    return lax.all_gather(source, "col", axis=0, tiled=True)


def row_sums(term_fn, rows):
    return lax.psum_scatter(
        term_fn(jnp.int32(0), rows * lax.axis_size("row")).astype(jnp.bfloat16),
        "row",
        scatter_dimension=0,
        tiled=True,
    ).astype(jnp.float32)


def span_step(
    state, acceptance_gate_entries, key_vecs, value_vecs, decay_logarithm, remove_dir, write_dir
):
    highest = lax.Precision.HIGHEST
    cumul = jnp.cumsum(decay_logarithm, axis=1)
    before = cumul - decay_logarithm
    last = cumul[:, -1]
    pull_t = remove_dir * jnp.exp(before)
    read_t = acceptance_gate_entries * jnp.exp(cumul)
    back = jnp.exp(-cumul)
    write_back = write_dir * back
    key_back = key_vecs * back
    order = jnp.arange(SPAN)
    strict = (order[:, None] > order[None, :]).astype(jnp.float32)
    upto = (order[:, None] >= order[None, :]).astype(jnp.float32)
    mix_write = jnp.einsum("sthk,suhk->shtu", pull_t, write_back, precision=highest) * strict
    mix_key = jnp.einsum("sthk,suhk->shtu", pull_t, key_back, precision=highest) * strict
    rhs_side = jnp.einsum("sthk,shvk->shtv", pull_t, state, precision=highest) + jnp.einsum(
        "shtu,suhv->shtv", mix_key, value_vecs, precision=highest
    )
    system = jnp.eye(SPAN, dtype=jnp.float32) - mix_write
    pulled = jax.scipy.linalg.solve_triangular(system, rhs_side, lower=True, unit_diagonal=True)
    read_write = jnp.einsum("sthk,suhk->shtu", read_t, write_back, precision=highest) * upto
    read_key = jnp.einsum("sthk,suhk->shtu", read_t, key_back, precision=highest) * upto
    output = jnp.einsum("sthk,shvk->sthv", read_t, state, precision=highest)
    output = output + jnp.einsum("shtu,shuv->sthv", read_write, pulled, precision=highest)
    output = output + jnp.einsum("shtu,suhv->sthv", read_key, value_vecs, precision=highest)
    tail = jnp.exp(last[:, None] - cumul)
    new_state = state * jnp.exp(last)[:, :, None, :]
    new_state = new_state + jnp.einsum(
        "shtv,sthk->shvk", pulled, write_dir * tail, precision=highest
    )
    new_state = new_state + jnp.einsum(
        "sthv,sthk->shvk", value_vecs, key_vecs * tail, precision=highest
    )
    return (new_state, output)


def time_core(
    acceptance_gate_entries,
    key_vecs,
    value_vecs,
    decay_lowrank,
    rate_lowrank,
    head_local,
    up_shard_local,
    prompt_lengths,
):
    rows_here, shard_width = acceptance_gate_entries.shape
    decay_input = jnp.tanh(decay_lowrank).astype(jnp.bfloat16)
    decay_logarithm = -0.606531 * jax.nn.sigmoid(
        head_local[0] + jnp.dot(decay_input, up_shard_local[0], preferred_element_type=jnp.float32)
    )
    incontext_rate = jax.nn.sigmoid(
        head_local[1]
        + jnp.dot(
            rate_lowrank.astype(jnp.bfloat16), up_shard_local[1], preferred_element_type=jnp.float32
        )
    )
    prompt_count = rows_here // LMAX
    head_count = shard_width // ATTENTION_DIM

    def split_heads(source):
        return source.reshape(prompt_count, LMAX, head_count, ATTENTION_DIM)

    acceptance_gate_entries = split_heads(acceptance_gate_entries)
    key_vecs = split_heads(key_vecs)
    value_vecs = split_heads(value_vecs)
    decay_logarithm = split_heads(decay_logarithm)
    incontext_rate = split_heads(incontext_rate)
    kappa = key_vecs * head_local[2].reshape(head_count, ATTENTION_DIM)
    kappa_hat = kappa * lax.rsqrt(jnp.sum(kappa * kappa, axis=-1, keepdims=True) + 1e-05)
    present_entries = (jnp.arange(LMAX)[None, :] < prompt_lengths[:, None]).astype(jnp.float32)[
        :, :, None, None
    ]
    remove_dir = -kappa_hat * present_entries
    write_dir = kappa_hat * incontext_rate * present_entries
    present_address_vector = key_vecs * present_entries
    present_payload_vector = value_vecs * present_entries
    block_total = LMAX // SPAN
    stacked = jnp.stack(
        [
            acceptance_gate_entries,
            present_address_vector,
            present_payload_vector,
            decay_logarithm * present_entries,
            remove_dir,
            write_dir,
        ]
    )
    stacked = stacked.reshape(6, prompt_count, block_total, SPAN, head_count, ATTENTION_DIM)

    def advance(block_index, carry):
        state, result_entries = carry
        weight_slices = lax.dynamic_index_in_dim(stacked, block_index, 2, keepdims=False)
        new_state, output = span_step(
            state,
            weight_slices[0],
            weight_slices[1],
            weight_slices[2],
            weight_slices[3],
            weight_slices[4],
            weight_slices[5],
        )
        result_entries = lax.dynamic_update_index_in_dim(result_entries, output, block_index, 1)
        return (new_state, result_entries)

    start_state = jnp.zeros((prompt_count, head_count, ATTENTION_DIM, ATTENTION_DIM), jnp.float32)
    start_out = jnp.zeros((prompt_count, block_total, SPAN, head_count, ATTENTION_DIM), jnp.float32)
    final, result_entries = lax.fori_loop(0, block_total, advance, (start_state, start_out))
    result_entries = result_entries.reshape(prompt_count, LMAX, head_count, ATTENTION_DIM)
    extra_reward_factor = (
        jnp.sum(
            acceptance_gate_entries
            * present_address_vector
            * head_local[3].reshape(head_count, ATTENTION_DIM),
            axis=-1,
            keepdims=True,
        )
        * present_payload_vector
    )
    attention_results = (result_entries + extra_reward_factor) * present_entries
    center = jnp.mean(attention_results, axis=-1, keepdims=True)
    spread = jnp.mean(jnp.square(attention_results - center), axis=-1, keepdims=True)
    grouped = ((attention_results - center) * lax.rsqrt(spread + 0.00064)).reshape(
        rows_here, shard_width
    )
    att = (grouped * head_local[4] + head_local[5]).astype(jnp.bfloat16)
    return (att, final.reshape(prompt_count, head_count, ATTENTION_DIM * ATTENTION_DIM))


def block_products(sources, weights, n_row):
    feat_width = sources[0].shape[1] // n_row

    def add_block(block_index, totals):
        start = block_index * feat_width
        result = []
        for source, weight, total in zip(sources, weights, totals):
            piece = lax.dynamic_slice_in_dim(source, start, feat_width, 1)
            weight_piece = lax.dynamic_slice_in_dim(weight, start, feat_width, 0)
            partial_sum = jnp.dot(piece, weight_piece, preferred_element_type=jnp.float32)
            result.append(
                total
                + lax.optimization_barrier(partial_sum.astype(jnp.bfloat16)).astype(jnp.float32)
            )
        return tuple(result)

    starts = tuple(
        (
            jnp.zeros((source.shape[0], weight.shape[1]), jnp.float32)
            for source, weight in zip(sources, weights)
        )
    )
    return lax.fori_loop(0, n_row, add_block, starts)


def per_device(
    hidden,
    lengths,
    square_matrix_shards,
    channel_mix_shards,
    lowrank_down,
    lowrank_up,
    token_shift_weights,
    attention_coefficients,
    norm_parameters,
):
    n_row = lax.axis_size("row")
    n_col = lax.axis_size("col")
    row_lookup = lax.axis_index("row")
    column_lookup = lax.axis_index("col")
    square_low = square_matrix_shards.astype(jnp.bfloat16)
    mlp_low = channel_mix_shards.astype(jnp.bfloat16)
    relay_part = square_low[4:7]
    next_base = 0
    square = lax.all_to_all(relay_part, "col", split_axis=2, concat_axis=1, tiled=True)
    mlp_group = lax.all_gather(mlp_low, "col", axis=1, tiled=True)
    mlp_weights = lax.all_to_all(mlp_group, "row", split_axis=2, concat_axis=1, tiled=True)
    feature_row = hidden.shape[1]
    row_mix = lax.dynamic_slice_in_dim(
        token_shift_weights, row_lookup * feature_row, feature_row, 1
    )
    resid = hidden.astype(jnp.float32)
    first = normed(resid, norm_parameters[0], norm_parameters[1])
    time_group = lax.all_gather(square_low[0:4], "col", axis=1, tiled=True)
    time_weights = lax.all_to_all(time_group, "row", split_axis=2, concat_axis=1, tiled=True)
    full_features = lax.all_gather(first, "row", axis=1, tiled=True)
    shift_blends = [
        mixed(full_features, token_shift_weights[column_step]) for column_step in range(5)
    ]
    rows_mine = full_features.shape[0]
    shard_width = time_weights.shape[2]
    acceptance_gate_entries, key_vecs, value_vecs, decay_lowrank, rate_lowrank = block_products(
        shift_blends,
        [time_weights[0], time_weights[1], time_weights[2], lowrank_down[0], lowrank_down[1]],
        n_row,
    )
    head_local = lax.dynamic_slice_in_dim(
        attention_coefficients, row_lookup * shard_width, shard_width, 1
    )
    up_shard_local = lax.dynamic_slice_in_dim(lowrank_up, row_lookup * shard_width, shard_width, 2)
    prompt_count = rows_mine // LMAX
    prompt_lengths = lax.dynamic_slice_in_dim(
        lengths, column_lookup * prompt_count, prompt_count, 0
    )
    att, final_local = time_core(
        acceptance_gate_entries,
        key_vecs,
        value_vecs,
        decay_lowrank,
        rate_lowrank,
        head_local,
        up_shard_local,
        prompt_lengths,
    )
    partial_out = lax.dot_general(
        att, time_weights[3], (((1,), (1,)), ((), ())), preferred_element_type=jnp.float32
    )
    attn_out = lax.psum_scatter(
        partial_out.astype(jnp.bfloat16), "row", scatter_dimension=1, tiled=True
    ).astype(jnp.float32)
    states_all = lax.all_gather(final_local.astype(jnp.bfloat16), "col", axis=0, tiled=True).astype(
        final_local.dtype
    )
    states_mine = lax.all_to_all(
        states_all.astype(jnp.bfloat16), "row", split_axis=0, concat_axis=1, tiled=True
    ).astype(states_all.dtype)
    head_share = states_mine.shape[1] // n_col
    final_state = lax.dynamic_slice_in_dim(states_mine, column_lookup * head_share, head_share, 1)
    mid = (resid + attn_out).astype(jnp.bfloat16)
    mid_wide = mid.astype(jnp.float32)
    channel_in = mixed(normed(mid_wide, norm_parameters[2], norm_parameters[3]), row_mix[5])
    rows_next = channel_in.shape[0] * n_col // n_row
    full_rows = lax.all_gather(channel_in, "row", axis=1, tiled=True)
    pre_act = jnp.dot(full_rows, mlp_weights[0], preferred_element_type=jnp.float32)
    act = jnp.square(jax.nn.relu(pre_act)).astype(jnp.bfloat16)
    partial_mlp = lax.dot_general(
        act, mlp_weights[1], (((1,), (1,)), ((), ())), preferred_element_type=jnp.float32
    )
    channel_out = lax.psum_scatter(
        partial_mlp.astype(jnp.bfloat16), "row", scatter_dimension=1, tiled=True
    ).astype(jnp.float32)
    out_hidden = (mid_wide + channel_out).astype(jnp.bfloat16)
    third = normed(out_hidden.astype(jnp.float32), norm_parameters[4], norm_parameters[5])
    third_all = gather_cols(third)
    next_mixes = [mixed(third_all, row_mix[6 + column_step]) for column_step in range(3)]
    next_width = square.shape[2]

    def next_terms(start, count):
        parts = [
            jnp.dot(
                next_mixes[column_step],
                square[next_base + column_step],
                preferred_element_type=jnp.float32,
            )
            for column_step in range(3)
        ]
        return jnp.concatenate(parts, axis=1)

    next_summed = row_sums(next_terms, rows_next)
    next_rkv = jnp.stack(
        [
            next_summed[:, column_step * next_width : (column_step + 1) * next_width]
            for column_step in range(3)
        ]
    ).astype(jnp.bfloat16)
    return (out_hidden, next_rkv, final_state)


def solution(mesh):
    return jax.shard_map(
        per_device,
        mesh=mesh,
        in_specs=(
            P("col", "row"),
            P(),
            P(None, ("row", "col"), None),
            P(None, ("row", "col"), None),
            P(),
            P(),
            P(),
            P(),
            P(None, "row"),
        ),
        out_specs=(P("col", "row"), P(None, "row", "col"), P("row", "col", None)),
        check_vma=False,
    )
```

profile of v0, /device:TPU:1, one launch (start us, length us, event | category | flops | bytes accessed | tf_op | source)
XLA Modules:
  0.0 1199.4 jit_solution(12120380743877669897)
XLA Ops:
  10.6 29.0 %all-reduce.5 = (f32[1024]{0:T(1024)S(1)}, f32[1024]{0:T(1024)S(1)}) all-reduce(f32[1024]{0:T(1024)S(1)} %get-tuple-element.485, f32[1024]{0:T(1024)S(1)} %get-tuple-element.484), channel_id=1, replica_groups=mesh['row'=16,'col'=8] {'row'}, use_global_device_ids=true, to_apply=%region_3.0 | all-reduce | flops 2048 | bytes 16384 | tf_op jit(solution)/shard_map/psum | solution.py:24
  42.5 25.6 %all-gather.9.cloned.1.call-done = bf16[4,128,2048]{2,0,1:T(4,128)(2,1)} async-done(((bf16[4,16,2048]{2,0,1:T(4,128)(2,1)}), bf16[4,128,2048]{2,0,1:T(4,128)(2,1)}) %all-gather.9.cloned.1.call-update) | async-done | bytes 2097168 | tf_op jit(solution)/shard_map/all_gather | solution.py:228
  68.0 5.6 copy.281
  73.6 6.5 all-to-all-start
  87.4 25.9 %all-to-all-done = bf16[4,128,2048]{1,0,2:T(4,128)(2,1)} async-done(((bf16[4,128,2048]{1,0,2:T(4,128)(2,1)}), bf16[4,128,2048]{1,0,2:T(4,128)(2,1)}, u32[]{:S(2)}, u32[]{:S(2)}) %all-to-all-start) | async-done | bytes 2097184 | tf_op jit(solution)/shard_map/all_to_all | solution.py:229
  123.6 14.0 %all-gather.7.cloned.1.call-done = bf16[1024,2048]{1,0:T(8,128)(2,1)} async-done(((bf16[1024,128]{1,0:T(8,128)(2,1)}), bf16[1024,2048]{1,0:T(8,128)(2,1)}) %all-gather.7.cloned.1.call-update) | async-done | bytes 4194320 | tf_op jit(solution)/shard_map/all_gather | solution.py:230
  137.6 3.2 slice.259
  140.8 4.3 concatenate.20
  145.1 12.6 %fusion.64 = (bf16[1024,2048]{1,0:T(8,128)(2,1)}, bf16[1024,2048]{1,0:T(8,128)(2,1)}, bf16[1024,2048]{1,0:T(8,128)(2,1)}, bf16[1024,2048]{1,0:T(8,128)(2,1)}, bf16[1024,2048]{1,0:T(8,128)(2,1)}) fusion(bf16[1024,2048]{1,0:T(8,128)(2,1)S(1)} %copy-done.2, f32[2048]{0:T(1024)S(1)} %bitcast.344, f32[8,128,2048]{2,1,0:T(8,128)} %concatenate.20, ...), kind=kLoop, calls=%fused_computation.109 | loop fusion | flops 35651584 | bytes 33595392 | tf_op jit(solution)/shard_map/convert_element_type | solution.py:20
  157.7 135.7 %while.38 = (s32[]{:T(128)}, f32[1024,128]{1,0:T(8,128)S(1)}, f32[1024,128]{1,0:T(8,128)S(1)}, f32[1024,128]{1,0:T(8,128)S(1)}, f32[1024,96]{0,1:T(8,128)}, /*in...) while((s32[]{:T(128)}, f32[1024,128]{1,0:T(8,128)S(1)}, ...), condition=%wide.region_5.0_spmd.clone, body=%wide.region_4.0_spmd.clone.sunk | while | flops 153354240 | bytes 8557807 | solution.py:197
  170.2 2.2 select_add_fusion.10
  178.8 2.2 select_add_fusion.10
  187.3 2.2 select_add_fusion.10
  195.9 2.2 select_add_fusion.10
  204.4 2.2 select_add_fusion.10
  213.0 2.2 select_add_fusion.10
  221.5 2.2 select_add_fusion.10
  230.1 2.2 select_add_fusion.10
  238.6 2.2 select_add_fusion.10
  247.2 2.2 select_add_fusion.10
  255.7 2.2 select_add_fusion.10
  281.4 2.2 select_add_fusion.10
  304.6 2.3 constant_dynamic-update-slice_fusion
  308.1 2.6 reshape.357
  312.9 2.8 reshape.359
  317.7 3.1 multiply_dynamic-update-slice_fusion.3
  322.8 3.2 multiply_dynamic-update-slice_fusion.1
  326.0 3.4 multiply_dynamic-update-slice_fusion
  329.5 230.6 %while.39 = (s32[]{:T(128)}, f32[8,2,64,64]{3,2,1,0:T(8,128)S(1)}, f32[8,8,16,2,64]{4,3,2,1,0:T(2,128)}, f32[6,8,8,16,2,64]{5,4,3,2,1,0:T(2,128)}, s32[]{:T(128)...) while((s32[]{:T(128)}, f32[8,2,64,64]{3,2,1,0:T(8,128)S(1)}, ...), condition=%wide.region_9.10_spmd.clone, body=%wide.region_7.9_spmd.clone.sunk | while | flops 76495128 | bytes 5365069 | solution.py:153
  331.4 19.8 %custom-call.19 = f32[8,2,1,16,16]{3,4,2,1,0:T(8,128)S(1)} custom-call(f32[8,2,1,16,16]{4,3,2,1,0:T(8,128)S(1)} %fusion.208), custom_call_target="InvertDiagBlocksLowerTriangular" | custom-call | tf_op jit(solution)/shard_map/while/body/eval_jaxpr/jit(_solve_triangular)/vmap(vmap())/triangular_solve | solution.py:65
  360.2 19.8 %custom-call.19 = f32[8,2,1,16,16]{3,4,2,1,0:T(8,128)S(1)} custom-call(f32[8,2,1,16,16]{4,3,2,1,0:T(8,128)S(1)} %fusion.208), custom_call_target="InvertDiagBlocksLowerTriangular" | custom-call | tf_op jit(solution)/shard_map/while/body/eval_jaxpr/jit(_solve_triangular)/vmap(vmap())/triangular_solve | solution.py:65
  389.1 19.8 %custom-call.19 = f32[8,2,1,16,16]{3,4,2,1,0:T(8,128)S(1)} custom-call(f32[8,2,1,16,16]{4,3,2,1,0:T(8,128)S(1)} %fusion.208), custom_call_target="InvertDiagBlocksLowerTriangular" | custom-call | tf_op jit(solution)/shard_map/while/body/eval_jaxpr/jit(_solve_triangular)/vmap(vmap())/triangular_solve | solution.py:65
  417.9 19.8 %custom-call.19 = f32[8,2,1,16,16]{3,4,2,1,0:T(8,128)S(1)} custom-call(f32[8,2,1,16,16]{4,3,2,1,0:T(8,128)S(1)} %fusion.208), custom_call_target="InvertDiagBlocksLowerTriangular" | custom-call | tf_op jit(solution)/shard_map/while/body/eval_jaxpr/jit(_solve_triangular)/vmap(vmap())/triangular_solve | solution.py:65
  446.7 19.8 %custom-call.19 = f32[8,2,1,16,16]{3,4,2,1,0:T(8,128)S(1)} custom-call(f32[8,2,1,16,16]{4,3,2,1,0:T(8,128)S(1)} %fusion.208), custom_call_target="InvertDiagBlocksLowerTriangular" | custom-call | tf_op jit(solution)/shard_map/while/body/eval_jaxpr/jit(_solve_triangular)/vmap(vmap())/triangular_solve | solution.py:65
  475.5 19.8 %custom-call.19 = f32[8,2,1,16,16]{3,4,2,1,0:T(8,128)S(1)} custom-call(f32[8,2,1,16,16]{4,3,2,1,0:T(8,128)S(1)} %fusion.208), custom_call_target="InvertDiagBlocksLowerTriangular" | custom-call | tf_op jit(solution)/shard_map/while/body/eval_jaxpr/jit(_solve_triangular)/vmap(vmap())/triangular_solve | solution.py:65
  504.4 19.8 %custom-call.19 = f32[8,2,1,16,16]{3,4,2,1,0:T(8,128)S(1)} custom-call(f32[8,2,1,16,16]{4,3,2,1,0:T(8,128)S(1)} %fusion.208), custom_call_target="InvertDiagBlocksLowerTriangular" | custom-call | tf_op jit(solution)/shard_map/while/body/eval_jaxpr/jit(_solve_triangular)/vmap(vmap())/triangular_solve | solution.py:65
  533.2 19.8 %custom-call.19 = f32[8,2,1,16,16]{3,4,2,1,0:T(8,128)S(1)} custom-call(f32[8,2,1,16,16]{4,3,2,1,0:T(8,128)S(1)} %fusion.208), custom_call_target="InvertDiagBlocksLowerTriangular" | custom-call | tf_op jit(solution)/shard_map/while/body/eval_jaxpr/jit(_solve_triangular)/vmap(vmap())/triangular_solve | solution.py:65
  560.2 4.9 fusion.104
  567.6 7.9 multiply_reduce_fusion
  582.6 4.3 convolution_convert_fusion.9
  586.9 6.4 copy.323
  597.2 61.3 %reduce-scatter.10.cloned.1.call-done = bf16[128,1024]{1,0:T(8,128)(2,1)} async-done(((bf16[2048,1024]{1,0:T(8,128)(2,1)}), bf16[128,1024]{1,0:T(8,128)(2,1)}) %reduce-scatter.10.cloned.1.call-update) | async-done | bytes 262160
  659.9 31.6 %all-reduce.4 = (f32[1024]{0:T(1024)S(1)}, f32[1024]{0:T(1024)S(1)}) all-reduce(f32[1024]{0:T(1024)S(1)} %get-tuple-element.483, f32[1024]{0:T(1024)S(1)} %get-tuple-element.482), channel_id=1, replica_groups=mesh['row'=16,'col'=8] {'row'}, use_global_device_ids=true, to_apply=%region_17.18 | all-reduce | flops 2048 | bytes 16384 | tf_op jit(solution)/shard_map/psum | solution.py:24
  693.0 41.8 %all-gather.13.cloned.1.call-done = bf16[2,128,8192]{2,0,1:T(2,128)(2,1)} async-done(((bf16[2,16,8192]{2,0,1:T(2,128)(2,1)}), bf16[2,128,8192]{2,0,1:T(2,128)(2,1)}) %all-gather.13.cloned.1.call-update) | async-done | bytes 4194320 | tf_op jit(solution)/shard_map/all_gather | solution.py:220
  734.8 14.8 %copy.305 = bf16[2,128,8192]{1,0,2:T(2,128)(2,1)} copy(bf16[2,128,8192]{2,0,1:T(2,128)(2,1)} %all-gather.13.cloned.1.call-done) | data formatting | bytes 8388608 | tf_op jit(solution)/shard_map/all_gather | solution.py:220
  749.6 66.3 %all_to_all.54 = bf16[2,128,8192]{1,0,2:T(2,128)(2,1)S(1)} all-to-all(bf16[2,128,8192]{1,0,2:T(2,128)(2,1)} %copy.305), channel_id=1, replica_groups=mesh['row'=16,'col'=8] {'row'}, dimensions={2} | all-to-all | bytes 8388608 | tf_op jit(solution)/shard_map/all_to_all | solution.py:221
  816.5 2.3 fusion.107
  818.8 3.9 copy.307
  822.7 3.9 copy.308
  826.6 9.9 convolution_convert_fusion.8
  836.5 6.4 copy.325
  843.0 61.2 %reduce-scatter.12.cloned.1.call-done = bf16[128,1024]{1,0:T(8,128)(2,1)} async-done(((bf16[2048,1024]{1,0:T(8,128)(2,1)}), bf16[128,1024]{1,0:T(8,128)(2,1)}) %reduce-scatter.12.cloned.1.call-update) | async-done | bytes 262160
  905.7 31.1 %all-reduce.3 = (f32[1024]{0:T(1024)S(1)}, f32[1024]{0:T(1024)S(1)}) all-reduce(f32[1024]{0:T(1024)S(1)} %get-tuple-element.481, f32[1024]{0:T(1024)S(1)} %get-tuple-element.480), channel_id=1, replica_groups=mesh['row'=16,'col'=8] {'row'}, use_global_device_ids=true, to_apply=%region_22.23 | all-reduce | flops 2048 | bytes 16384 | tf_op jit(solution)/shard_map/psum | solution.py:24
  939.2 2.5 copy.309
  941.7 3.5 reshape.388
  945.3 13.9 %all_to_all.55 = bf16[8,2,6144]{2,1,0:T(2,128)(2,1)S(1)} all-to-all(bf16[8,2,6144]{2,1,0:T(2,128)(2,1)S(1)} %reshape.388), channel_id=1, replica_groups=mesh['row'=16,'col'=8] {'col'}, dimensions={0} | all-to-all | bytes 393216 | tf_op jit(solution)/shard_map/all_to_all | solution.py:219
  959.2 3.1 reshape.389
  962.3 2.3 copy.322
  966.0 26.9 %all-gather.15.cloned.1.call-done = bf16[8192,128]{1,0:T(8,128)(2,1)} async-done(((bf16[1024,128]{1,0:T(8,128)(2,1)}), bf16[8192,128]{1,0:T(8,128)(2,1)}) %all-gather.15.cloned.1.call-update) | async-done | bytes 2097168 | tf_op jit(solution)/shard_map/all_gather | solution.py:32
  1002.0 12.7 %pad_maximum_fusion = bf16[8192,768]{0,1:T(8,128)(2,1)} fusion(bf16[8192,256]{0,1:T(8,128)(2,1)S(1)} %convolution_convert_fusion.5, bf16[8192,256]{0,1:T(8,128)(2,1)S(1)} %convolution_convert_fusion.6, bf16[8192,256]{0,1:T(8,128)(2,1)S(1)} %convolution_convert_fusion.7), kind=kLoop, calls=%fused_computation.95 | loop fusion | flops 37748736 | bytes 25165824 | tf_op jit(solution)/shard_map/concatenate | solution.py:301
  1014.7 27.6 %all-gather.17.cloned.1.call-done = bf16[64,2,4096]{2,1,0:T(2,128)(2,1)} async-done(((bf16[8,2,4096]{2,1,0:T(2,128)(2,1)}), bf16[64,2,4096]{2,1,0:T(2,128)(2,1)}) %all-gather.17.cloned.1.call-update) | async-done | bytes 1048592 | tf_op jit(solution)/shard_map/all_gather | solution.py:265
  1042.3 5.9 all-to-all-start.3
  1048.2 16.4 %all-to-all-done.3 = bf16[64,2,4096]{2,1,0:T(2,128)(2,1)S(1)} async-done(((bf16[64,2,4096]{2,1,0:T(2,128)(2,1)}), bf16[64,2,4096]{2,1,0:T(2,128)(2,1)S(1)}, u32[]{:S(2)}, u32[]{:S(2)}) %all-to-all-start.3) | async-done | bytes 1048608 | tf_op jit(solution)/shard_map/all_to_all | solution.py:268
  1067.9 122.1 %reduce-scatter.8.cloned.1.call-done = bf16[512,768]{0,1:T(8,128)(2,1)} async-done(((bf16[8192,768]{0,1:T(8,128)(2,1)}), bf16[512,768]{0,1:T(8,128)(2,1)}) %reduce-scatter.8.cloned.1.call-update) | async-done | bytes 786448 | tf_op jit(solution)/shard_map/reduce_scatter | solution.py:36
  (455 shorter events, 259.0 us)
Async XLA Ops:
  7.2 299.8 %copy-start = (bf16[2,96,2048]{2,1,0:T(8,128)(2,1)S(1)}, bf16[2,96,2048]{2,1,0:T(8,128)(2,1)}, u32[]{:S(2)}) copy-start(bf16[2,96,2048]{2,1,0:T(8,128)(2,1)} %param.18) | copy-start | bytes 2359300
  7.2 60.9 %all-gather.9.cloned.1.call-start = ((), (), s32[]{:S(2)}) async-start(), calls=%async_computation.8 | async-start | bytes 2359296 | tf_op jit(solution)/shard_map/all_gather | solution.py:228
  9.3 128.3 %all-gather.7.cloned.1.call-start = ((), (), s32[]{:S(2)}) async-start(), calls=%async_computation.7 | async-start | bytes 4456448 | tf_op jit(solution)/shard_map/all_gather | solution.py:230
  73.6 12.4 %copy-start.13 = (s32[64]{0:T(128)S(1)}, s32[64]{0:T(128)}, u32[]{:S(2)}) copy-start(s32[64]{0:T(128)} %param.14) | copy-start | bytes 772
  73.6 39.7 %all-to-all-start = ((bf16[4,128,2048]{1,0,2:T(4,128)(2,1)}), bf16[4,128,2048]{1,0,2:T(4,128)(2,1)}, u32[]{:S(2)}, u32[]{:S(2)}) async-start(bf16[4,128,2048]{1,0,2:T(4,128)(2,1)} %copy.281), calls=%async_computation | async-start | bytes 4194304 | tf_op jit(solution)/shard_map/all_to_all | solution.py:229
  80.1 578.3 %reduce-scatter.10.cloned.1.call-start = ((), (), s32[]{:S(2)}) async-start(), calls=%async_computation.14 | async-start | bytes 4456448
  140.8 4.3 copy-start.2
  297.7 9.2 copy-start.4
  312.9 9.9 copy-start.6
  315.6 5.1 copy-start.7
  315.6 10.4 copy-start.8
  560.0 6.9 copy-start.5
  577.0 5.7 copy-start.10
  593.4 1.2 copy-start.12
  593.4 66.2 %copy-start.9 = (bf16[1024,128]{1,0:T(8,128)(2,1)S(1)}, bf16[1024,128]{1,0:T(8,128)(2,1)}, u32[]{:S(2)}) copy-start(bf16[1024,128]{1,0:T(8,128)(2,1)} %param.13) | copy-start | bytes 786436
  593.4 141.4 %all-gather.13.cloned.1.call-start = ((), (), s32[]{:S(2)}) async-start(), calls=%async_computation.10 | async-start | bytes 4718592 | tf_op jit(solution)/shard_map/all_gather | solution.py:220
  596.2 230.4 %all-gather.11.cloned.1.call-start = ((), (), s32[]{:S(2)}) async-start(), calls=%async_computation.9 | async-start | bytes 4456448 | tf_op jit(solution)/shard_map/all_gather | solution.py:277
  692.9 211.3 %reduce-scatter.12.cloned.1.call-start = ((), (), s32[]{:S(2)}) async-start(), calls=%async_computation.15 | async-start | bytes 4456448
  843.0 149.9 %all-gather.15.cloned.1.call-start = ((), (), s32[]{:S(2)}) async-start(), calls=%async_computation.11 | async-start | bytes 2359296 | tf_op jit(solution)/shard_map/all_gather | solution.py:32
  905.7 56.6 %copy-start.11 = (bf16[1024,128]{1,0:T(8,128)(2,1)}, bf16[1024,128]{1,0:T(8,128)(2,1)S(1)}, u32[]{:S(2)}) copy-start(bf16[1024,128]{1,0:T(8,128)(2,1)S(1)} %get-tuple-element.534) | copy-start | bytes 786436
  937.9 104.4 %all-gather.17.cloned.1.call-start = ((), (), s32[]{:S(2)}) async-start(), calls=%async_computation.13 | async-start | bytes 1179648 | tf_op jit(solution)/shard_map/all_gather | solution.py:265
  965.7 224.3 %reduce-scatter.8.cloned.1.call-start = ((), (), s32[]{:S(2)}) async-start(), calls=%async_computation.12 | async-start | bytes 13369344 | tf_op jit(solution)/shard_map/reduce_scatter | solution.py:36
  995.0 1.6 copy-start.3
  1042.3 22.4 %all-to-all-start.3 = ((bf16[64,2,4096]{2,1,0:T(2,128)(2,1)}), bf16[64,2,4096]{2,1,0:T(2,128)(2,1)S(1)}, u32[]{:S(2)}, u32[]{:S(2)}) async-start(bf16[64,2,4096]{2,1,0:T(2,128)(2,1)} %all-gather.17.cloned.1.call-done), calls=%async_computation.4 | async-start | bytes 2097152 | tf_op jit(solution)/shard_map/all_to_all | solution.py:268
  1064.7 127.7 %copy-start.1 = (bf16[2,96,2048]{2,1,0:T(8,128)(2,1)S(1)}, bf16[2,96,2048]{2,1,0:T(8,128)(2,1)}, u32[]{:S(2)}) copy-start(bf16[2,96,2048]{2,1,0:T(8,128)(2,1)} %param.18) | copy-start | bytes 2359300
Sparse Core Ops, SparseCore 0:
  10.9 57.0 all-gather.8
  70.2 67.3 all-gather.6
  593.5 64.8 reduce-scatter.9
  661.2 73.5 all-gather.12
  736.8 80.0 all-gather.10
  843.1 61.0 reduce-scatter.11
  938.1 54.7 all-gather.14
  995.8 46.4 all-gather.16
  1044.7 145.2 reduce-scatter.7
where the time goes:
time: 1210 us; the launch traced here: 1200 us
  waiting for transfers between devices  423 us (35%)
  other arithmetic  262 us (22%)
  blocking collectives  172 us (14%)
  matrix products  169 us (14%)
  local copies, waits for them, and re-layouts  144 us (12%)
  between operations  14.8 us (1%)
  starting transfers between devices  13.2 us (1%)
    another operation x24, other arithmetic, span_step(): jax.scipy.linalg.solve_triangular(system, rhs_side, lower=True, unit_diag...  159 us
    unnamed x11, waiting for transfers between devices  123 us
    reduce_scatter x1, waiting for transfers between devices, row_sums(): lax.psum_scatter(term_fn(jnp.int32(0), rows * lax.axis_size('row')).astyp...  122 us
    dot_general x80, matrix products, add_block(): jnp.dot(piece, weight_piece, preferred_element_type=jnp.float32)  94.5 us
    psum x3, blocking collectives, normed(): lax.psum((jnp.sum(source, axis=-1), jnp.sum(source * source, axis=-1)), '...  91.6 us
    all_to_all x1, blocking collectives, per_device(): lax.all_to_all(mlp_group, 'row', split_axis=2, concat_axis=1, tiled=True)  66.3 us
    all_gather x1, waiting for transfers between devices, per_device(): mlp_group = lax.all_gather(mlp_low, 'col', axis=1, tiled=True)  41.8 us
    add x48, other arithmetic, add_block(): total + lax.optimization_barrier(partial_sum.astype(jnp.bfloat16)).astype...  40.1 us
  transfers between devices with their start and end apart: 11, of which 10 were waited for; matrix products, arithmetic and copies ran while one was open for 8% of the time, Pallas kernels for 0%

commit v1 on v0

v1 whole, which is shorter than its diff:
```python
import jax
import jax.numpy as jnp
from jax import lax
from jax.experimental import pallas as pl
from jax.experimental.pallas import tpu as pltpu
from jax.sharding import PartitionSpec as P

WIDTH = 2048
HEAD = 64
LMAX = 128
F32 = jnp.float32
BF16 = jnp.bfloat16
MESH = pl.DeviceIdType.MESH
ANY = pl.BlockSpec(memory_space=pl.ANY)
VMEM = pl.BlockSpec(memory_space=pltpu.VMEM)
N_ROW = 16
N_COL = 8
N_CHIP = 8
MINE = 512
FEAT = 128
SLICE = 256


def greet(devices):
    barrier = pltpu.get_barrier_semaphore()
    for device in devices:
        pl.semaphore_signal(barrier, inc=1, device_id=device, device_id_type=MESH)
    pl.semaphore_wait(barrier, len(devices))


def send(source, target, send_sem, recv_sem, device):
    copy = pltpu.make_async_remote_copy(
        src_ref=source,
        dst_ref=target,
        send_sem=send_sem,
        recv_sem=recv_sem,
        device_id=device,
        device_id_type=MESH,
    )
    copy.start()
    return copy


def keep(source, target, sem):
    copy = pltpu.make_async_copy(source, target, sem)
    copy.start()
    return copy


def exchange(kernel, outs, n_remote, n_local, collective_id, *operands):
    return pl.pallas_call(
        kernel,
        out_shape=[jax.ShapeDtypeStruct(*out) for out in outs],
        in_specs=[ANY] * len(operands),
        out_specs=[ANY] * len(outs),
        scratch_shapes=[
            pltpu.SemaphoreType.DMA((n_remote,)),
            pltpu.SemaphoreType.DMA((n_remote,)),
            pltpu.SemaphoreType.DMA((n_local,)),
        ],
        compiler_params=pltpu.CompilerParams(collective_id=collective_id, has_side_effects=True),
        cost_estimate=pl.CostEstimate(flops=0, bytes_accessed=48 * 2**20, transcendentals=0),
    )(*operands)


def start_kernel(
    hid, wa, wm, wn, par, hx, wt, wmr, wnr, parg, send_sem, recv_sem, local_sem
):
    r = lax.axis_index("row")
    c = lax.axis_index("col")
    h = lax.rem(r, 2)
    sibling = r + 1 - 2 * h
    rows = [lax.rem(r + d, N_ROW) for d in range(1, N_ROW)]
    cols = [lax.rem(c + d, N_COL) for d in range(1, N_COL)]
    greet([(p, c) for p in rows] + [(r, p) for p in cols])
    slot = iter(range(200))

    def go(source, target, device):
        at = next(slot)
        return send(source, target, send_sem.at[at], recv_sem.at[at], device)

    local = [
        keep(wa.at[r], wt.at[h, r, c], local_sem.at[0]),
        keep(hid.at[pl.ds(h * MINE, MINE)], hx.at[r], local_sem.at[1]),
        keep(wm.at[r], wmr.at[r], local_sem.at[2]),
        keep(wn.at[c], wnr.at[c], local_sem.at[3]),
        keep(par, parg.at[r], local_sem.at[4]),
    ]
    first = [go(wa.at[p], wt.at[lax.rem(p, 2), r, c], (p, c)) for p in rows]
    rest = [
        go(hid.at[pl.ds(lax.rem(p, 2) * MINE, MINE)], hx.at[r], (p, c)) for p in rows
    ]
    rest += [go(par, parg.at[r], (p, c)) for p in rows]
    for copy in first:
        copy.wait_recv()
    local[0].wait()
    spread = [go(wt.at[h, :, c], wt.at[h, :, c], (r, p)) for p in cols]
    rest += [go(wt.at[h, :, c], wt.at[h, :, c], (sibling, c))]
    rest += [go(wm.at[p], wmr.at[r], (p, c)) for p in rows]
    rest += [go(wn.at[p], wnr.at[c], (r, p)) for p in cols]
    for d in range(1, N_COL):
        spread[d - 1].wait_recv()
        origin = lax.rem(c - d + N_COL, N_COL)
        rest += [go(wt.at[h, :, origin], wt.at[h, :, origin], (sibling, c))]
    for copy in rest:
        copy.wait_recv()
    for copy in first + spread + rest:
        copy.wait_send()
    for copy in local[1:]:
        copy.wait()


def att_kernel(att, w3, attg, w3x, send_sem, recv_sem, local_sem):
    r = lax.axis_index("row")
    c = lax.axis_index("col")
    h = lax.rem(r, 2)
    q = lax.div(r, 2)
    sibling = r + 1 - 2 * h
    rows = [lax.rem(r + 2 * d, N_ROW) for d in range(1, N_CHIP)]
    greet([(p, c) for p in rows] + [(sibling, c)])
    local = [keep(att, attg.at[q], local_sem.at[0]), keep(w3, w3x.at[h], local_sem.at[1])]
    copies = [
        send(att, attg.at[q], send_sem.at[i], recv_sem.at[i], (p, c))
        for i, p in enumerate(rows)
    ]
    copies += [send(w3, w3x.at[h], send_sem.at[7], recv_sem.at[7], (sibling, c))]
    for copy in local + copies:
        copy.wait()


def mid_kernel(mid, wmg, midg, mlpw, send_sem, recv_sem, local_sem):
    r = lax.axis_index("row")
    c = lax.axis_index("col")
    h = lax.rem(r, 2)
    q = lax.div(r, 2)
    sibling = r + 1 - 2 * h
    rows = [lax.rem(r + 2 * d, N_ROW) for d in range(1, N_CHIP)]
    greet([(p, c) for p in rows] + [(sibling, c)])
    copies = [
        send(mid, midg.at[q], send_sem.at[i], recv_sem.at[i], (p, c))
        for i, p in enumerate(rows)
    ]
    local = [keep(mid, midg.at[q], local_sem.at[8])]
    for k in range(N_COL):
        copies += [
            send(
                wmg.at[k], mlpw.at[h, :, k], send_sem.at[7 + k], recv_sem.at[7 + k], (sibling, c)
            )
        ]
        local += [keep(wmg.at[k], mlpw.at[h, :, k], local_sem.at[k])]
    for copy in local + copies:
        copy.wait()


def sum_kernel(part, got, send_sem, recv_sem, local_sem):
    r = lax.axis_index("row")
    c = lax.axis_index("col")
    rows = [lax.rem(r + d, N_ROW) for d in range(1, N_ROW)]
    greet([(p, c) for p in rows])
    local = keep(part.at[r], got.at[r], local_sem.at[0])
    copies = [
        send(part.at[p], got.at[r], send_sem.at[i], recv_sem.at[i], (p, c))
        for i, p in enumerate(rows)
    ]
    local.wait()
    for copy in copies:
        copy.wait()


def next_kernel(out, got, send_sem, recv_sem, local_sem):
    r = lax.axis_index("row")
    c = lax.axis_index("col")
    h = lax.rem(r, 2)
    q = lax.div(r, 2)
    barrier = pltpu.get_barrier_semaphore()

    @pl.when(q != c)
    def _():
        pl.semaphore_signal(barrier, inc=1, device_id=(r, q), device_id_type=MESH)

    for d in range(1, N_ROW):
        pl.semaphore_signal(
            barrier, inc=1, device_id=(lax.rem(r + d, N_ROW), q), device_id_type=MESH
        )
    pl.semaphore_wait(barrier, N_ROW - (q == c).astype(jnp.int32))

    def move(i, e):
        half = lax.rem(h + i, 2)
        return pltpu.make_async_remote_copy(
            src_ref=out.at[pl.ds(half * MINE, MINE)],
            dst_ref=got.at[r],
            send_sem=send_sem.at[i * N_COL + e],
            recv_sem=recv_sem.at[r],
            device_id=(2 * c + half, lax.rem(c + e, N_COL)),
            device_id_type=MESH,
        )

    @pl.when(q == c)
    def _():
        keep(out.at[pl.ds(h * MINE, MINE)], got.at[r], recv_sem.at[r])

    @pl.when(q != c)
    def _():
        move(0, 0).start()

    for e in range(N_COL):
        for i in range(2):
            if i + e > 0:
                move(i, e).start()
    for s in range(N_ROW):
        pltpu.make_async_copy(got.at[s], got.at[s], recv_sem.at[s]).wait()

    @pl.when(q != c)
    def _():
        move(0, 0).wait_send()

    for e in range(N_COL):
        for i in range(2):
            if i + e > 0:
                move(i, e).wait_send()


def compute(kernel, outs, operands, scratch=(), grid=None, in_specs=None, out_specs=None, flops=0):
    return pl.pallas_call(
        kernel,
        grid=grid if grid is not None else (),
        out_shape=[jax.ShapeDtypeStruct(*out) for out in outs],
        in_specs=in_specs if in_specs is not None else [VMEM] * len(operands),
        out_specs=out_specs if out_specs is not None else [VMEM] * len(outs),
        scratch_shapes=list(scratch),
        compiler_params=pltpu.CompilerParams(vmem_limit_bytes=56 * 2**20),
        cost_estimate=pl.CostEstimate(flops=flops, bytes_accessed=16 * 2**20, transcendentals=0),
    )(*operands)


def dot(a, b, dims=((1,), (0,))):
    return lax.dot_general(a, b, (dims, ((), ())), preferred_element_type=F32)


def split(x):
    high = x.astype(BF16)
    return high, (x - high.astype(F32)).astype(BF16)


def dot3(a, b, dims=((1,), (0,))):
    a_high, a_low = a
    b_high, b_low = b
    return dot(a_high, b_high, dims) + (dot(a_high, b_low, dims) + dot(a_low, b_high, dims))


def norm(source, gain, bias):
    center = jnp.sum(source, axis=-1, keepdims=True) / WIDTH
    second = jnp.sum(source * source, axis=-1, keepdims=True) / WIDTH
    scaled = (source - center) * lax.rsqrt(second - center * center + 1e-05)
    return (scaled * gain + bias).astype(BF16).astype(F32)


def step_back(z):
    position = lax.rem(lax.broadcasted_iota(jnp.int32, z.shape, 0), LMAX)
    return jnp.where(position == 0, 0.0, pltpu.roll(z, 1, 0)) - z


TILE = 256


def blocks_of(ref, at):
    return jnp.concatenate(
        [ref[j, pl.ds(at, TILE), :].astype(F32) for j in range(ref.shape[0])], axis=1
    )


def mix_kernel(hx, par, shift, wt, down, rkv, low):
    @pl.loop(0, MINE // TILE)
    def _(m):
        at = pl.multiple_of(m * TILE, TILE)
        z = norm(blocks_of(hx, at), par[0:1, :], par[1:2, :])
        dz = step_back(z)
        for j in range(5):
            blend = (z + dz * shift[j : j + 1, :]).astype(BF16)
            if j < 3:
                weight = jnp.concatenate(
                    [wt[side, :, j * FEAT : (j + 1) * FEAT] for side in range(2)], axis=1
                )
                rkv[j, pl.ds(at, TILE), :] = dot(blend, weight)
            else:
                low[j - 3, pl.ds(at, TILE), :] = dot(blend, down[j - 3])


def core_kernel(lens, rkv, low, coef, up, att, final):
    length = lens[pl.program_id(0)]
    wide = SLICE
    heads = wide // HEAD
    live = (lax.broadcasted_iota(jnp.int32, (LMAX, wide), 0) < length).astype(F32)
    lane = lax.broadcasted_iota(jnp.int32, (LMAX, wide), 1) // HEAD
    t = lax.broadcasted_iota(jnp.int32, (LMAX, LMAX), 0)
    u = lax.broadcasted_iota(jnp.int32, (LMAX, LMAX), 1)
    seg = (
        lax.broadcasted_iota(jnp.int32, (wide, wide), 0) // HEAD
        == lax.broadcasted_iota(jnp.int32, (wide, wide), 1) // HEAD
    ).astype(F32).astype(BF16)
    lower = (t >= u).astype(F32).astype(BF16)

    def head_sum(x):
        high, low_part = split(x)
        return dot(high, seg) + dot(low_part, seg)

    def only(x, k):
        return jnp.where(lane == k, x, jnp.zeros_like(x))

    receptance, key, value = rkv[0], rkv[1], rkv[2]
    decay = (
        -0.606531
        * jax.nn.sigmoid(coef[0:1, :] + dot(jnp.tanh(low[0]).astype(BF16), up[0]))
        * live
    )
    rate = jax.nn.sigmoid(coef[1:2, :] + dot(low[1].astype(BF16), up[1]))
    kappa = key * coef[2:3, :]
    kappa = kappa * lax.rsqrt(head_sum(kappa * kappa) + 1e-05)
    remove = -kappa * live
    write = kappa * rate * live
    key = key * live
    value = value * live
    d_high, d_rest = split(decay)
    d_mid, d_low = split(decay - d_high.astype(F32))
    total = dot(lower, d_high) + (dot(lower, d_mid) + dot(lower, d_low))
    middle = total[LMAX // 2 - 1 : LMAX // 2, :]
    last = total[LMAX - 1 : LMAX, :]
    back = jnp.exp(middle - total)
    pull = split(remove * jnp.exp(total - decay - middle))
    read = split(receptance * jnp.exp(total - middle))
    write_back = split(write * back)
    key_back = split(key * back)
    value_parts = split(value)

    left = tuple(
        jnp.concatenate([x for k in range(heads) for x in (only(pull[i], k), only(read[i], k))])
        for i in range(2)
    )
    right = tuple(jnp.concatenate([write_back[i], key_back[i]]) for i in range(2))
    pairs = dot3(left, right, ((1,), (1,)))
    strict = t > u
    t2 = lax.broadcasted_iota(jnp.int32, (LMAX, 2 * LMAX), 0)
    u2 = lax.rem(lax.broadcasted_iota(jnp.int32, (LMAX, 2 * LMAX), 1), LMAX)
    upto = t2 >= u2
    solves, pull_key, reads = [], [], []
    for k in range(heads):
        base = k * 2 * LMAX
        system = jnp.where(strict, pairs[base : base + LMAX, :LMAX], 0.0)
        pull_key.append(split(jnp.where(strict, pairs[base : base + LMAX, LMAX:], 0.0)))
        reads.append(split(jnp.where(upto, pairs[base + LMAX : base + 2 * LMAX], 0.0)))
        solves.append(system)
    inverse = []
    for k in range(heads):
        near = (t // 2 == u // 2)
        inverse.append(
            jnp.where(near, solves[k], 0.0) + (t == u).astype(F32)
        )
    size = 2
    while size < LMAX:
        inside = (t // (2 * size) == u // (2 * size)) & (t // size != u // size)
        grown = []
        for k in range(heads):
            known = split(inverse[k])
            cross = split(jnp.where(inside, solves[k], 0.0))
            product = split(dot3(known, cross))
            grown.append(inverse[k] + dot3(product, known))
        inverse = grown
        size *= 2

    def across(mats, parts):
        wide_left = tuple(jnp.concatenate([mat[i] for mat in mats], axis=1) for i in range(2))
        tall = tuple(
            jnp.concatenate([only(part[i], k) for k in range(heads) for part in parts])
            for i in range(2)
        )
        return dot3(wide_left, tall)

    start = across(pull_key, [value_parts])
    pulled = split(across([split(x) for x in inverse], [split(start)]))
    output = across(reads, [pulled, value_parts])
    tail = jnp.exp(last - total)
    write_tail = split(write * tail)
    key_tail = split(key * tail)
    tall = tuple(jnp.concatenate([pulled[i], value_parts[i]]) for i in range(2))
    tails = tuple(jnp.concatenate([write_tail[i], key_tail[i]]) for i in range(2))
    state = dot3(tall, tails, ((0,), (0,)))
    for k in range(heads):
        final[0, k] = state[k * HEAD : (k + 1) * HEAD, k * HEAD : (k + 1) * HEAD]
    bonus = head_sum(receptance * key * coef[3:4, :])
    out = (output + bonus * value) * live
    center = head_sum(out) * (1.0 / HEAD)
    out = out - center
    spread = head_sum(out * out) * (1.0 / HEAD)
    att[...] = (out * lax.rsqrt(spread + 0.00064) * coef[4:5, :] + coef[5:6, :]).astype(BF16)


def project_kernel(attg, own, w3, mid):
    q = lax.div(lax.axis_index("row"), 2)

    @pl.loop(0, MINE // TILE)
    def _(m):
        at = pl.multiple_of(m * TILE, TILE)
        wide = jnp.concatenate([attg[j, pl.ds(at, TILE), :] for j in range(N_CHIP)], axis=1)
        hidden = jnp.concatenate(
            [own[2 * q + side, pl.ds(at, TILE), :] for side in range(2)], axis=1
        )
        mid[pl.ds(at, TILE), :] = (
            hidden.astype(F32) + dot(wide, w3[...], ((1,), (1,)))
        ).astype(BF16)


def mlp_kernel(midg, par, shift, mlpw, own, part, act_scr):
    q = lax.div(lax.axis_index("row"), 2)

    @pl.loop(0, MINE // TILE)
    def _(m):
        at = pl.multiple_of(m * TILE, TILE)
        z = norm(blocks_of(midg, at), par[2:3, :], par[3:4, :])
        blend = (z + step_back(z) * shift[5:6, :]).astype(BF16)
        for side in range(2):
            act = jnp.square(jnp.maximum(dot(blend, mlpw[side, :, :MINE]), 0.0))
            act_scr[side] = act.astype(BF16)

        @pl.loop(0, N_CHIP)
        def _(n):
            rows = pl.ds(pl.multiple_of(n * SLICE, SLICE), SLICE)
            total = dot(act_scr[0], mlpw[0, rows, MINE:], ((1,), (1,)))
            total += dot(act_scr[1], mlpw[1, rows, MINE:], ((1,), (1,)))
            total += jnp.where(n == q, own[pl.ds(at, TILE), :].astype(F32), 0.0)
            for side in range(2):
                part[2 * n + side, pl.ds(at, TILE), :] = total[
                    :, side * FEAT : (side + 1) * FEAT
                ].astype(BF16)


def last_kernel(nx, par, shift, weight, out):
    @pl.loop(0, MINE // TILE)
    def _(m):
        at = pl.multiple_of(m * TILE, TILE)
        z = norm(blocks_of(nx, at), par[4:5, :], par[5:6, :])
        dz = step_back(z)
        for j in range(3):
            blend = (z + dz * shift[6 + j : 7 + j, :]).astype(BF16)
            out[j, pl.ds(at, TILE), :] = dot(
                blend, weight[:, j * SLICE : (j + 1) * SLICE]
            ).astype(BF16)


def time_core(lens, rkv, low, coef, up):
    prompts = rkv.shape[1] // LMAX
    return compute(
        core_kernel,
        [((prompts * LMAX, SLICE), BF16), ((prompts, SLICE // HEAD, HEAD, HEAD), F32)],
        (lens, rkv, low, coef, up),
        grid=(prompts,),
        in_specs=[
            pl.BlockSpec(memory_space=pltpu.SMEM),
            pl.BlockSpec((3, LMAX, SLICE), lambda p: (0, p, 0)),
            pl.BlockSpec((2, LMAX, low.shape[2]), lambda p: (0, p, 0)),
            pl.BlockSpec(coef.shape, lambda p: (0, 0)),
            pl.BlockSpec(up.shape, lambda p: (0, 0, 0)),
        ],
        out_specs=[
            pl.BlockSpec((LMAX, SLICE), lambda p: (p, 0)),
            pl.BlockSpec((1, SLICE // HEAD, HEAD, HEAD), lambda p: (p, 0, 0, 0)),
        ],
        flops=4 * 10**9,
    )


def per_device(
    hidden,
    lengths,
    square_matrix_shards,
    channel_mix_shards,
    lowrank_down,
    lowrank_up,
    token_shift_weights,
    attention_coefficients,
    norm_parameters,
):
    r = lax.axis_index("row")
    c = lax.axis_index("col")
    h = lax.rem(r, 2)
    q = lax.div(r, 2)
    square = square_matrix_shards.astype(BF16)
    mlp = channel_mix_shards.astype(BF16)
    wa = square[0:3].reshape(3, 16, N_ROW, FEAT).transpose(2, 1, 0, 3).reshape(N_ROW, 16, 3 * FEAT)
    wm = mlp.reshape(2, 16, N_ROW, MINE).transpose(2, 1, 0, 3).reshape(N_ROW, 16, 2 * MINE)
    wn = square[4:7].reshape(3, 16, N_COL, SLICE).transpose(2, 1, 0, 3)
    wn = wn.reshape(N_COL, 16, 3 * SLICE)
    par = jnp.concatenate([norm_parameters, jnp.zeros((2, FEAT), F32)])
    w3 = lax.all_gather(square[3], "col", axis=0, tiled=True)
    hx, wt, wmr, wnr, parg = exchange(
        start_kernel,
        [
            ((N_ROW, MINE, FEAT), BF16),
            ((2, N_ROW, N_COL, 16, 3 * FEAT), BF16),
            ((N_ROW, 16, 2 * MINE), BF16),
            ((N_COL, 16, 3 * SLICE), BF16),
            ((N_ROW, 8, FEAT), F32),
        ],
        82,
        5,
        1,
        hidden,
        wa,
        wm,
        wn,
        par,
    )
    wmg = lax.all_gather(wmr, "col", axis=0)
    weight_next = lax.all_gather(wnr.reshape(FEAT, 3 * SLICE), "row", axis=0, tiled=True)
    params = parg.transpose(1, 0, 2).reshape(8, WIDTH)
    rkv, low = compute(
        mix_kernel,
        [((3, MINE, SLICE), F32), ((2, MINE, lowrank_down.shape[2]), F32)],
        (hx, params, token_shift_weights, wt.reshape(2, WIDTH, 3 * FEAT), lowrank_down),
        flops=4 * 10**9,
    )
    coef = lax.dynamic_slice_in_dim(attention_coefficients, q * SLICE, SLICE, 1)
    up = lax.dynamic_slice_in_dim(lowrank_up, q * SLICE, SLICE, 2)
    lens = lax.dynamic_slice_in_dim(lengths, c * 8 + h * 4, 4, 0)
    att, final = time_core(lens, rkv, low, coef, up)
    attg, w3x = exchange(
        att_kernel,
        [((N_CHIP, MINE, SLICE), BF16), ((2, FEAT, WIDTH), BF16)],
        8,
        2,
        2,
        att,
        w3,
    )
    moves = [
        ((2 * a + b) * N_COL + d, (2 * d + b) * N_COL + a)
        for a in range(N_CHIP)
        for b in range(2)
        for d in range(N_COL)
    ]
    final = lax.ppermute(final, ("row", "col"), moves)
    final_state = final.reshape(4, 4, HEAD * HEAD)
    (mid,) = compute(
        project_kernel,
        [((MINE, SLICE), BF16)],
        (attg, hx, w3x.reshape(SLICE, WIDTH)),
        flops=10**9,
    )
    midg, mlpw = exchange(
        mid_kernel,
        [((N_CHIP, MINE, SLICE), BF16), ((2, N_ROW, N_COL, 16, 2 * MINE), BF16)],
        15,
        9,
        3,
        mid,
        wmg,
    )
    (part,) = compute(
        mlp_kernel,
        [((N_ROW, MINE, FEAT), BF16)],
        (midg, params, token_shift_weights, mlpw.reshape(2, WIDTH, 2 * MINE), mid),
        scratch=[pltpu.VMEM((2, TILE, MINE), BF16)],
        flops=5 * 10**9,
    )
    (got,) = exchange(sum_kernel, [((N_ROW, MINE, FEAT), BF16)], 15, 1, 4, part)
    out_hidden = (
        jnp.sum(got.reshape(N_CHIP, 2 * MINE, FEAT).astype(F32), axis=0).astype(BF16)
    )
    (nx,) = exchange(next_kernel, [((N_ROW, MINE, FEAT), BF16)], 16, 1, 5, out_hidden)
    (next_rkv,) = compute(
        last_kernel,
        [((3, MINE, SLICE), BF16)],
        (nx, params, token_shift_weights, weight_next),
        flops=2 * 10**9,
    )
    return (out_hidden, next_rkv, final_state)


def solution(mesh):
    return jax.shard_map(
        per_device,
        mesh=mesh,
        in_specs=(
            P("col", "row"),
            P(),
            P(None, ("row", "col"), None),
            P(None, ("row", "col"), None),
            P(),
            P(),
            P(),
            P(),
            P(None, "row"),
        ),
        out_specs=(P("col", "row"), P(None, "row", "col"), P("row", "col", None)),
        check_vma=False,
    )
```

time: 1210 us -> 558 us (0.46)
  the two profiles are of different devices: /device:TPU:1 before, /device:TPU:53 now
where the time goes in v1:
time: 558 us
  Pallas kernels  471 us (84%)
  blocking collectives  52.6 us (9%)
  between operations  14.2 us (3%)
  local copies, waits for them, and re-layouts  9.41 us (2%)
    pallas_call x5, Pallas kernels, exchange(): pl.pallas_call(kernel, out_shape=[jax.ShapeDtypeStruct(*out) for out in o...  413 us
    pallas_call x5, Pallas kernels, compute(): pl.pallas_call(kernel, grid=grid if grid is not None else (), out_shape=[...  58.6 us
    all_gather x1, blocking collectives, per_device(): w3 = lax.all_gather(square[3], 'col', axis=0, tiled=True)  52.6 us
  transfers between devices with their start and end apart: 3, of which 0 were waited for; matrix products, arithmetic and copies ran while one was open for 1% of the time, Pallas kernels for 73%

profile of v1, /device:TPU:53, one launch (start us, length us, event | category | flops | bytes accessed | tf_op | source)
XLA Modules:
  0.0 557.8 jit_solution(17256501619045415832)
XLA Ops:
  7.2 0.0 copy-start
  7.2 0.0 copy-start.1
  7.2 0.0 all-gather.7.cloned.1.call-start
  7.2 1.4 convert_element_type.8
  8.7 0.2 copy.32
  8.8 0.8 reshape.46.wa
  9.7 0.2 copy.31
  9.9 0.9 reshape.50.wn
  10.8 0.0 copy-done.1
  10.8 0.0 copy-start.3
  10.8 0.1 convert_element_type.9
  10.9 0.2 copy.25
  11.0 0.0 copy-start.2
  11.1 0.5 copy.30
  11.6 1.2 reshape.48.wm
  12.8 0.0 copy-done.3
  12.8 0.0 copy-start.4
  12.8 0.6 concatenate.3.par
  13.4 56.5 %shard_map.112 = (bf16[16,512,128]{2,1,0:T(8,128)(2,1)}, bf16[2,16,8,16,384]{4,3,2,1,0:T(8,128)(2,1)}, bf16[16,16,1024]{2,1,0:T(8,128)(2,1)}, bf16[8,16,768]{2,1,0:T(8,128)(2,1)}, f32[16,8,128]{2,1,0:T(8,128)}) custom-call(bf16[1024,128]{1,0:T(8,128)(2,1)} %hid.1, bf16[16,16,384]{2,1,0:T(8,128)(2,1)} %reshape.46.wa, bf16[16,16,1024]{2,1,0:T(8,128)(2,1)} %reshape.48.wm, ...), custom_call_target="tpu_custom_call" | custom-call | bytes 50331648 | tf_op jit(solution)/shard_map/pallas_call | solution.py:51
  69.9 0.0 all-gather.7.cloned.1.call-update
  69.9 0.0 all-gather.5.cloned.1.call-start
  70.0 0.7 all-gather.5.cloned.1.call-update
  70.7 0.0 copy-done.2
  70.7 1.3 copy.23.down
  72.0 0.0 copy-done.4
  72.0 0.6 dynamic_slice.9.lens
  72.6 1.3 constant_dynamic-slice_fusion.1.coef
  73.8 0.0 copy-done
  73.9 0.7 constant_dynamic-slice_fusion.up
  74.5 8.5 %shard_map.113 = (f32[3,512,256]{2,1,0:T(8,128)}, f32[2,512,96]{2,1,0:T(8,128)}) custom-call(bf16[16,512,128]{2,1,0:T(8,128)(2,1)} %get-tuple-element.16.hx.own, f32[8,2048]{1,0:T(8,128)} %bitcast.51, f32[9,2048]{1,0:T(8,128)} %shift.5, bf16[2,2048,384]{2,1,0:T(8,128)(2,1)} %bitcast.50, bf16[2,2048,96]{2,1,0:T(8,128)(2,1)} %copy.23.down), custom_call_target="tpu_custom_call" | custom-call | flops 4000000000 | bytes 16777216 | tf_op jit(solution)/shard_map/pallas_call | solution.py:224
  83.0 24.1 %shard_map.114 = (bf16[512,256]{1,0:T(8,128)(2,1)}, f32[4,4,64,64]{3,2,1,0:T(8,128)}) custom-call(s32[4]{0:T(128)} %dynamic_slice.9.lens, f32[3,512,256]{2,1,0:T(8,128)} %get-tuple-element.19.rkv, f32[2,512,96]{2,1,0:T(8,128)} %get-tuple-element.20.low, f32[6,256]{1,0:T(8,128)} %constant_dynamic-slice_fusion.1.coef, ...), custom_call_target="tpu_custom_call" | custom-call | flops 4000000000 | bytes 16777216 | tf_op jit(solution)/shard_map/pallas_call | solution.py:224
  107.1 5.3 collective-permute-start
  112.5 52.6 %all-gather = bf16[1,128,2048]{2,1,0:T(8,128)(2,1)} all-gather(bf16[1,16,2048]{2,1,0:T(8,128)(2,1)S(1)} %slice.14), channel_id=2, replica_groups=mesh['row'=16,'col'=8] {'col'}, dimensions={1}, use_global_device_ids=true | all-gather | bytes 589824 | tf_op jit(solution)/shard_map/all_gather | solution.py:493
  165.1 44.4 %shard_map.115 = (bf16[8,512,256]{2,1,0:T(8,128)(2,1)}, bf16[2,128,2048]{2,1,0:T(8,128)(2,1)}) custom-call(bf16[512,256]{1,0:T(8,128)(2,1)} %get-tuple-element.21.att, bf16[128,2048]{1,0:T(8,128)(2,1)} %bitcast.38), custom_call_target="tpu_custom_call" | custom-call | bytes 50331648 | tf_op jit(solution)/shard_map/pallas_call | solution.py:51
  209.4 4.2 shard_map.116.mid.own
  213.6 0.0 collective-permute-done
  213.6 0.9 reshape.57
  214.6 0.0 all-gather.7.cloned.1.call-done
  214.6 141.5 %shard_map.117 = (bf16[8,512,256]{2,1,0:T(8,128)(2,1)}, bf16[2,16,8,16,1024]{4,3,2,1,0:T(8,128)(2,1)}) custom-call(bf16[512,256]{1,0:T(8,128)(2,1)} %shard_map.116.mid.own, bf16[8,16,16,1024]{3,2,1,0:T(8,128)(2,1)} %bitcast.36), custom_call_target="tpu_custom_call" | custom-call | bytes 50331648 | tf_op jit(solution)/shard_map/pallas_call | solution.py:51
  356.1 14.7 %shard_map.118.part = bf16[16,512,128]{2,1,0:T(8,128)(2,1)} custom-call(bf16[8,512,256]{2,1,0:T(8,128)(2,1)} %get-tuple-element.25.midg, f32[8,2048]{1,0:T(8,128)} %bitcast.52, f32[9,2048]{1,0:T(8,128)} %shift.5, bf16[2,2048,1024]{2,1,0:T(8,128)(2,1)} %bitcast.49, bf16[512,256]{1,0:T(8,128)(2,1)} %shard_map.116.mid.own), custom_call_target="tpu_custom_call" | custom-call | flops 5000000000 | bytes 16777216 | tf_op jit(solution)/shard_map/pallas_call | solution.py:224
  370.7 40.5 %shard_map.119 = bf16[16,512,128]{2,1,0:T(8,128)(2,1)} custom-call(bf16[16,512,128]{2,1,0:T(8,128)(2,1)} %shard_map.118.part), custom_call_target="tpu_custom_call" | custom-call | bytes 50331648 | tf_op jit(solution)/shard_map/pallas_call | solution.py:51
  411.2 2.6 bitcast_reduce_fusion.out
  413.9 130.0 %shard_map.120.nx = bf16[16,512,128]{2,1,0:T(8,128)(2,1)} custom-call(bf16[1024,128]{1,0:T(8,128)(2,1)} %bitcast_reduce_fusion.out), custom_call_target="tpu_custom_call" | custom-call | bytes 50331648 | tf_op jit(solution)/shard_map/pallas_call | solution.py:51
  543.9 0.0 all-gather.5.cloned.1.call-done.weight
  543.9 7.1 %shard_map.121 = bf16[3,512,256]{2,1,0:T(8,128)(2,1)} custom-call(bf16[16,512,128]{2,1,0:T(8,128)(2,1)} %shard_map.120.nx, f32[8,2048]{1,0:T(8,128)} %bitcast.53, f32[9,2048]{1,0:T(8,128)} %shift.5, bf16[2048,768]{1,0:T(8,128)(2,1)} %all-gather.5.cloned.1.call-done.weight), custom_call_target="tpu_custom_call" | custom-call | flops 2000000000 | bytes 16777216 | tf_op jit(solution)/shard_map/pallas_call | solution.py:224
  (4 shorter events, 0.1 us)
Async XLA Ops:
  7.2 66.7 %copy-start = (bf16[2,96,2048]{2,1,0:T(8,128)(2,1)S(1)}, bf16[2,96,2048]{2,1,0:T(8,128)(2,1)}, u32[]{:S(2)}) copy-start(bf16[2,96,2048]{2,1,0:T(8,128)(2,1)} %param.14) | copy-start | bytes 2359300
  7.2 3.6 copy-start.1
  7.2 207.4 %all-gather.7.cloned.1.call-start = ((), (), s32[]{:S(2)}) async-start(), calls=%async_computation.1 | async-start | bytes 4718592 | tf_op jit(solution)/shard_map/all_gather | solution.py:512
  10.8 1.9 copy-start.3
  11.0 59.6 %copy-start.2 = (bf16[2,2048,96]{1,2,0:T(8,128)(2,1)S(1)}, bf16[2,2048,96]{1,2,0:T(8,128)(2,1)}, u32[]{:S(2)}) copy-start(bf16[2,2048,96]{1,2,0:T(8,128)(2,1)} %param.13) | copy-start | bytes 2359300
  12.8 59.2 %copy-start.4 = (s32[64]{0:T(128)S(1)}, s32[64]{0:T(128)}, u32[]{:S(2)}) copy-start(s32[64]{0:T(128)} %param.10) | copy-start | bytes 772
  69.9 474.0 %all-gather.5.cloned.1.call-start = ((), (), s32[]{:S(2)}) async-start(), calls=%async_computation | async-start | bytes 3342336 | tf_op jit(solution)/shard_map/all_gather | solution.py:513
  107.1 106.5 %collective-permute-start = (f32[4,4,64,64]{3,2,1,0:T(8,128)}, f32[4,4,64,64]{3,2,1,0:T(8,128)S(1)}, u32[]{:S(2)}, u32[]{:S(2)}) collective-permute-start(f32[4,4,64,64]{3,2,1,0:T(8,128)} %get-tuple-element.28), channel_id=1, source_target_pairs={{0,0},{1,16},{2,32},{3,48},{4,64},{5,80},{6,96},{7,112},{8,8},{9,2... | collective-permute-start | bytes 786440 | tf_op jit(solution)/shard_map/ppermute | solution.py:540
Sparse Core Ops, SparseCore 0:
  70.0 105.0 all-gather.6
  176.8 48.5 all-gather.4

commit v2 on v1

--- a/solution.py
+++ b/solution.py
@@ -63,161 +63,262 @@
     )(*operands)
 
 
-def start_kernel(
-    hid, wa, wm, wn, par, hx, wt, wmr, wnr, parg, send_sem, recv_sem, local_sem
-):
+def place():
     r = lax.axis_index("row")
     c = lax.axis_index("col")
     h = lax.rem(r, 2)
-    sibling = r + 1 - 2 * h
+    return r, c, h, lax.div(r, 2), r + 1 - 2 * h
+
+
+class Links:
+    def __init__(self, send_sem, recv_sem, first=0):
+        self.send_sem = send_sem
+        self.recv_sem = recv_sem
+        self.slot = first
+        self.copies = []
+
+    def go(self, source, target, device):
+        copy = send(
+            source, target, self.send_sem.at[self.slot], self.recv_sem.at[self.slot], device
+        )
+        self.slot += 1
+        self.copies.append(copy)
+        return copy
+
+    def finish(self, received=()):
+        done = {id(copy) for copy in received}
+        for copy in self.copies:
+            if id(copy) not in done:
+                copy.wait_recv()
+        for copy in self.copies:
+            copy.wait_send()
+
+
+def ring_peers(r, c):
+    h = lax.rem(r, 2)
+    z_peer = h + 2 * (lax.div(r, 2) + 1 - 2 * lax.rem(lax.div(r, 2), 2))
+    return (z_peer, c), (lax.rem(r + 4, N_ROW), c), (lax.rem(r + 12, N_ROW), c)
+
+
+def ring_gather(links, own, got, ready):
+    r, c, h, q, _ = place()
+    z_peer, plus, minus = ring_peers(r, c)
+    z_chip = q + 1 - 2 * lax.rem(q, 2)
+    before = lax.rem(q + 6, N_CHIP)
+    after = lax.rem(q + 2, N_CHIP)
+    across = lax.rem(q + 4, N_CHIP)
+    first = {}
+    for side in own:
+        ready(side)
+        for name, device in (("p", plus), ("m", minus), ("z", z_peer)):
+            which = own[side][1]
+            first[name, side] = links.go(own[side][0], got.at[2 * q + which], device)
+    sides = list(own)
+    done = []
+
+    def arrived(copy):
+        copy.wait_recv()
+        done.append(copy)
+
+    def forward(chip, side, device):
+        return links.go(got.at[2 * chip + side], got.at[2 * chip + side], device)
+
+    for side in sides:
+        arrived(first["p", side])
+    low = forward(before, 0, plus)
+    for side in sides:
+        arrived(first["m", side])
+    high = forward(after, 1, minus)
+    for side in sides:
+        arrived(first["z", side])
+        which = own[side][1]
+        forward(z_chip, which, plus)
+        forward(z_chip, which, minus)
+    arrived(low)
+    forward(across, 0, z_peer)
+    arrived(high)
+    forward(across, 1, z_peer)
+    return done
+
+
+RING = 14
+
+
+def swap_kernel(square, mlp, par, wa, wm, wn, parg, send_sem, recv_sem, local_sem):
+    r, c, h, q, sibling = place()
     rows = [lax.rem(r + d, N_ROW) for d in range(1, N_ROW)]
     cols = [lax.rem(c + d, N_COL) for d in range(1, N_COL)]
+
+    def time_part(p):
+        return square.at[pl.ds(0, 3), :, pl.ds(pl.multiple_of(p * FEAT, FEAT), FEAT)]
+
+    def mlp_part(p):
+        return mlp.at[:, :, pl.ds(pl.multiple_of(p * MINE, MINE), MINE)]
+
+    def next_part(p):
+        return square.at[pl.ds(4, 3), :, pl.ds(pl.multiple_of(p * SLICE, SLICE), SLICE)]
+
+    local = [
+        keep(time_part(r), wa.at[:, r], local_sem.at[0]),
+        keep(mlp_part(r), wm.at[r], local_sem.at[1]),
+        keep(next_part(c), wn.at[c], local_sem.at[2]),
+        keep(par, parg.at[r], local_sem.at[3]),
+    ]
     greet([(p, c) for p in rows] + [(r, p) for p in cols])
-    slot = iter(range(200))
-
-    def go(source, target, device):
-        at = next(slot)
-        return send(source, target, send_sem.at[at], recv_sem.at[at], device)
-
+    links = Links(send_sem, recv_sem)
+    for p in rows:
+        links.go(mlp_part(p), wm.at[r], (p, c))
+    for p in rows:
+        links.go(time_part(p), wa.at[:, r], (p, c))
+    for p in cols:
+        links.go(next_part(p), wn.at[c], (r, p))
+    for p in rows:
+        links.go(par, parg.at[r], (p, c))
+    links.finish()
+    for copy in local:
+        copy.wait()
+
+
+def start_kernel(hid, wa, hx, wt, send_sem, recv_sem, local_sem):
+    r, c, h, q, sibling = place()
+    cols = [lax.rem(c + d, N_COL) for d in range(1, N_COL)]
+    mine = hid.at[pl.ds(pl.multiple_of(h * MINE, MINE), MINE)]
     local = [
-        keep(wa.at[r], wt.at[h, r, c], local_sem.at[0]),
-        keep(hid.at[pl.ds(h * MINE, MINE)], hx.at[r], local_sem.at[1]),
-        keep(wm.at[r], wmr.at[r], local_sem.at[2]),
-        keep(wn.at[c], wnr.at[c], local_sem.at[3]),
-        keep(par, parg.at[r], local_sem.at[4]),
+        keep(mine, hx.at[r], local_sem.at[0]),
+        keep(wa, wt.at[h, :, :, c], local_sem.at[1]),
     ]
-    first = [go(wa.at[p], wt.at[lax.rem(p, 2), r, c], (p, c)) for p in rows]
-    rest = [
-        go(hid.at[pl.ds(lax.rem(p, 2) * MINE, MINE)], hx.at[r], (p, c)) for p in rows
-    ]
-    rest += [go(par, parg.at[r], (p, c)) for p in rows]
-    for copy in first:
-        copy.wait_recv()
-    local[0].wait()
-    spread = [go(wt.at[h, :, c], wt.at[h, :, c], (r, p)) for p in cols]
-    rest += [go(wt.at[h, :, c], wt.at[h, :, c], (sibling, c))]
-    rest += [go(wm.at[p], wmr.at[r], (p, c)) for p in rows]
-    rest += [go(wn.at[p], wnr.at[c], (r, p)) for p in cols]
+    greet([(sibling, c), *ring_peers(r, c)] + [(r, p) for p in cols])
+    links = Links(send_sem, recv_sem)
+    theirs = links.go(
+        hid.at[pl.ds(pl.multiple_of((1 - h) * MINE, MINE), MINE)], hx.at[r], (sibling, c)
+    )
+    spread = [links.go(wa, wt.at[h, :, :, c], (r, p)) for p in cols]
+    links.go(wa, wt.at[h, :, :, c], (sibling, c))
+    done = [theirs]
+
+    def ready(side):
+        if side == 1:
+            theirs.wait_recv()
+
+    done += ring_gather(links, {0: (mine, h), 1: (hx.at[sibling], 1 - h)}, hx, ready)
     for d in range(1, N_COL):
         spread[d - 1].wait_recv()
+        done.append(spread[d - 1])
         origin = lax.rem(c - d + N_COL, N_COL)
-        rest += [go(wt.at[h, :, origin], wt.at[h, :, origin], (sibling, c))]
-    for copy in rest:
-        copy.wait_recv()
-    for copy in first + spread + rest:
-        copy.wait_send()
-    for copy in local[1:]:
+        links.go(wt.at[h, :, :, origin], wt.at[h, :, :, origin], (sibling, c))
+    links.finish(done)
+    for copy in local:
         copy.wait()
 
 
 def att_kernel(att, w3, attg, w3x, send_sem, recv_sem, local_sem):
-    r = lax.axis_index("row")
-    c = lax.axis_index("col")
-    h = lax.rem(r, 2)
-    q = lax.div(r, 2)
-    sibling = r + 1 - 2 * h
-    rows = [lax.rem(r + 2 * d, N_ROW) for d in range(1, N_CHIP)]
-    greet([(p, c) for p in rows] + [(sibling, c)])
-    local = [keep(att, attg.at[q], local_sem.at[0]), keep(w3, w3x.at[h], local_sem.at[1])]
-    copies = [
-        send(att, attg.at[q], send_sem.at[i], recv_sem.at[i], (p, c))
-        for i, p in enumerate(rows)
+    r, c, h, q, sibling = place()
+    cols = [lax.rem(c + d, N_COL) for d in range(1, N_COL)]
+    local = [
+        keep(att.at[0], attg.at[2 * q], local_sem.at[0]),
+        keep(att.at[1], attg.at[2 * q + 1], local_sem.at[1]),
+        keep(w3, w3x.at[h, c], local_sem.at[2]),
     ]
-    copies += [send(w3, w3x.at[h], send_sem.at[7], recv_sem.at[7], (sibling, c))]
-    for copy in local + copies:
+    greet([(sibling, c), *ring_peers(r, c)] + [(r, p) for p in cols])
+    links = Links(send_sem, recv_sem)
+    spread = [links.go(w3, w3x.at[h, c], (r, p)) for p in cols]
+    links.go(w3, w3x.at[h, c], (sibling, c))
+    done = ring_gather(
+        links, {0: (att.at[0], 0), 1: (att.at[1], 1)}, attg, lambda side: None
+    )
+    for d in range(1, N_COL):
+        spread[d - 1].wait_recv()
+        done.append(spread[d - 1])
+        origin = lax.rem(c - d + N_COL, N_COL)
+        links.go(w3x.at[h, origin], w3x.at[h, origin], (sibling, c))
+    links.finish(done)
+    for copy in local:
         copy.wait()
 
 
-def mid_kernel(mid, wmg, midg, mlpw, send_sem, recv_sem, local_sem):
-    r = lax.axis_index("row")
-    c = lax.axis_index("col")
-    h = lax.rem(r, 2)
-    q = lax.div(r, 2)
-    sibling = r + 1 - 2 * h
-    rows = [lax.rem(r + 2 * d, N_ROW) for d in range(1, N_CHIP)]
-    greet([(p, c) for p in rows] + [(sibling, c)])
-    copies = [
-        send(mid, midg.at[q], send_sem.at[i], recv_sem.at[i], (p, c))
-        for i, p in enumerate(rows)
+def mid_kernel(mid, wmg, midg, theirs, send_sem, recv_sem, local_sem):
+    r, c, h, q, sibling = place()
+    local = [
+        keep(mid.at[0], midg.at[2 * q], local_sem.at[0]),
+        keep(mid.at[1], midg.at[2 * q + 1], local_sem.at[1]),
     ]
-    local = [keep(mid, midg.at[q], local_sem.at[8])]
+    greet([(sibling, c), *ring_peers(r, c)])
+    links = Links(send_sem, recv_sem)
     for k in range(N_COL):
-        copies += [
-            send(
-                wmg.at[k], mlpw.at[h, :, k], send_sem.at[7 + k], recv_sem.at[7 + k], (sibling, c)
-            )
-        ]
-        local += [keep(wmg.at[k], mlpw.at[h, :, k], local_sem.at[k])]
-    for copy in local + copies:
+        for m in range(2):
+            links.go(wmg.at[k, :, m], theirs.at[m, :, k], (sibling, c))
+    done = ring_gather(
+        links, {0: (mid.at[0], 0), 1: (mid.at[1], 1)}, midg, lambda side: None
+    )
+    links.finish(done)
+    for copy in local:
         copy.wait()
 
 
 def sum_kernel(part, got, send_sem, recv_sem, local_sem):
-    r = lax.axis_index("row")
-    c = lax.axis_index("col")
+    r, c, h, q, sibling = place()
     rows = [lax.rem(r + d, N_ROW) for d in range(1, N_ROW)]
+    local = keep(part.at[r], got.at[r], local_sem.at[0])
     greet([(p, c) for p in rows])
-    local = keep(part.at[r], got.at[r], local_sem.at[0])
-    copies = [
-        send(part.at[p], got.at[r], send_sem.at[i], recv_sem.at[i], (p, c))
-        for i, p in enumerate(rows)
-    ]
+    links = Links(send_sem, recv_sem)
+    for p in rows:
+        links.go(part.at[p], got.at[r], (p, c))
+    links.finish()
     local.wait()
-    for copy in copies:
-        copy.wait()
 
 
 def next_kernel(out, got, send_sem, recv_sem, local_sem):
-    r = lax.axis_index("row")
-    c = lax.axis_index("col")
-    h = lax.rem(r, 2)
-    q = lax.div(r, 2)
+    r, c, h, q, sibling = place()
+    cols = [lax.rem(c + d, N_COL) for d in range(1, N_COL)]
     barrier = pltpu.get_barrier_semaphore()
+
+    def target(i):
+        return (2 * c + lax.rem(h + i, 2), q)
 
     @pl.when(q != c)
     def _():
-        pl.semaphore_signal(barrier, inc=1, device_id=(r, q), device_id_type=MESH)
-
-    for d in range(1, N_ROW):
-        pl.semaphore_signal(
-            barrier, inc=1, device_id=(lax.rem(r + d, N_ROW), q), device_id_type=MESH
-        )
-    pl.semaphore_wait(barrier, N_ROW - (q == c).astype(jnp.int32))
-
-    def move(i, e):
+        pl.semaphore_signal(barrier, inc=1, device_id=target(0), device_id_type=MESH)
+
+    for device in [target(1)] + [(r, p) for p in cols]:
+        pl.semaphore_signal(barrier, inc=1, device_id=device, device_id_type=MESH)
+    pl.semaphore_wait(barrier, N_COL + 1 - (q == c).astype(jnp.int32))
+
+    def piece(i):
         half = lax.rem(h + i, 2)
+        return out.at[pl.ds(pl.multiple_of(half * MINE, MINE), MINE)]
+
+    def move(i):
         return pltpu.make_async_remote_copy(
-            src_ref=out.at[pl.ds(half * MINE, MINE)],
-            dst_ref=got.at[r],
-            send_sem=send_sem.at[i * N_COL + e],
-            recv_sem=recv_sem.at[r],
-            device_id=(2 * c + half, lax.rem(c + e, N_COL)),
+            src_ref=piece(i),
+            dst_ref=got.at[2 * q + h],
+            send_sem=send_sem.at[i],
+            recv_sem=recv_sem.at[h],
+            device_id=target(i),
             device_id_type=MESH,
         )
 
     @pl.when(q == c)
     def _():
-        keep(out.at[pl.ds(h * MINE, MINE)], got.at[r], recv_sem.at[r])
+        keep(piece(0), got.at[r], recv_sem.at[h])
 
     @pl.when(q != c)
     def _():
-        move(0, 0).start()
-
-    for e in range(N_COL):
-        for i in range(2):
-            if i + e > 0:
-                move(i, e).start()
-    for s in range(N_ROW):
-        pltpu.make_async_copy(got.at[s], got.at[s], recv_sem.at[s]).wait()
+        move(0).start()
+
+    move(1).start()
+    links = Links(send_sem, recv_sem, 2)
+    for side in range(2):
+        block = got.at[2 * c + side]
+        pltpu.make_async_copy(block, block, recv_sem.at[side]).wait()
+        for p in cols:
+            links.go(block, block, (r, p))
+    links.finish()
 
     @pl.when(q != c)
     def _():
-        move(0, 0).wait_send()
-
-    for e in range(N_COL):
-        for i in range(2):
-            if i + e > 0:
-                move(i, e).wait_send()
+        move(0).wait_send()
+
+    move(1).wait_send()
 
 
 def compute(kernel, outs, operands, scratch=(), grid=None, in_specs=None, out_specs=None, flops=0):
@@ -255,6 +356,10 @@
     return (scaled * gain + bias).astype(BF16).astype(F32)
 
 
+def row_of(par, i):
+    return jnp.concatenate([par[j, i : i + 1, :] for j in range(N_ROW)], axis=1)
+
+
 def step_back(z):
     position = lax.rem(lax.broadcasted_iota(jnp.int32, z.shape, 0), LMAX)
     return jnp.where(position == 0, 0.0, pltpu.roll(z, 1, 0)) - z
@@ -273,13 +378,13 @@
     @pl.loop(0, MINE // TILE)
     def _(m):
         at = pl.multiple_of(m * TILE, TILE)
-        z = norm(blocks_of(hx, at), par[0:1, :], par[1:2, :])
+        z = norm(blocks_of(hx, at), row_of(par, 0), row_of(par, 1))
         dz = step_back(z)
         for j in range(5):
             blend = (z + dz * shift[j : j + 1, :]).astype(BF16)
             if j < 3:
                 weight = jnp.concatenate(
-                    [wt[side, :, j * FEAT : (j + 1) * FEAT] for side in range(2)], axis=1
+                    [wt[side, j].reshape(WIDTH, FEAT) for side in range(2)], axis=1
                 )
                 rkv[j, pl.ds(at, TILE), :] = dot(blend, weight)
             else:
@@ -391,58 +496,71 @@
     center = head_sum(out) * (1.0 / HEAD)
     out = out - center
     spread = head_sum(out * out) * (1.0 / HEAD)
-    att[...] = (out * lax.rsqrt(spread + 0.00064) * coef[4:5, :] + coef[5:6, :]).astype(BF16)
+    out = (out * lax.rsqrt(spread + 0.00064) * coef[4:5, :] + coef[5:6, :]).astype(BF16)
+    for side in range(2):
+        att[side] = out[:, side * FEAT : (side + 1) * FEAT]
 
 
 def project_kernel(attg, own, w3, mid):
     q = lax.div(lax.axis_index("row"), 2)
+
+    @pl.loop(0, MINE // TILE)
+    def _(m):
+        rows = pl.ds(pl.multiple_of(m * TILE, TILE), TILE)
+        wide = jnp.concatenate([attg[j, rows, :] for j in range(N_ROW)], axis=1)
+        weight = w3[...].reshape(SLICE, WIDTH)
+        total = dot(wide, weight, ((1,), (1,)))
+        for side in range(2):
+            mid[side, rows, :] = (
+                own[2 * q + side, rows, :].astype(F32) + total[:, side * FEAT : (side + 1) * FEAT]
+            ).astype(BF16)
+
+
+def mlp_kernel(midg, par, shift, wmg, theirs, own, part, held, act_scr, sems):
+    q = lax.div(lax.axis_index("row"), 2)
+    copies = [
+        pltpu.make_async_copy(wmg.at[k, :, m], held.at[m, :, k], sems.at[m, k])
+        for m in range(2)
+        for k in range(N_COL)
+    ]
+    for copy in copies:
+        copy.start()
+    for copy in copies:
+        copy.wait()
 
     @pl.loop(0, MINE // TILE)
     def _(m):
         at = pl.multiple_of(m * TILE, TILE)
-        wide = jnp.concatenate([attg[j, pl.ds(at, TILE), :] for j in range(N_CHIP)], axis=1)
-        hidden = jnp.concatenate(
-            [own[2 * q + side, pl.ds(at, TILE), :] for side in range(2)], axis=1
-        )
-        mid[pl.ds(at, TILE), :] = (
-            hidden.astype(F32) + dot(wide, w3[...], ((1,), (1,)))
-        ).astype(BF16)
-
-
-def mlp_kernel(midg, par, shift, mlpw, own, part, act_scr):
-    q = lax.div(lax.axis_index("row"), 2)
-
-    @pl.loop(0, MINE // TILE)
-    def _(m):
-        at = pl.multiple_of(m * TILE, TILE)
-        z = norm(blocks_of(midg, at), par[2:3, :], par[3:4, :])
+        z = norm(blocks_of(midg, at), row_of(par, 2), row_of(par, 3))
         blend = (z + step_back(z) * shift[5:6, :]).astype(BF16)
-        for side in range(2):
-            act = jnp.square(jnp.maximum(dot(blend, mlpw[side, :, :MINE]), 0.0))
+        for side, weights in enumerate((held, theirs)):
+            act = jnp.square(jnp.maximum(dot(blend, weights[0].reshape(WIDTH, MINE)), 0.0))
             act_scr[side] = act.astype(BF16)
 
         @pl.loop(0, N_CHIP)
         def _(n):
-            rows = pl.ds(pl.multiple_of(n * SLICE, SLICE), SLICE)
-            total = dot(act_scr[0], mlpw[0, rows, MINE:], ((1,), (1,)))
-            total += dot(act_scr[1], mlpw[1, rows, MINE:], ((1,), (1,)))
-            total += jnp.where(n == q, own[pl.ds(at, TILE), :].astype(F32), 0.0)
+            total = None
+            for side, weights in enumerate((held, theirs)):
+                weight = weights[1, pl.ds(2 * n, 2)].reshape(SLICE, MINE)
+                term = dot(act_scr[side], weight, ((1,), (1,)))
+                total = term if total is None else total + term
             for side in range(2):
-                part[2 * n + side, pl.ds(at, TILE), :] = total[
-                    :, side * FEAT : (side + 1) * FEAT
-                ].astype(BF16)
+                added = jnp.where(n == q, own[side, pl.ds(at, TILE), :].astype(F32), 0.0)
+                part[2 * n + side, pl.ds(at, TILE), :] = (
+                    total[:, side * FEAT : (side + 1) * FEAT] + added
+                ).astype(BF16)
 
 
 def last_kernel(nx, par, shift, weight, out):
     @pl.loop(0, MINE // TILE)
     def _(m):
         at = pl.multiple_of(m * TILE, TILE)
-        z = norm(blocks_of(nx, at), par[4:5, :], par[5:6, :])
+        z = norm(blocks_of(nx, at), row_of(par, 4), row_of(par, 5))
         dz = step_back(z)
         for j in range(3):
             blend = (z + dz * shift[6 + j : 7 + j, :]).astype(BF16)
             out[j, pl.ds(at, TILE), :] = dot(
-                blend, weight[:, j * SLICE : (j + 1) * SLICE]
+                blend, weight[:, :, j].reshape(WIDTH, SLICE)
             ).astype(BF16)
 
 
@@ -450,7 +568,7 @@
     prompts = rkv.shape[1] // LMAX
     return compute(
         core_kernel,
-        [((prompts * LMAX, SLICE), BF16), ((prompts, SLICE // HEAD, HEAD, HEAD), F32)],
+        [((2, prompts * LMAX, FEAT), BF16), ((prompts, SLICE // HEAD, HEAD, HEAD), F32)],
         (lens, rkv, low, coef, up),
         grid=(prompts,),
         in_specs=[
@@ -461,7 +579,7 @@
             pl.BlockSpec(up.shape, lambda p: (0, 0, 0)),
         ],
         out_specs=[
-            pl.BlockSpec((LMAX, SLICE), lambda p: (p, 0)),
+            pl.BlockSpec((2, LMAX, FEAT), lambda p: (0, p, 0)),
             pl.BlockSpec((1, SLICE // HEAD, HEAD, HEAD), lambda p: (p, 0, 0, 0)),
         ],
         flops=4 * 10**9,
@@ -485,37 +603,36 @@
     q = lax.div(r, 2)
     square = square_matrix_shards.astype(BF16)
     mlp = channel_mix_shards.astype(BF16)
-    wa = square[0:3].reshape(3, 16, N_ROW, FEAT).transpose(2, 1, 0, 3).reshape(N_ROW, 16, 3 * FEAT)
-    wm = mlp.reshape(2, 16, N_ROW, MINE).transpose(2, 1, 0, 3).reshape(N_ROW, 16, 2 * MINE)
-    wn = square[4:7].reshape(3, 16, N_COL, SLICE).transpose(2, 1, 0, 3)
-    wn = wn.reshape(N_COL, 16, 3 * SLICE)
-    par = jnp.concatenate([norm_parameters, jnp.zeros((2, FEAT), F32)])
-    w3 = lax.all_gather(square[3], "col", axis=0, tiled=True)
-    hx, wt, wmr, wnr, parg = exchange(
+    wa, wm, wn, parg = exchange(
+        swap_kernel,
+        [
+            ((3, N_ROW, 16, FEAT), BF16),
+            ((N_ROW, 2, 16, MINE), BF16),
+            ((N_COL, 3, 16, SLICE), BF16),
+            ((N_ROW, 6, FEAT), F32),
+        ],
+        52,
+        4,
+        1,
+        square,
+        mlp,
+        norm_parameters,
+    )
+    wmg = lax.all_gather(wm, "col", axis=0)
+    weight_next = lax.all_gather(wn, "row", axis=0)
+    hx, wt = exchange(
         start_kernel,
-        [
-            ((N_ROW, MINE, FEAT), BF16),
-            ((2, N_ROW, N_COL, 16, 3 * FEAT), BF16),
-            ((N_ROW, 16, 2 * MINE), BF16),
-            ((N_COL, 16, 3 * SLICE), BF16),
-            ((N_ROW, 8, FEAT), F32),
-        ],
-        82,
-        5,
-        1,
+        [((N_ROW, MINE, FEAT), BF16), ((2, 3, N_ROW, N_COL, 16, FEAT), BF16)],
+        1 + 7 + 1 + RING + 7,
+        2,
+        6,
         hidden,
         wa,
-        wm,
-        wn,
-        par,
-    )
-    wmg = lax.all_gather(wmr, "col", axis=0)
-    weight_next = lax.all_gather(wnr.reshape(FEAT, 3 * SLICE), "row", axis=0, tiled=True)
-    params = parg.transpose(1, 0, 2).reshape(8, WIDTH)
+    )
     rkv, low = compute(
         mix_kernel,
         [((3, MINE, SLICE), F32), ((2, MINE, lowrank_down.shape[2]), F32)],
-        (hx, params, token_shift_weights, wt.reshape(2, WIDTH, 3 * FEAT), lowrank_down),
+        (hx, parg, token_shift_weights, wt, lowrank_down),
         flops=4 * 10**9,
     )
     coef = lax.dynamic_slice_in_dim(attention_coefficients, q * SLICE, SLICE, 1)
@@ -524,12 +641,12 @@
     att, final = time_core(lens, rkv, low, coef, up)
     attg, w3x = exchange(
         att_kernel,
-        [((N_CHIP, MINE, SLICE), BF16), ((2, FEAT, WIDTH), BF16)],
-        8,
-        2,
+        [((N_ROW, MINE, FEAT), BF16), ((2, N_COL, 16, WIDTH), BF16)],
+        7 + 1 + RING + 7,
+        3,
         2,
         att,
-        w3,
+        square[3],
     )
     moves = [
         ((2 * a + b) * N_COL + d, (2 * d + b) * N_COL + a)
@@ -541,15 +658,15 @@
     final_state = final.reshape(4, 4, HEAD * HEAD)
     (mid,) = compute(
         project_kernel,
-        [((MINE, SLICE), BF16)],
-        (attg, hx, w3x.reshape(SLICE, WIDTH)),
+        [((2, MINE, FEAT), BF16)],
+        (attg, hx, w3x),
         flops=10**9,
     )
-    midg, mlpw = exchange(
+    midg, theirs = exchange(
         mid_kernel,
-        [((N_CHIP, MINE, SLICE), BF16), ((2, N_ROW, N_COL, 16, 2 * MINE), BF16)],
-        15,
-        9,
+        [((N_ROW, MINE, FEAT), BF16), ((2, N_ROW, N_COL, 16, MINE), BF16)],
+        16 + RING,
+        2,
         3,
         mid,
         wmg,
@@ -557,8 +674,13 @@
     (part,) = compute(
         mlp_kernel,
         [((N_ROW, MINE, FEAT), BF16)],
-        (midg, params, token_shift_weights, mlpw.reshape(2, WIDTH, 2 * MINE), mid),
-        scratch=[pltpu.VMEM((2, TILE, MINE), BF16)],
+        (midg, parg, token_shift_weights, wmg, theirs, mid),
+        scratch=[
+            pltpu.VMEM((2, N_ROW, N_COL, 16, MINE), BF16),
+            pltpu.VMEM((2, TILE, MINE), BF16),
+            pltpu.SemaphoreType.DMA((2, N_COL)),
+        ],
+        in_specs=[VMEM, VMEM, VMEM, ANY, VMEM, VMEM],
         flops=5 * 10**9,
     )
     (got,) = exchange(sum_kernel, [((N_ROW, MINE, FEAT), BF16)], 15, 1, 4, part)
@@ -569,7 +691,7 @@
     (next_rkv,) = compute(
         last_kernel,
         [((3, MINE, SLICE), BF16)],
-        (nx, params, token_shift_weights, weight_next),
+        (nx, parg, token_shift_weights, weight_next),
         flops=2 * 10**9,
     )
     return (out_hidden, next_rkv, final_state)

time: 558 us -> 301 us (0.54)
  the two profiles are of different devices: /device:TPU:53 before, /device:TPU:1 now
where the time goes in v2:
time: 301 us; the launch traced here: 297 us
  Pallas kernels  268 us (89%)
  between operations  14.2 us (5%)
  local copies, waits for them, and re-layouts  6.36 us (2%)
  other arithmetic  5.68 us (2%)
    pallas_call x6, Pallas kernels, exchange(): pl.pallas_call(kernel, out_shape=[jax.ShapeDtypeStruct(*out) for out in o...  208 us
    pallas_call x5, Pallas kernels, compute(): pl.pallas_call(kernel, grid=grid if grid is not None else (), out_shape=[...  59.6 us
  transfers between devices with their start and end apart: 3, of which 0 were waited for; matrix products, arithmetic and copies ran while one was open for 3% of the time, Pallas kernels for 81%

profile of v2, /device:TPU:1, one launch (start us, length us, event | category | flops | bytes accessed | tf_op | source)
XLA Modules:
  0.0 296.8 jit_solution(3721096988179175926)
XLA Ops:
  7.2 0.0 copy-start
  7.2 0.0 copy-start.1
  7.2 0.0 copy-start.2
  7.2 0.0 all-gather.5.cloned.1.call-start
  7.2 2.2 convert_element_type.8.square
  9.4 0.0 copy-done.1
  9.4 0.8 convert_element_type.9.mlp
  10.3 0.0 copy-start.3
  10.3 21.2 %shard_map.112 = (bf16[3,16,16,128]{3,2,1,0:T(8,128)(2,1)}, bf16[16,2,16,512]{3,2,1,0:T(8,128)(2,1)}, bf16[8,3,16,256]{3,2,1,0:T(8,128)(2,1)}, f32[16,6,128]{2,1,0:T(8,128)}) custom-call(bf16[7,16,2048]{2,1,0:T(8,128)(2,1)} %convert_element_type.8.square, bf16[2,16,8192]{2,1,0:T(8,128)(2,1)} %convert_element_type.9.mlp, f32[6,128]{1,0:T(8,128)} %par.1), custom_call_target="tpu_custom_call" | custom-call | bytes 50331648 | tf_op jit(solution)/shard_map/pallas_call | solution.py:51
  31.4 0.0 all-gather.5.cloned.1.call-update
  31.5 0.0 all-gather.7.cloned.1.call-start
  31.5 0.7 all-gather.7.cloned.1.call-update
  32.2 0.0 copy-done.2
  32.3 1.3 copy.13.down
  33.6 0.0 copy-done.3
  33.6 0.7 dynamic_slice.9.lens
  34.2 40.1 %shard_map.113 = (bf16[16,512,128]{2,1,0:T(8,128)(2,1)}, bf16[2,3,16,8,16,128]{5,4,3,2,1,0:T(8,128)(2,1)}) custom-call(bf16[1024,128]{1,0:T(8,128)(2,1)} %hid.1, bf16[3,16,16,128]{3,2,1,0:T(8,128)(2,1)} %get-tuple-element.17.wa), custom_call_target="tpu_custom_call" | custom-call | bytes 50331648 | tf_op jit(solution)/shard_map/pallas_call | solution.py:51
  74.4 1.3 constant_dynamic-slice_fusion.1.coef
  75.7 0.0 copy-done
  75.7 0.7 constant_dynamic-slice_fusion.up
  76.3 8.5 %shard_map.114 = (f32[3,512,256]{2,1,0:T(8,128)}, f32[2,512,96]{2,1,0:T(8,128)}) custom-call(bf16[16,512,128]{2,1,0:T(8,128)(2,1)} %get-tuple-element.18.hx.own, f32[16,6,128]{2,1,0:T(8,128)} %get-tuple-element.19.par, f32[9,2048]{1,0:T(8,128)} %shift.5, bf16[2,3,16,8,16,128]{5,4,3,2,1,0:T(8,128)(2,1)} %get-tuple-element.20.wt, bf16[2,2048,96]{2,1,0:T(8,128)(2,1)} %copy.13.down), custom_call_target="tpu_custom_call" | custom-call | flops 4000000000 | bytes 16777216 | tf_op jit(solution)/shard_map/pallas_call | solution.py:325
  84.8 24.2 %shard_map.115 = (bf16[2,512,128]{2,1,0:T(8,128)(2,1)}, f32[4,4,64,64]{3,2,1,0:T(8,128)}) custom-call(s32[4]{0:T(128)} %dynamic_slice.9.lens, f32[3,512,256]{2,1,0:T(8,128)} %get-tuple-element.21.rkv, f32[2,512,96]{2,1,0:T(8,128)} %get-tuple-element.22.low, f32[6,256]{1,0:T(8,128)} %constant_dynamic-slice_fusion.1.coef, ...), custom_call_target="tpu_custom_call" | custom-call | flops 4000000000 | bytes 16777216 | tf_op jit(solution)/shard_map/pallas_call | solution.py:325
  109.0 1.7 collective-permute-start
  110.7 1.5 slice_bitcast_fusion.w3
  112.2 43.7 %shard_map.116 = (bf16[16,512,128]{2,1,0:T(8,128)(2,1)}, bf16[2,8,16,2048]{3,2,1,0:T(8,128)(2,1)}) custom-call(bf16[2,512,128]{2,1,0:T(8,128)(2,1)} %get-tuple-element.23.att, bf16[16,2048]{1,0:T(8,128)(2,1)} %slice_bitcast_fusion.w3), custom_call_target="tpu_custom_call" | custom-call | bytes 50331648 | tf_op jit(solution)/shard_map/pallas_call | solution.py:51
  155.9 4.2 %shard_map.117.mid.own = bf16[2,512,128]{2,1,0:T(8,128)(2,1)} custom-call(bf16[16,512,128]{2,1,0:T(8,128)(2,1)} %get-tuple-element.24.attg, bf16[16,512,128]{2,1,0:T(8,128)(2,1)} %get-tuple-element.18.hx.own, bf16[2,8,16,2048]{3,2,1,0:T(8,128)(2,1)} %get-tuple-element.25.w3), custom_call_target="tpu_custom_call" | custom-call | flops 1000000000 | bytes 16777216 | tf_op jit(solution)/shard_map/pallas_call | solution.py:325
  160.1 0.0 collective-permute-done
  160.1 0.9 reshape.13
  161.0 0.0 all-gather.5.cloned.1.call-done
  161.0 24.9 %shard_map.118 = (bf16[16,512,128]{2,1,0:T(8,128)(2,1)}, bf16[2,16,8,16,512]{4,3,2,1,0:T(8,128)(2,1)}) custom-call(bf16[2,512,128]{2,1,0:T(8,128)(2,1)} %shard_map.117.mid.own, bf16[8,16,2,16,512]{4,3,2,1,0:T(8,128)(2,1)} %bitcast.10), custom_call_target="tpu_custom_call" | custom-call | bytes 50331648 | tf_op jit(solution)/shard_map/pallas_call | solution.py:51
  186.0 15.6 %shard_map.119.part = bf16[16,512,128]{2,1,0:T(8,128)(2,1)} custom-call(bf16[16,512,128]{2,1,0:T(8,128)(2,1)} %get-tuple-element.27.midg, f32[16,6,128]{2,1,0:T(8,128)} %get-tuple-element.19.par, f32[9,2048]{1,0:T(8,128)} %shift.5, bf16[8,16,2,16,512]{4,3,2,1,0:T(8,128)(2,1)} %bitcast.11, bf16[2,16,8,16,512]{4,3,2,1,0:T(8,128)(2,1)} %get-tuple-element.28.theirs, ...), custom_call_target="tpu_custom_call" | custom-call | flops 5000000000 | bytes 16777216 | tf_op jit(solution)/shard_map/pallas_call | solution.py:325
  201.6 37.1 %shard_map.120 = bf16[16,512,128]{2,1,0:T(8,128)(2,1)} custom-call(bf16[16,512,128]{2,1,0:T(8,128)(2,1)} %shard_map.119.part), custom_call_target="tpu_custom_call" | custom-call | bytes 50331648 | tf_op jit(solution)/shard_map/pallas_call | solution.py:51
  238.7 2.6 bitcast_reduce_fusion.out
  241.4 41.5 %shard_map.121.nx = bf16[16,512,128]{2,1,0:T(8,128)(2,1)} custom-call(bf16[1024,128]{1,0:T(8,128)(2,1)} %bitcast_reduce_fusion.out), custom_call_target="tpu_custom_call" | custom-call | bytes 50331648 | tf_op jit(solution)/shard_map/pallas_call | solution.py:51
  282.9 0.0 all-gather.7.cloned.1.call-done
  282.9 7.1 %shard_map.122 = bf16[3,512,256]{2,1,0:T(8,128)(2,1)} custom-call(bf16[16,512,128]{2,1,0:T(8,128)(2,1)} %shard_map.121.nx, f32[16,6,128]{2,1,0:T(8,128)} %get-tuple-element.19.par, f32[9,2048]{1,0:T(8,128)} %shift.5, bf16[16,8,3,16,256]{4,3,2,1,0:T(8,128)(2,1)} %bitcast.12), custom_call_target="tpu_custom_call" | custom-call | flops 2000000000 | bytes 16777216 | tf_op jit(solution)/shard_map/pallas_call | solution.py:325
Async XLA Ops:
  7.2 68.5 %copy-start = (bf16[2,96,2048]{2,1,0:T(8,128)(2,1)S(1)}, bf16[2,96,2048]{2,1,0:T(8,128)(2,1)}, u32[]{:S(2)}) copy-start(bf16[2,96,2048]{2,1,0:T(8,128)(2,1)} %param.14) | copy-start | bytes 2359300
  7.2 2.3 copy-start.1
  7.2 25.1 %copy-start.2 = (bf16[2,2048,96]{1,2,0:T(8,128)(2,1)S(1)}, bf16[2,2048,96]{1,2,0:T(8,128)(2,1)}, u32[]{:S(2)}) copy-start(bf16[2,2048,96]{1,2,0:T(8,128)(2,1)} %param.13) | copy-start | bytes 2359300
  7.2 153.8 %all-gather.5.cloned.1.call-start = ((), (), s32[]{:S(2)}) async-start(), calls=%async_computation | async-start | bytes 4718592 | tf_op jit(solution)/shard_map/all_gather | solution.py:621
  10.3 23.3 %copy-start.3 = (s32[64]{0:T(128)S(1)}, s32[64]{0:T(128)}, u32[]{:S(2)}) copy-start(s32[64]{0:T(128)} %param.10) | copy-start | bytes 772
  31.5 251.4 %all-gather.7.cloned.1.call-start = ((), (), s32[]{:S(2)}) async-start(), calls=%async_computation.1 | async-start | bytes 3342336 | tf_op jit(solution)/shard_map/all_gather | solution.py:622
  109.0 51.1 %collective-permute-start = (f32[4,4,64,64]{3,2,1,0:T(8,128)}, f32[4,4,64,64]{3,2,1,0:T(8,128)S(1)}, u32[]{:S(2)}, u32[]{:S(2)}) collective-permute-start(f32[4,4,64,64]{3,2,1,0:T(8,128)} %get-tuple-element.30), channel_id=1, source_target_pairs={{0,0},{1,16},{2,32},{3,48},{4,64},{5,80},{6,96},{7,112},{8,8},{9,2... | collective-permute-start | bytes 786440 | tf_op jit(solution)/shard_map/ppermute | solution.py:657
Sparse Core Ops, SparseCore 0:
  31.6 106.8 all-gather.4
  140.2 43.9 all-gather.6

commit v3 on v2

--- a/solution.py
+++ b/solution.py
@@ -76,6 +76,7 @@
         self.recv_sem = recv_sem
         self.slot = first
         self.copies = []
+        self.open = []
 
     def go(self, source, target, device):
         copy = send(
@@ -83,174 +84,267 @@
         )
         self.slot += 1
         self.copies.append(copy)
+        self.open.append(copy)
         return copy
 
-    def finish(self, received=()):
-        done = {id(copy) for copy in received}
-        for copy in self.copies:
-            if id(copy) not in done:
-                copy.wait_recv()
+    def arrive(self, copy):
+        copy.wait_recv()
+        self.open = [other for other in self.open if other is not copy]
+
+    def finish(self):
+        for copy in self.open:
+            copy.wait_recv()
         for copy in self.copies:
             copy.wait_send()
 
 
-def ring_peers(r, c):
-    h = lax.rem(r, 2)
-    z_peer = h + 2 * (lax.div(r, 2) + 1 - 2 * lax.rem(lax.div(r, 2), 2))
-    return (z_peer, c), (lax.rem(r + 4, N_ROW), c), (lax.rem(r + 12, N_ROW), c)
-
-
-def ring_gather(links, own, got, ready):
+RING = 14
+
+
+def ring_at(axis):
     r, c, h, q, _ = place()
-    z_peer, plus, minus = ring_peers(r, c)
-    z_chip = q + 1 - 2 * lax.rem(q, 2)
-    before = lax.rem(q + 6, N_CHIP)
-    after = lax.rem(q + 2, N_CHIP)
-    across = lax.rem(q + 4, N_CHIP)
+    here = q if axis == "row" else c
+    step_z = 1 - 2 * lax.rem(here, 2)
+    chips = {
+        "p": lax.rem(here + 2, 8),
+        "m": lax.rem(here + 6, 8),
+        "z": here + step_z,
+        "o": lax.rem(here + 4, 8),
+        "pz": lax.rem(here + 2, 8) + step_z,
+        "mz": lax.rem(here + 6, 8) + step_z,
+        "oz": lax.rem(here + 4, 8) + step_z,
+    }
+    devices = {
+        side: (2 * chips[side] + h, c) if axis == "row" else (r, chips[side]) for side in "pmz"
+    }
+    return here, chips, devices
+
+
+def ring_peers(axis):
+    return list(ring_at(axis)[2].values())
+
+
+def ring(links, axis, slot, own=None, which=(0, 1), ready=None, seen=None):
+    here, chips, to = ring_at(axis)
+    heavy = axis == "row"
+    seen = seen or (lambda chip, half: None)
+
+    def take(copy, chip, half):
+        links.arrive(copy)
+        seen(chip, half)
+
+    def forward(chip, half, side):
+        return links.go(slot(chip, half), slot(chip, half), to[side])
+
     first = {}
-    for side in own:
-        ready(side)
-        for name, device in (("p", plus), ("m", minus), ("z", z_peer)):
-            which = own[side][1]
-            first[name, side] = links.go(own[side][0], got.at[2 * q + which], device)
-    sides = list(own)
-    done = []
-
-    def arrived(copy):
-        copy.wait_recv()
-        done.append(copy)
-
-    def forward(chip, side, device):
-        return links.go(got.at[2 * chip + side], got.at[2 * chip + side], device)
-
-    for side in sides:
-        arrived(first["p", side])
-    low = forward(before, 0, plus)
-    for side in sides:
-        arrived(first["m", side])
-    high = forward(after, 1, minus)
-    for side in sides:
-        arrived(first["z", side])
-        which = own[side][1]
-        forward(z_chip, which, plus)
-        forward(z_chip, which, minus)
-    arrived(low)
-    forward(across, 0, z_peer)
-    arrived(high)
-    forward(across, 1, z_peer)
-    return done
-
-
-RING = 14
-
-
-def swap_kernel(square, mlp, par, wa, wm, wn, parg, send_sem, recv_sem, local_sem):
+    for k in range(2):
+        if ready is not None:
+            ready(k)
+        source = own(k) if own is not None else slot(here, which[k])
+        for side in "pmz":
+            first[side, k] = links.go(source, slot(here, which[k]), to[side])
+    yield
+    for k in range(2):
+        take(first["p", k], chips["m"], which[k])
+    low = forward(chips["m"], 0, "p")
+    for k in range(2):
+        take(first["m", k], chips["p"], which[k])
+    high = forward(chips["p"], 1, "m")
+    yield
+    beside = {}
+    for k in range(2):
+        take(first["z", k], chips["z"], which[k])
+        for side in "pm":
+            beside[side, k] = forward(chips["z"], which[k], side)
+    yield
+    if heavy:
+        take(low, chips["o"], 0)
+        low = forward(chips["o"], 0, "z")
+        take(high, chips["o"], 1)
+        high = forward(chips["o"], 1, "z")
+        yield
+        for k in range(2):
+            take(beside["p", k], chips["mz"], which[k])
+            take(beside["m", k], chips["pz"], which[k])
+    else:
+        take(low, chips["o"], 0)
+        take(high, chips["o"], 1)
+        for k in range(2):
+            take(beside["p", k], chips["mz"], which[k])
+        low = forward(chips["mz"], 0, "p")
+        for k in range(2):
+            take(beside["m", k], chips["pz"], which[k])
+        high = forward(chips["pz"], 1, "m")
+        yield
+    take(low, chips["oz"], 0)
+    take(high, chips["oz"], 1)
+
+
+def together(*steps):
+    active = list(steps)
+    while active:
+        for step in list(active):
+            if next(step, StopIteration) is StopIteration:
+                active.remove(step)
+
+
+def aligned(index, size):
+    return pl.ds(pl.multiple_of(index * size, size), size)
+
+
+def start_kernel(
+    square, mlp, par, hid, hx, wt, w3, wk, wv, wn, parg, send_sem, recv_sem, local_sem
+):
     r, c, h, q, sibling = place()
     rows = [lax.rem(r + d, N_ROW) for d in range(1, N_ROW)]
     cols = [lax.rem(c + d, N_COL) for d in range(1, N_COL)]
 
     def time_part(p):
-        return square.at[pl.ds(0, 3), :, pl.ds(pl.multiple_of(p * FEAT, FEAT), FEAT)]
-
-    def mlp_part(p):
-        return mlp.at[:, :, pl.ds(pl.multiple_of(p * MINE, MINE), MINE)]
+        return square.at[pl.ds(0, 3), :, aligned(p, FEAT)]
+
+    def key_part(p):
+        return mlp.at[0, :, aligned(p, MINE)]
+
+    def value_part(p):
+        return mlp.at[1, :, aligned(p, MINE)]
 
     def next_part(p):
-        return square.at[pl.ds(4, 3), :, pl.ds(pl.multiple_of(p * SLICE, SLICE), SLICE)]
-
+        return square.at[pl.ds(4, 3), :, aligned(p, SLICE)]
+
+    mine = hid.at[aligned(h, MINE)]
     local = [
-        keep(time_part(r), wa.at[:, r], local_sem.at[0]),
-        keep(mlp_part(r), wm.at[r], local_sem.at[1]),
-        keep(next_part(c), wn.at[c], local_sem.at[2]),
-        keep(par, parg.at[r], local_sem.at[3]),
+        keep(time_part(r), wt.at[h, :, r, c], local_sem.at[0]),
+        keep(par, parg.at[r], local_sem.at[1]),
+        keep(mine, hx.at[r], local_sem.at[2]),
+        keep(square.at[3], w3.at[c], local_sem.at[3]),
+        keep(key_part(r), wk.at[c, r], local_sem.at[4]),
+        keep(value_part(r), wv.at[c, r], local_sem.at[5]),
+        keep(next_part(c), wn.at[r, c], local_sem.at[6]),
     ]
     greet([(p, c) for p in rows] + [(r, p) for p in cols])
     links = Links(send_sem, recv_sem)
-    for p in rows:
-        links.go(mlp_part(p), wm.at[r], (p, c))
-    for p in rows:
-        links.go(time_part(p), wa.at[:, r], (p, c))
-    for p in cols:
-        links.go(next_part(p), wn.at[c], (r, p))
-    for p in rows:
-        links.go(par, parg.at[r], (p, c))
+    times = [links.go(time_part(p), wt.at[lax.rem(p, 2), :, r, c], (p, c)) for p in rows]
+    other = links.go(hid.at[aligned(1 - h, MINE)], hx.at[r], (sibling, c))
+
+    def hid_own(k):
+        return (mine, hx.at[sibling])[k]
+
+    def hid_ready(k):
+        if k == 1:
+            links.arrive(other)
+
+    def time_ready(k):
+        if k == 0:
+            for copy in times:
+                links.arrive(copy)
+            local[0].wait()
+            links.go(wt.at[h, :, :, c], wt.at[h, :, :, c], (sibling, c))
+
+    def time_slot(chip, half):
+        return wt.at[h, :, pl.ds(8 * half, 8), chip]
+
+    def time_seen(chip, half):
+        links.go(time_slot(chip, half), time_slot(chip, half), (sibling, c))
+
+    def out_slot(chip, half):
+        return w3.at[chip, :, pl.ds(1024 * half, 1024)]
+
+    def out_own(k):
+        return square.at[3, :, pl.ds(1024 * k, 1024)]
+
+    def rest():
+        for p in rows:
+            links.go(par, parg.at[r], (p, c))
+        yield
+        for p in rows:
+            links.go(key_part(p), wk.at[c, r], (p, c))
+        for p in cols:
+            links.go(next_part(p), wn.at[r, c], (r, p))
+        for p in rows:
+            links.go(value_part(p), wv.at[c, r], (p, c))
+
+    together(
+        ring(
+            links,
+            "row",
+            lambda chip, side: hx.at[2 * chip + side],
+            own=hid_own,
+            which=(h, 1 - h),
+            ready=hid_ready,
+        ),
+        ring(links, "col", time_slot, ready=time_ready, seen=time_seen),
+        rest(),
+        ring(links, "col", out_slot, own=out_own),
+    )
+    links.finish()
+    for copy in local[1:]:
+        copy.wait()
+
+
+def row_ring(links, source, target):
+    return ring(
+        links, "row", lambda chip, side: target.at[2 * chip + side], own=lambda k: source.at[k]
+    )
+
+
+def own_block(source, target, q, local_sem):
+    return [keep(source.at[k], target.at[2 * q + k], local_sem.at[k]) for k in range(2)]
+
+
+def att_kernel(att, w3, wk, attg, w3x, wkg, send_sem, recv_sem, local_sem):
+    r, c, h, q, sibling = place()
+    local = own_block(att, attg, q, local_sem)
+    greet([(sibling, c)] + ring_peers("row") + ring_peers("col"))
+    links = Links(send_sem, recv_sem)
+    links.go(w3, w3x, (sibling, c))
+    together(
+        row_ring(links, att, attg),
+        ring(
+            links,
+            "col",
+            lambda chip, half: wkg.at[chip, pl.ds(8 * half, 8)],
+            own=lambda k: wk.at[c, pl.ds(8 * k, 8)],
+        ),
+    )
     links.finish()
     for copy in local:
         copy.wait()
 
 
-def start_kernel(hid, wa, hx, wt, send_sem, recv_sem, local_sem):
+def mid_kernel(mid, wk, wkg, wv, midg, wvg, theirs, send_sem, recv_sem, local_sem):
     r, c, h, q, sibling = place()
-    cols = [lax.rem(c + d, N_COL) for d in range(1, N_COL)]
-    mine = hid.at[pl.ds(pl.multiple_of(h * MINE, MINE), MINE)]
-    local = [
-        keep(mine, hx.at[r], local_sem.at[0]),
-        keep(wa, wt.at[h, :, :, c], local_sem.at[1]),
-    ]
-    greet([(sibling, c), *ring_peers(r, c)] + [(r, p) for p in cols])
+    local = own_block(mid, midg, q, local_sem)
+    greet([(sibling, c)] + ring_peers("row") + ring_peers("col"))
     links = Links(send_sem, recv_sem)
-    theirs = links.go(
-        hid.at[pl.ds(pl.multiple_of((1 - h) * MINE, MINE), MINE)], hx.at[r], (sibling, c)
-    )
-    spread = [links.go(wa, wt.at[h, :, :, c], (r, p)) for p in cols]
-    links.go(wa, wt.at[h, :, :, c], (sibling, c))
-    done = [theirs]
-
-    def ready(side):
-        if side == 1:
-            theirs.wait_recv()
-
-    done += ring_gather(links, {0: (mine, h), 1: (hx.at[sibling], 1 - h)}, hx, ready)
-    for d in range(1, N_COL):
-        spread[d - 1].wait_recv()
-        done.append(spread[d - 1])
-        origin = lax.rem(c - d + N_COL, N_COL)
-        links.go(wt.at[h, :, :, origin], wt.at[h, :, :, origin], (sibling, c))
-    links.finish(done)
-    for copy in local:
-        copy.wait()
-
-
-def att_kernel(att, w3, attg, w3x, send_sem, recv_sem, local_sem):
-    r, c, h, q, sibling = place()
-    cols = [lax.rem(c + d, N_COL) for d in range(1, N_COL)]
-    local = [
-        keep(att.at[0], attg.at[2 * q], local_sem.at[0]),
-        keep(att.at[1], attg.at[2 * q + 1], local_sem.at[1]),
-        keep(w3, w3x.at[h, c], local_sem.at[2]),
-    ]
-    greet([(sibling, c), *ring_peers(r, c)] + [(r, p) for p in cols])
-    links = Links(send_sem, recv_sem)
-    spread = [links.go(w3, w3x.at[h, c], (r, p)) for p in cols]
-    links.go(w3, w3x.at[h, c], (sibling, c))
-    done = ring_gather(
-        links, {0: (att.at[0], 0), 1: (att.at[1], 1)}, attg, lambda side: None
-    )
-    for d in range(1, N_COL):
-        spread[d - 1].wait_recv()
-        done.append(spread[d - 1])
-        origin = lax.rem(c - d + N_COL, N_COL)
-        links.go(w3x.at[h, origin], w3x.at[h, origin], (sibling, c))
-    links.finish(done)
-    for copy in local:
-        copy.wait()
-
-
-def mid_kernel(mid, wmg, midg, theirs, send_sem, recv_sem, local_sem):
-    r, c, h, q, sibling = place()
-    local = [
-        keep(mid.at[0], midg.at[2 * q], local_sem.at[0]),
-        keep(mid.at[1], midg.at[2 * q + 1], local_sem.at[1]),
-    ]
-    greet([(sibling, c), *ring_peers(r, c)])
-    links = Links(send_sem, recv_sem)
-    for k in range(N_COL):
-        for m in range(2):
-            links.go(wmg.at[k, :, m], theirs.at[m, :, k], (sibling, c))
-    done = ring_gather(
-        links, {0: (mid.at[0], 0), 1: (mid.at[1], 1)}, midg, lambda side: None
-    )
-    links.finish(done)
+
+    def value_slot(chip, half):
+        return wvg.at[chip, pl.ds(8 * half, 8)]
+
+    def value_seen(chip, half):
+        links.go(
+            value_slot(chip, half), theirs.at[1, pl.ds(8 * half, 8), chip], (sibling, c)
+        )
+
+    def across():
+        links.go(wk.at[c], theirs.at[0, :, c], (sibling, c))
+        links.go(wv.at[c], theirs.at[1, :, c], (sibling, c))
+        for d in range(1, N_COL):
+            p = lax.rem(c + d, N_COL)
+            links.go(wkg.at[p], theirs.at[0, :, p], (sibling, c))
+        yield
+
+    together(
+        row_ring(links, mid, midg),
+        ring(
+            links,
+            "col",
+            value_slot,
+            own=lambda k: wv.at[c, pl.ds(8 * k, 8)],
+            seen=value_seen,
+        ),
+        across(),
+    )
+    links.finish()
     for copy in local:
         copy.wait()
 
@@ -267,25 +361,26 @@
     local.wait()
 
 
-def next_kernel(out, got, send_sem, recv_sem, local_sem):
+def next_kernel(out, wn, got, wng, send_sem, recv_sem, local_sem):
     r, c, h, q, sibling = place()
-    cols = [lax.rem(c + d, N_COL) for d in range(1, N_COL)]
     barrier = pltpu.get_barrier_semaphore()
 
     def target(i):
         return (2 * c + lax.rem(h + i, 2), q)
 
+    peers = ring_peers("row") + ring_peers("col") + [(sibling, c)]
+
     @pl.when(q != c)
     def _():
-        pl.semaphore_signal(barrier, inc=1, device_id=target(0), device_id_type=MESH)
-
-    for device in [target(1)] + [(r, p) for p in cols]:
+        for i in range(2):
+            pl.semaphore_signal(barrier, inc=1, device_id=target(i), device_id_type=MESH)
+
+    for device in peers:
         pl.semaphore_signal(barrier, inc=1, device_id=device, device_id_type=MESH)
-    pl.semaphore_wait(barrier, N_COL + 1 - (q == c).astype(jnp.int32))
+    pl.semaphore_wait(barrier, len(peers) + 2 * (q != c).astype(jnp.int32))
 
     def piece(i):
-        half = lax.rem(h + i, 2)
-        return out.at[pl.ds(pl.multiple_of(half * MINE, MINE), MINE)]
+        return out.at[aligned(lax.rem(h + i, 2), MINE)]
 
     def move(i):
         return pltpu.make_async_remote_copy(
@@ -306,13 +401,36 @@
         move(0).start()
 
     move(1).start()
+    local = keep(wn.at[r], wng.at[r], local_sem.at[0])
     links = Links(send_sem, recv_sem, 2)
-    for side in range(2):
-        block = got.at[2 * c + side]
-        pltpu.make_async_copy(block, block, recv_sem.at[side]).wait()
-        for p in cols:
-            links.go(block, block, (r, p))
+
+    def out_ready(k):
+        block = got.at[2 * c + k]
+        pltpu.make_async_copy(block, block, recv_sem.at[k]).wait()
+
+    def weight_slot(chip, half):
+        return wng.at[2 * chip + h, pl.ds(4 * half, 4)]
+
+    def weight_seen(chip, half):
+        links.go(weight_slot(chip, half), weight_slot(chip, half), (sibling, c))
+
+    def across():
+        links.go(wn.at[r], wng.at[r], (sibling, c))
+        yield
+
+    together(
+        across(),
+        ring(
+            links,
+            "row",
+            weight_slot,
+            own=lambda k: wn.at[r, pl.ds(4 * k, 4)],
+            seen=weight_seen,
+        ),
+        ring(links, "col", lambda chip, side: got.at[2 * chip + side], ready=out_ready),
+    )
     links.finish()
+    local.wait()
 
     @pl.when(q != c)
     def _():
@@ -501,28 +619,31 @@
         att[side] = out[:, side * FEAT : (side + 1) * FEAT]
 
 
-def project_kernel(attg, own, w3, mid):
-    q = lax.div(lax.axis_index("row"), 2)
+def project_kernel(attg, own, w3, w3x, mid):
+    r = lax.axis_index("row")
+    h = lax.rem(r, 2)
 
     @pl.loop(0, MINE // TILE)
     def _(m):
         rows = pl.ds(pl.multiple_of(m * TILE, TILE), TILE)
         wide = jnp.concatenate([attg[j, rows, :] for j in range(N_ROW)], axis=1)
-        weight = w3[...].reshape(SLICE, WIDTH)
+        weight = jnp.concatenate([w[...].reshape(FEAT, WIDTH) for w in (w3, w3x)])
         total = dot(wide, weight, ((1,), (1,)))
-        for side in range(2):
+        for k, side in enumerate((h, 1 - h)):
             mid[side, rows, :] = (
-                own[2 * q + side, rows, :].astype(F32) + total[:, side * FEAT : (side + 1) * FEAT]
+                own[r - h + side, rows, :].astype(F32) + total[:, k * FEAT : (k + 1) * FEAT]
             ).astype(BF16)
 
 
-def mlp_kernel(midg, par, shift, wmg, theirs, own, part, held, act_scr, sems):
+def mlp_kernel(midg, par, shift, wk, wkg, wv, wvg, theirs, own, part, held, act_scr, sems):
     q = lax.div(lax.axis_index("row"), 2)
-    copies = [
-        pltpu.make_async_copy(wmg.at[k, :, m], held.at[m, :, k], sems.at[m, k])
-        for m in range(2)
-        for k in range(N_COL)
-    ]
+    c = lax.axis_index("col")
+    copies = []
+    for m, (near, far) in enumerate(((wk, wkg), (wv, wvg))):
+        copies.append(pltpu.make_async_copy(near.at[c], held.at[m, :, c], sems.at[m, 0]))
+        for d in range(1, N_COL):
+            p = lax.rem(c + d, N_COL)
+            copies.append(pltpu.make_async_copy(far.at[p], held.at[m, :, p], sems.at[m, d]))
     for copy in copies:
         copy.start()
     for copy in copies:
@@ -603,31 +724,24 @@
     q = lax.div(r, 2)
     square = square_matrix_shards.astype(BF16)
     mlp = channel_mix_shards.astype(BF16)
-    wa, wm, wn, parg = exchange(
-        swap_kernel,
+    hx, wt, w3, wk, wv, wn, parg = exchange(
+        start_kernel,
         [
-            ((3, N_ROW, 16, FEAT), BF16),
-            ((N_ROW, 2, 16, MINE), BF16),
-            ((N_COL, 3, 16, SLICE), BF16),
+            ((N_ROW, MINE, FEAT), BF16),
+            ((2, 3, N_ROW, N_COL, 16, FEAT), BF16),
+            ((N_COL, 16, WIDTH), BF16),
+            ((N_COL, N_ROW, 16, MINE), BF16),
+            ((N_COL, N_ROW, 16, MINE), BF16),
+            ((N_ROW, N_COL, 3, 16, SLICE), BF16),
             ((N_ROW, 6, FEAT), F32),
         ],
-        52,
-        4,
+        15 + 1 + 3 * RING + 1 + 14 + 15 + 15 + 7 + 15,
+        7,
         1,
         square,
         mlp,
         norm_parameters,
-    )
-    wmg = lax.all_gather(wm, "col", axis=0)
-    weight_next = lax.all_gather(wn, "row", axis=0)
-    hx, wt = exchange(
-        start_kernel,
-        [((N_ROW, MINE, FEAT), BF16), ((2, 3, N_ROW, N_COL, 16, FEAT), BF16)],
-        1 + 7 + 1 + RING + 7,
-        2,
-        6,
         hidden,
-        wa,
     )
     rkv, low = compute(
         mix_kernel,
@@ -639,14 +753,19 @@
     up = lax.dynamic_slice_in_dim(lowrank_up, q * SLICE, SLICE, 2)
     lens = lax.dynamic_slice_in_dim(lengths, c * 8 + h * 4, 4, 0)
     att, final = time_core(lens, rkv, low, coef, up)
-    attg, w3x = exchange(
+    attg, w3x, wkg = exchange(
         att_kernel,
-        [((N_ROW, MINE, FEAT), BF16), ((2, N_COL, 16, WIDTH), BF16)],
-        7 + 1 + RING + 7,
-        3,
+        [
+            ((N_ROW, MINE, FEAT), BF16),
+            ((N_COL, 16, WIDTH), BF16),
+            ((N_COL, N_ROW, 16, MINE), BF16),
+        ],
+        1 + 2 * RING,
+        2,
         2,
         att,
-        square[3],
+        w3,
+        wk,
     )
     moves = [
         ((2 * a + b) * N_COL + d, (2 * d + b) * N_COL + a)
@@ -659,35 +778,49 @@
     (mid,) = compute(
         project_kernel,
         [((2, MINE, FEAT), BF16)],
-        (attg, hx, w3x),
+        (attg, hx, w3, w3x),
         flops=10**9,
     )
-    midg, theirs = exchange(
+    midg, wvg, theirs = exchange(
         mid_kernel,
-        [((N_ROW, MINE, FEAT), BF16), ((2, N_ROW, N_COL, 16, MINE), BF16)],
-        16 + RING,
+        [
+            ((N_ROW, MINE, FEAT), BF16),
+            ((N_COL, N_ROW, 16, MINE), BF16),
+            ((2, N_ROW, N_COL, 16, MINE), BF16),
+        ],
+        9 + 14 + 2 * RING,
         2,
         3,
         mid,
-        wmg,
+        wk,
+        wkg,
+        wv,
     )
     (part,) = compute(
         mlp_kernel,
         [((N_ROW, MINE, FEAT), BF16)],
-        (midg, parg, token_shift_weights, wmg, theirs, mid),
+        (midg, parg, token_shift_weights, wk, wkg, wv, wvg, theirs, mid),
         scratch=[
             pltpu.VMEM((2, N_ROW, N_COL, 16, MINE), BF16),
             pltpu.VMEM((2, TILE, MINE), BF16),
             pltpu.SemaphoreType.DMA((2, N_COL)),
         ],
-        in_specs=[VMEM, VMEM, VMEM, ANY, VMEM, VMEM],
+        in_specs=[VMEM] * 3 + [ANY] * 4 + [VMEM] * 2,
         flops=5 * 10**9,
     )
     (got,) = exchange(sum_kernel, [((N_ROW, MINE, FEAT), BF16)], 15, 1, 4, part)
     out_hidden = (
         jnp.sum(got.reshape(N_CHIP, 2 * MINE, FEAT).astype(F32), axis=0).astype(BF16)
     )
-    (nx,) = exchange(next_kernel, [((N_ROW, MINE, FEAT), BF16)], 16, 1, 5, out_hidden)
+    nx, weight_next = exchange(
+        next_kernel,
+        [((N_ROW, MINE, FEAT), BF16), ((N_ROW, N_COL, 3, 16, SLICE), BF16)],
+        2 + 1 + 14 + 2 * RING,
+        1,
+        5,
+        out_hidden,
+        wn,
+    )
     (next_rkv,) = compute(
         last_kernel,
         [((3, MINE, SLICE), BF16)],

time: 301 us -> 271 us (0.900)
  between operations: 14.2 us -> 0.73 us
  Pallas kernels: 268 us -> 255 us
    pallas_call x6 -> x5, Pallas kernels: 208 us -> 195 us  [exchange(): pl.pallas_call(kernel, out_shape=[jax.ShapeDtypeStruct(*out) for out in o...]
  transfers between devices with their start and end apart: 3 -> 1, of which waited for: 0 -> 0; matrix products, arithmetic and copies ran while one was open for 3% -> 1% of each run, Pallas kernels for 81% -> 68%
where the time goes in v3:
time: 271 us; the launch traced here: 268 us
  Pallas kernels  255 us (94%)
  other arithmetic  5.5 us (2%)
  local copies, waits for them, and re-layouts  4.98 us (2%)
    pallas_call x5, Pallas kernels, exchange(): pl.pallas_call(kernel, out_shape=[jax.ShapeDtypeStruct(*out) for out in o...  195 us
    pallas_call x5, Pallas kernels, compute(): pl.pallas_call(kernel, grid=grid if grid is not None else (), out_shape=[...  59.5 us
  transfers between devices with their start and end apart: 1, of which 0 were waited for; matrix products, arithmetic and copies ran while one was open for 1% of the time, Pallas kernels for 68%

profile of v3, /device:TPU:1, one launch (start us, length us, event | category | flops | bytes accessed | tf_op | source)
XLA Modules:
  0.0 267.5 jit_solution(1170172541601373169)
XLA Ops:
  0.6 0.0 copy-start
  0.6 0.0 copy-start.1
  0.7 0.0 copy-start.2
  0.7 1.4 constant_dynamic-slice_fusion.1.coef
  2.1 0.0 copy-done
  2.1 0.7 constant_dynamic-slice_fusion.up
  2.8 0.0 copy-start.3
  2.8 2.0 convert_element_type.8.square
  4.8 0.0 copy-done.1
  4.8 0.8 convert_element_type.9.mlp
  5.6 0.0 copy-done.2
  5.6 1.3 copy.12.down
  6.9 0.0 copy-done.3
  6.9 0.6 dynamic_slice.9.lens
  7.6 41.0 %shard_map.112 = (bf16[16,512,128]{2,1,0:T(8,128)(2,1)}, bf16[2,3,16,8,16,128]{5,4,3,2,1,0:T(8,128)(2,1)}, bf16[8,16,2048]{2,1,0:T(8,128)(2,1)}, bf16[8,16,16,51...) custom-call(bf16[7,16,2048]{2,1,0:T(8,128)(2,1)} %convert_element_ty, ...), custom_call_target="tpu_custom_call" | custom-call | bytes 50331648 | tf_op jit(solution)/shard_map/pallas_call | solution.py:51
  48.5 8.5 %shard_map.113 = (f32[3,512,256]{2,1,0:T(8,128)}, f32[2,512,96]{2,1,0:T(8,128)}) custom-call(bf16[16,512,128]{2,1,0:T(8,128)(2,1)} %get-tuple-element.22.hx.own, f32[16,6,128]{2,1,0:T(8,128)} %get-tuple-element.23.par, f32[9,2048]{1,0:T(8,128)} %shift.5, bf16[2,3,16,8,16,128]{5,4,3,2,1,0:T(8,128)(2,1)} %get-tuple-element.24.wt, bf16[2,2048,96]{2,1,0:T(8,128)(2,1)} %copy.12.down), custom_call_target="tpu_custom_call" | custom-call | flops 4000000000 | bytes 16777216 | tf_op jit(solution)/shard_map/pallas_call | solution.py:443
  57.0 24.2 %shard_map.114 = (bf16[2,512,128]{2,1,0:T(8,128)(2,1)}, f32[4,4,64,64]{3,2,1,0:T(8,128)}) custom-call(s32[4]{0:T(128)} %dynamic_slice.9.lens, f32[3,512,256]{2,1,0:T(8,128)} %get-tuple-element.25.rkv, f32[2,512,96]{2,1,0:T(8,128)} %get-tuple-element.26.low, f32[6,256]{1,0:T(8,128)} %constant_dynamic-slice_fusion.1.coef, ...), custom_call_target="tpu_custom_call" | custom-call | flops 4000000000 | bytes 16777216 | tf_op jit(solution)/shard_map/pallas_call | solution.py:443
  81.2 1.7 collective-permute-start
  82.9 47.4 %shard_map.115 = (bf16[16,512,128]{2,1,0:T(8,128)(2,1)}, bf16[8,16,2048]{2,1,0:T(8,128)(2,1)}, bf16[8,16,16,512]{3,2,1,0:T(8,128)(2,1)}) custom-call(bf16[2,512,128]{2,1,0:T(8,128)(2,1)} %get-tuple-element.27.att, bf16[8,16,2048]{2,1,0:T(8,128)(2,1)} %get-tuple-element.28.w3, bf16[8,16,16,512]{3,2,1,0:T(8,128)(2,1)} %get-tuple-element.29.wk), custom_call_target="tpu_custom_call" | custom-call | bytes 50331648 | tf_op jit(solution)/shard_map/pallas_call | solution.py:51
  130.3 4.1 %shard_map.116.mid.own = bf16[2,512,128]{2,1,0:T(8,128)(2,1)} custom-call(bf16[16,512,128]{2,1,0:T(8,128)(2,1)} %get-tuple-element.30.attg, bf16[16,512,128]{2,1,0:T(8,128)(2,1)} %get-tuple-element.22.hx.own, bf16[8,16,2048]{2,1,0:T(8,128)(2,1)} %get-tuple-element.28.w3, bf16[8,16,2048]{2,1,0:T(8,128)(2,1)} %get-tuple-element.31.w3x), custom_call_target="tpu_custom_call" | custom-call | flops 1000000000 | bytes 16777216 | tf_op jit(solution)/shard_map/pallas_call | solution.py:443
  134.5 33.4 %shard_map.117 = (bf16[16,512,128]{2,1,0:T(8,128)(2,1)}, bf16[8,16,16,512]{3,2,1,0:T(8,128)(2,1)}, bf16[2,16,8,16,512]{4,3,2,1,0:T(8,128)(2,1)}) custom-call(bf16[2,512,128]{2,1,0:T(8,128)(2,1)} %shard_map.116.mid.own, bf16[8,16,16,512]{3,2,1,0:T(8,128)(2,1)} %get-tuple-element.29.wk, bf16[8,16,16,512]{3,2,1,0:T(8,128)(2,1)} %get-tuple-element.32.wkg, ...), custom_call_target="tpu_custom_call" | custom-call | bytes 50331648 | tf_op jit(solution)/shard_map/pallas_call | solution.py:51
  167.8 15.6 %shard_map.118.part = bf16[16,512,128]{2,1,0:T(8,128)(2,1)} custom-call(bf16[16,512,128]{2,1,0:T(8,128)(2,1)} %get-tuple-element.34.midg, f32[16,6,128]{2,1,0:T(8,128)} %get-tuple-element.23.par, f32[9,2048]{1,0:T(8,128)} %shift.5, bf16[8,16,16,512]{3,2,1,0:T(8,128)(2,1)} %get-tuple-element.29.wk, bf16[8,16,16,512]{3,2,1,0:T(8,128)(2,1)} %get-tuple-element.32.wkg, ...), custom_call_target="tpu_custom_call" | custom-call | flops 5000000000 | bytes 16777216 | tf_op jit(solution)/shard_map/pallas_call | solution.py:443
  183.5 31.5 %shard_map.119 = bf16[16,512,128]{2,1,0:T(8,128)(2,1)} custom-call(bf16[16,512,128]{2,1,0:T(8,128)(2,1)} %shard_map.118.part), custom_call_target="tpu_custom_call" | custom-call | bytes 50331648 | tf_op jit(solution)/shard_map/pallas_call | solution.py:51
  215.0 2.6 bitcast_reduce_fusion.out
  217.6 41.9 %shard_map.120 = (bf16[16,512,128]{2,1,0:T(8,128)(2,1)}, bf16[16,8,3,16,256]{4,3,2,1,0:T(8,128)(2,1)}) custom-call(bf16[1024,128]{1,0:T(8,128)(2,1)} %bitcast_reduce_fusion.out, bf16[16,8,3,16,256]{4,3,2,1,0:T(8,128)(2,1)} %get-tuple-element.37.wn), custom_call_target="tpu_custom_call" | custom-call | bytes 50331648 | tf_op jit(solution)/shard_map/pallas_call | solution.py:51
  259.5 7.1 %shard_map.121 = bf16[3,512,256]{2,1,0:T(8,128)(2,1)} custom-call(bf16[16,512,128]{2,1,0:T(8,128)(2,1)} %get-tuple-element.38.nx, f32[16,6,128]{2,1,0:T(8,128)} %get-tuple-element.23.par, f32[9,2048]{1,0:T(8,128)} %shift.5, bf16[16,8,3,16,256]{4,3,2,1,0:T(8,128)(2,1)} %get-tuple-element.39.weight), custom_call_target="tpu_custom_call" | custom-call | flops 2000000000 | bytes 16777216 | tf_op jit(solution)/shard_map/pallas_call | solution.py:443
  266.6 0.0 collective-permute-done
  266.6 0.9 reshape.13
Async XLA Ops:
  0.6 1.5 copy-start
  0.6 4.2 %copy-start.1 = (f32[2,16,8192]{2,1,0:T(8,128)S(1)}, f32[2,16,8192]{2,1,0:T(8,128)}, u32[]{:S(2)}) copy-start(f32[2,16,8192]{2,1,0:T(8,128)} %param.12) | copy-start | bytes 3145732
  0.7 5.0 %copy-start.2 = (bf16[2,2048,96]{1,2,0:T(8,128)(2,1)S(1)}, bf16[2,2048,96]{1,2,0:T(8,128)(2,1)}, u32[]{:S(2)}) copy-start(bf16[2,2048,96]{1,2,0:T(8,128)(2,1)} %param.13) | copy-start | bytes 2359300
  2.8 4.2 %copy-start.3 = (s32[64]{0:T(128)S(1)}, s32[64]{0:T(128)}, u32[]{:S(2)}) copy-start(s32[64]{0:T(128)} %param.10) | copy-start | bytes 772
  81.2 185.4 %collective-permute-start = (f32[4,4,64,64]{3,2,1,0:T(8,128)}, f32[4,4,64,64]{3,2,1,0:T(8,128)S(1)}, u32[]{:S(2)}, u32[]{:S(2)}) collective-permute-start(f32[4,4,64,64]{3,2,1,0:T(8,128)} %get-tuple-element.40), channel_id=1, source_target_pairs={{0,0},{1,16},{2,32},{3,48},{4,64},{5,80},{6,96},{7,112},{8,8},{9,2... | collective-permute-start | bytes 786440 | tf_op jit(solution)/shard_map/ppermute | solution.py:776

commit v4 on v3

--- a/solution.py
+++ b/solution.py
@@ -47,18 +47,31 @@
     return copy
 
 
-def exchange(kernel, outs, n_remote, n_local, collective_id, *operands):
+def exchange(
+    kernel,
+    outs,
+    n_remote,
+    n_local,
+    collective_id,
+    *operands,
+    scratch=(),
+    in_specs=None,
+    out_specs=None,
+):
     return pl.pallas_call(
         kernel,
         out_shape=[jax.ShapeDtypeStruct(*out) for out in outs],
-        in_specs=[ANY] * len(operands),
-        out_specs=[ANY] * len(outs),
+        in_specs=in_specs or [ANY] * len(operands),
+        out_specs=out_specs or [ANY] * len(outs),
         scratch_shapes=[
             pltpu.SemaphoreType.DMA((n_remote,)),
             pltpu.SemaphoreType.DMA((n_remote,)),
             pltpu.SemaphoreType.DMA((n_local,)),
+            *scratch,
         ],
-        compiler_params=pltpu.CompilerParams(collective_id=collective_id, has_side_effects=True),
+        compiler_params=pltpu.CompilerParams(
+            collective_id=collective_id, has_side_effects=True, vmem_limit_bytes=56 * 2**20
+        ),
         cost_estimate=pl.CostEstimate(flops=0, bytes_accessed=48 * 2**20, transcendentals=0),
     )(*operands)
 
@@ -193,7 +206,24 @@
 
 
 def start_kernel(
-    square, mlp, par, hid, hx, wt, w3, wk, wv, wn, parg, send_sem, recv_sem, local_sem
+    square_in,
+    mlp_in,
+    par,
+    hid,
+    hx,
+    wt,
+    w3,
+    wk,
+    wv,
+    wn,
+    parg,
+    send_sem,
+    recv_sem,
+    local_sem,
+    square_wide,
+    mlp_wide,
+    square,
+    mlp,
 ):
     r, c, h, q, sibling = place()
     rows = [lax.rem(r + d, N_ROW) for d in range(1, N_ROW)]
@@ -212,18 +242,15 @@
         return square.at[pl.ds(4, 3), :, aligned(p, SLICE)]
 
     mine = hid.at[aligned(h, MINE)]
+    square_load = keep(square_in, square_wide, local_sem.at[7])
+    mlp_load = keep(mlp_in, mlp_wide, local_sem.at[8])
     local = [
-        keep(time_part(r), wt.at[h, :, r, c], local_sem.at[0]),
         keep(par, parg.at[r], local_sem.at[1]),
         keep(mine, hx.at[r], local_sem.at[2]),
-        keep(square.at[3], w3.at[c], local_sem.at[3]),
-        keep(key_part(r), wk.at[c, r], local_sem.at[4]),
-        keep(value_part(r), wv.at[c, r], local_sem.at[5]),
-        keep(next_part(c), wn.at[r, c], local_sem.at[6]),
     ]
     greet([(p, c) for p in rows] + [(r, p) for p in cols])
     links = Links(send_sem, recv_sem)
-    times = [links.go(time_part(p), wt.at[lax.rem(p, 2), :, r, c], (p, c)) for p in rows]
+    times = []
     other = links.go(hid.at[aligned(1 - h, MINE)], hx.at[r], (sibling, c))
 
     def hid_own(k):
@@ -237,7 +264,6 @@
         if k == 0:
             for copy in times:
                 links.arrive(copy)
-            local[0].wait()
             links.go(wt.at[h, :, :, c], wt.at[h, :, :, c], (sibling, c))
 
     def time_slot(chip, half):
@@ -252,7 +278,29 @@
     def out_own(k):
         return square.at[3, :, pl.ds(1024 * k, 1024)]
 
+    def feed():
+        square_load.wait()
+        for j in range(3):
+            square[j] = square_wide[j].astype(BF16)
+        for p in rows:
+            times.append(links.go(time_part(p), wt.at[lax.rem(p, 2), :, r, c], (p, c)))
+        own_time = keep(time_part(r), wt.at[h, :, r, c], local_sem.at[0])
+        for j in range(3, 7):
+            square[j] = square_wide[j].astype(BF16)
+        mlp_load.wait()
+        mlp[...] = mlp_wide[...].astype(BF16)
+        own_time.wait()
+        yield
+
     def rest():
+        local.extend(
+            [
+                keep(square.at[3], w3.at[c], local_sem.at[3]),
+                keep(key_part(r), wk.at[c, r], local_sem.at[4]),
+                keep(value_part(r), wv.at[c, r], local_sem.at[5]),
+                keep(next_part(c), wn.at[r, c], local_sem.at[6]),
+            ]
+        )
         for p in rows:
             links.go(par, parg.at[r], (p, c))
         yield
@@ -272,12 +320,13 @@
             which=(h, 1 - h),
             ready=hid_ready,
         ),
+        feed(),
         ring(links, "col", time_slot, ready=time_ready, seen=time_seen),
         rest(),
         ring(links, "col", out_slot, own=out_own),
     )
     links.finish()
-    for copy in local[1:]:
+    for copy in local:
         copy.wait()
 
 
@@ -349,18 +398,6 @@
         copy.wait()
 
 
-def sum_kernel(part, got, send_sem, recv_sem, local_sem):
-    r, c, h, q, sibling = place()
-    rows = [lax.rem(r + d, N_ROW) for d in range(1, N_ROW)]
-    local = keep(part.at[r], got.at[r], local_sem.at[0])
-    greet([(p, c) for p in rows])
-    links = Links(send_sem, recv_sem)
-    for p in rows:
-        links.go(part.at[p], got.at[r], (p, c))
-    links.finish()
-    local.wait()
-
-
 def next_kernel(out, wn, got, wng, send_sem, recv_sem, local_sem):
     r, c, h, q, sibling = place()
     barrier = pltpu.get_barrier_semaphore()
@@ -419,6 +456,7 @@
         yield
 
     together(
+        ring(links, "col", lambda chip, side: got.at[2 * chip + side], ready=out_ready),
         across(),
         ring(
             links,
@@ -427,7 +465,6 @@
             own=lambda k: wn.at[r, pl.ds(4 * k, 4)],
             seen=weight_seen,
         ),
-        ring(links, "col", lambda chip, side: got.at[2 * chip + side], ready=out_ready),
     )
     links.finish()
     local.wait()
@@ -506,12 +543,14 @@
                 )
                 rkv[j, pl.ds(at, TILE), :] = dot(blend, weight)
             else:
-                low[j - 3, pl.ds(at, TILE), :] = dot(blend, down[j - 3])
+                low[j - 3, pl.ds(at, TILE), :] = dot(blend, down[j - 3], ((1,), (1,)))
 
 
 def core_kernel(lens, rkv, low, coef, up, att, final):
-    length = lens[pl.program_id(0)]
+    r, c, h, q, _ = place()
+    length = lens[c * 8 + h * 4 + pl.program_id(0)]
     wide = SLICE
+    channels = aligned(q, SLICE)
     heads = wide // HEAD
     live = (lax.broadcasted_iota(jnp.int32, (LMAX, wide), 0) < length).astype(F32)
     lane = lax.broadcasted_iota(jnp.int32, (LMAX, wide), 1) // HEAD
@@ -533,11 +572,11 @@
     receptance, key, value = rkv[0], rkv[1], rkv[2]
     decay = (
         -0.606531
-        * jax.nn.sigmoid(coef[0:1, :] + dot(jnp.tanh(low[0]).astype(BF16), up[0]))
+        * jax.nn.sigmoid(coef[0:1, channels] + dot(jnp.tanh(low[0]).astype(BF16), up[0, :, channels]))
         * live
     )
-    rate = jax.nn.sigmoid(coef[1:2, :] + dot(low[1].astype(BF16), up[1]))
-    kappa = key * coef[2:3, :]
+    rate = jax.nn.sigmoid(coef[1:2, channels] + dot(low[1].astype(BF16), up[1, :, channels]))
+    kappa = key * coef[2:3, channels]
     kappa = kappa * lax.rsqrt(head_sum(kappa * kappa) + 1e-05)
     remove = -kappa * live
     write = kappa * rate * live
@@ -607,14 +646,20 @@
     tall = tuple(jnp.concatenate([pulled[i], value_parts[i]]) for i in range(2))
     tails = tuple(jnp.concatenate([write_tail[i], key_tail[i]]) for i in range(2))
     state = dot3(tall, tails, ((0,), (0,)))
-    for k in range(heads):
-        final[0, k] = state[k * HEAD : (k + 1) * HEAD, k * HEAD : (k + 1) * HEAD]
-    bonus = head_sum(receptance * key * coef[3:4, :])
+    even = lax.broadcasted_iota(jnp.int32, (HEAD, FEAT), 1) < HEAD
+    for k in range(heads // 2):
+        lanes = slice(k * FEAT, (k + 1) * FEAT)
+        final[0, k] = jnp.where(
+            even,
+            state[k * FEAT : k * FEAT + HEAD, lanes],
+            state[k * FEAT + HEAD : (k + 1) * FEAT, lanes],
+        ).astype(BF16)
+    bonus = head_sum(receptance * key * coef[3:4, channels])
     out = (output + bonus * value) * live
     center = head_sum(out) * (1.0 / HEAD)
     out = out - center
     spread = head_sum(out * out) * (1.0 / HEAD)
-    out = (out * lax.rsqrt(spread + 0.00064) * coef[4:5, :] + coef[5:6, :]).astype(BF16)
+    out = (out * lax.rsqrt(spread + 0.00064) * coef[4:5, channels] + coef[5:6, channels]).astype(BF16)
     for side in range(2):
         att[side] = out[:, side * FEAT : (side + 1) * FEAT]
 
@@ -635,24 +680,62 @@
             ).astype(BF16)
 
 
-def mlp_kernel(midg, par, shift, wk, wkg, wv, wvg, theirs, own, part, held, act_scr, sems):
-    q = lax.div(lax.axis_index("row"), 2)
-    c = lax.axis_index("col")
+STEP = 128
+
+
+def mlp_kernel(
+    midg,
+    par,
+    shift,
+    wk,
+    wkg,
+    wv,
+    wvg,
+    theirs,
+    own,
+    out,
+    send_sem,
+    recv_sem,
+    local_sem,
+    held,
+    act_scr,
+    part,
+    got,
+):
+    r, c, h, q, sibling = place()
     copies = []
     for m, (near, far) in enumerate(((wk, wkg), (wv, wvg))):
-        copies.append(pltpu.make_async_copy(near.at[c], held.at[m, :, c], sems.at[m, 0]))
+        copies.append(keep(near.at[c], held.at[m, :, c], local_sem.at[8 * m]))
         for d in range(1, N_COL):
             p = lax.rem(c + d, N_COL)
-            copies.append(pltpu.make_async_copy(far.at[p], held.at[m, :, p], sems.at[m, d]))
-    for copy in copies:
-        copy.start()
+            copies.append(keep(far.at[p], held.at[m, :, p], local_sem.at[8 * m + d]))
+    rows = [lax.rem(r + d, N_ROW) for d in range(1, N_ROW)]
+    greet([(p, c) for p in rows])
     for copy in copies:
         copy.wait()
 
-    @pl.loop(0, MINE // TILE)
+    def moves(m):
+        tokens = pl.ds(pl.multiple_of(m * STEP, STEP), STEP)
+        return [
+            pltpu.make_async_remote_copy(
+                src_ref=part.at[p, tokens],
+                dst_ref=got.at[r, tokens],
+                send_sem=send_sem.at[m * (N_ROW - 1) + i],
+                recv_sem=recv_sem.at[m * (N_ROW - 1) + i],
+                device_id=(p, c),
+                device_id_type=MESH,
+            )
+            for i, p in enumerate(rows)
+        ]
+
+    @pl.loop(0, MINE // STEP)
     def _(m):
-        at = pl.multiple_of(m * TILE, TILE)
-        z = norm(blocks_of(midg, at), row_of(par, 2), row_of(par, 3))
+        tokens = pl.ds(pl.multiple_of(m * STEP, STEP), STEP)
+        z = norm(
+            jnp.concatenate([midg[j, tokens, :].astype(F32) for j in range(N_ROW)], axis=1),
+            row_of(par, 2),
+            row_of(par, 3),
+        )
         blend = (z + step_back(z) * shift[5:6, :]).astype(BF16)
         for side, weights in enumerate((held, theirs)):
             act = jnp.square(jnp.maximum(dot(blend, weights[0].reshape(WIDTH, MINE)), 0.0))
@@ -666,10 +749,25 @@
                 term = dot(act_scr[side], weight, ((1,), (1,)))
                 total = term if total is None else total + term
             for side in range(2):
-                added = jnp.where(n == q, own[side, pl.ds(at, TILE), :].astype(F32), 0.0)
-                part[2 * n + side, pl.ds(at, TILE), :] = (
+                added = jnp.where(n == q, own[side, tokens, :].astype(F32), 0.0)
+                part[2 * n + side, tokens, :] = (
                     total[:, side * FEAT : (side + 1) * FEAT] + added
                 ).astype(BF16)
+
+        for copy in moves(m):
+            copy.start()
+        got[r, tokens, :] = part[r, tokens, :]
+
+    @pl.loop(0, MINE // STEP)
+    def _(m):
+        for copy in moves(m):
+            copy.wait()
+
+    for side in range(2):
+        total = got[side].astype(F32)
+        for k in range(1, N_CHIP):
+            total += got[2 * k + side].astype(F32)
+        out[pl.ds(side * MINE, MINE), :] = total.astype(BF16)
 
 
 def last_kernel(nx, par, shift, weight, out):
@@ -689,7 +787,7 @@
     prompts = rkv.shape[1] // LMAX
     return compute(
         core_kernel,
-        [((2, prompts * LMAX, FEAT), BF16), ((prompts, SLICE // HEAD, HEAD, HEAD), F32)],
+        [((2, prompts * LMAX, FEAT), BF16), ((prompts, 2, HEAD, FEAT), BF16)],
         (lens, rkv, low, coef, up),
         grid=(prompts,),
         in_specs=[
@@ -701,7 +799,7 @@
         ],
         out_specs=[
             pl.BlockSpec((2, LMAX, FEAT), lambda p: (0, p, 0)),
-            pl.BlockSpec((1, SLICE // HEAD, HEAD, HEAD), lambda p: (p, 0, 0, 0)),
+            pl.BlockSpec((1, 2, HEAD, FEAT), lambda p: (p, 0, 0, 0)),
         ],
         flops=4 * 10**9,
     )
@@ -718,12 +816,6 @@
     attention_coefficients,
     norm_parameters,
 ):
-    r = lax.axis_index("row")
-    c = lax.axis_index("col")
-    h = lax.rem(r, 2)
-    q = lax.div(r, 2)
-    square = square_matrix_shards.astype(BF16)
-    mlp = channel_mix_shards.astype(BF16)
     hx, wt, w3, wk, wv, wn, parg = exchange(
         start_kernel,
         [
@@ -736,23 +828,28 @@
             ((N_ROW, 6, FEAT), F32),
         ],
         15 + 1 + 3 * RING + 1 + 14 + 15 + 15 + 7 + 15,
-        7,
+        9,
         1,
-        square,
-        mlp,
+        square_matrix_shards,
+        channel_mix_shards,
         norm_parameters,
         hidden,
+        scratch=[
+            pltpu.VMEM(square_matrix_shards.shape, F32),
+            pltpu.VMEM(channel_mix_shards.shape, F32),
+            pltpu.VMEM(square_matrix_shards.shape, BF16),
+            pltpu.VMEM(channel_mix_shards.shape, BF16),
+        ],
     )
     rkv, low = compute(
         mix_kernel,
         [((3, MINE, SLICE), F32), ((2, MINE, lowrank_down.shape[2]), F32)],
-        (hx, parg, token_shift_weights, wt, lowrank_down),
+        (hx, parg, token_shift_weights, wt, lowrank_down.transpose(0, 2, 1)),
         flops=4 * 10**9,
     )
-    coef = lax.dynamic_slice_in_dim(attention_coefficients, q * SLICE, SLICE, 1)
-    up = lax.dynamic_slice_in_dim(lowrank_up, q * SLICE, SLICE, 2)
-    lens = lax.dynamic_slice_in_dim(lengths, c * 8 + h * 4, 4, 0)
-    att, final = time_core(lens, rkv, low, coef, up)
+    att, final = time_core(
+        lengths, rkv, low, attention_coefficients, lowrank_up
+    )
     attg, w3x, wkg = exchange(
         att_kernel,
         [
@@ -773,8 +870,6 @@
         for b in range(2)
         for d in range(N_COL)
     ]
-    final = lax.ppermute(final, ("row", "col"), moves)
-    final_state = final.reshape(4, 4, HEAD * HEAD)
     (mid,) = compute(
         project_kernel,
         [((2, MINE, FEAT), BF16)],
@@ -796,21 +891,33 @@
         wkg,
         wv,
     )
-    (part,) = compute(
+    final, midg = lax.optimization_barrier((final, midg))
+    final = lax.ppermute(final, ("row", "col"), moves)
+    final = final.reshape(4, 2, HEAD, 2, HEAD).transpose(0, 1, 3, 2, 4).astype(F32)
+    final_state = final.reshape(4, 4, HEAD * HEAD)
+    (out_hidden,) = exchange(
         mlp_kernel,
-        [((N_ROW, MINE, FEAT), BF16)],
-        (midg, parg, token_shift_weights, wk, wkg, wv, wvg, theirs, mid),
+        [((2 * MINE, FEAT), BF16)],
+        15 * MINE // STEP,
+        16,
+        4,
+        midg,
+        parg,
+        token_shift_weights,
+        wk,
+        wkg,
+        wv,
+        wvg,
+        theirs,
+        mid,
         scratch=[
             pltpu.VMEM((2, N_ROW, N_COL, 16, MINE), BF16),
-            pltpu.VMEM((2, TILE, MINE), BF16),
-            pltpu.SemaphoreType.DMA((2, N_COL)),
+            pltpu.VMEM((2, STEP, MINE), BF16),
+            pltpu.VMEM((N_ROW, MINE, FEAT), BF16),
+            pltpu.VMEM((N_ROW, MINE, FEAT), BF16),
         ],
         in_specs=[VMEM] * 3 + [ANY] * 4 + [VMEM] * 2,
-        flops=5 * 10**9,
-    )
-    (got,) = exchange(sum_kernel, [((N_ROW, MINE, FEAT), BF16)], 15, 1, 4, part)
-    out_hidden = (
-        jnp.sum(got.reshape(N_CHIP, 2 * MINE, FEAT).astype(F32), axis=0).astype(BF16)
+        out_specs=[VMEM],
     )
     nx, weight_next = exchange(
         next_kernel,

time: 271 us -> 232 us (0.86); the launches traced: 268 us -> 232 us
  Pallas kernels: 255 us -> 228 us
  other arithmetic: 5.5 us -> 0 us
  local copies, waits for them, and re-layouts: 4.98 us -> 2 us
    pallas_call x5 -> x4, Pallas kernels: 59.5 us -> 44.1 us  [compute(): pl.pallas_call(kernel, grid=grid if grid is not None else (), out_shape=[...]
    pallas_call x5, Pallas kernels: 195 us -> 184 us  [exchange(): pl.pallas_call(kernel, out_shape=[jax.ShapeDtypeStruct(*out) for out in o...]
    convert_element_type x2 -> x0, other arithmetic: 2.85 us -> none  [the longest x1 2.01 us: per_device(): square = square_matrix_shards.astype(BF16)]
    dynamic_slice x3 -> x0, local copies, waits for them, and re-layouts: 2.74 us -> none  [the longest x1 1.45 us: per_device(): coef = lax.dynamic_slice_in_dim(attention_coefficients, q * SLICE, SLICE, 1)]
  transfers between devices with their start and end apart: 1 -> 1, of which waited for: 0 -> 0; matrix products, arithmetic and copies ran while one was open for 1% -> 0% of each run, Pallas kernels for 68% -> 40%
where the time goes in v4:
time: 232 us
  Pallas kernels  228 us (98%)
    pallas_call x5, Pallas kernels, exchange(): pl.pallas_call(kernel, out_shape=[jax.ShapeDtypeStruct(*out) for out in o...  184 us
    pallas_call x4, Pallas kernels, compute(): pl.pallas_call(kernel, grid=grid if grid is not None else (), out_shape=[...  44.1 us
  transfers between devices with their start and end apart: 1, of which 0 were waited for; matrix products, arithmetic and copies ran while one was open for 0% of the time, Pallas kernels for 40%

profile of v4, /device:TPU:1, one launch (start us, length us, event | category | flops | bytes accessed | tf_op | source)
XLA Modules:
  0.0 231.7 jit_solution(9836317950617118324)
XLA Ops:
  0.6 45.9 %shard_map.112 = (bf16[16,512,128]{2,1,0:T(8,128)(2,1)}, bf16[2,3,16,8,16,128]{5,4,3,2,1,0:T(8,128)(2,1)}, bf16[8,16,2048]{2,1,0:T(8,128)(2,1)}, bf16[8,16,16,51...) custom-call(f32[7,16,2048]{2,1,0:T(8,128)} %square_in.1, ...), custom_call_target="tpu_custom_call" | custom-call | bytes 50331648 | tf_op jit(solution)/shard_map/pallas_call | solution.py:61
  46.6 8.3 %shard_map.113 = (f32[3,512,256]{2,1,0:T(8,128)}, f32[2,512,96]{2,1,0:T(8,128)}) custom-call(bf16[16,512,128]{2,1,0:T(8,128)(2,1)} %get-tuple-element.24.hx.own, f32[16,6,128]{2,1,0:T(8,128)} %get-tuple-element.25.par, f32[9,2048]{1,0:T(8,128)} %shift.5, bf16[2,3,16,8,16,128]{5,4,3,2,1,0:T(8,128)(2,1)} %get-tuple-element.26.wt, bf16[2,96,2048]{2,1,0:T(8,128)(2,1)} %bitcast.7), custom_call_target="tpu_custom_call" | custom-call | flops 4000000000 | bytes 16777216 | tf_op jit(solution)/shard_map/pallas_call | solution.py:480
  54.8 24.6 %shard_map.114 = (bf16[2,512,128]{2,1,0:T(8,128)(2,1)}, bf16[4,2,64,128]{3,2,1,0:T(8,128)(2,1)}) custom-call(s32[64]{0:T(128)} %lens.1, f32[3,512,256]{2,1,0:T(8,128)} %get-tuple-element.27.rkv, f32[2,512,96]{2,1,0:T(8,128)} %get-tuple-element.28.low, f32[6,2048]{1,0:T(8,128)} %coef.1, bf16[2,96,2048]{2,1,0:T(8,128)(2,1)} %up.1), custom_call_target="tpu_custom_call" | custom-call | flops 4000000000 | bytes 16777216 | tf_op jit(solution)/shard_map/pallas_call | solution.py:480
  79.4 25.0 %shard_map.115 = (bf16[16,512,128]{2,1,0:T(8,128)(2,1)}, bf16[8,16,2048]{2,1,0:T(8,128)(2,1)}, bf16[8,16,16,512]{3,2,1,0:T(8,128)(2,1)}) custom-call(bf16[2,512,128]{2,1,0:T(8,128)(2,1)} %get-tuple-element.30.att, bf16[8,16,2048]{2,1,0:T(8,128)(2,1)} %get-tuple-element.31.w3, bf16[8,16,16,512]{3,2,1,0:T(8,128)(2,1)} %get-tuple-element.32.wk), custom_call_target="tpu_custom_call" | custom-call | bytes 50331648 | tf_op jit(solution)/shard_map/pallas_call | solution.py:61
  104.5 4.1 %shard_map.116.mid.own = bf16[2,512,128]{2,1,0:T(8,128)(2,1)} custom-call(bf16[16,512,128]{2,1,0:T(8,128)(2,1)} %get-tuple-element.33.attg, bf16[16,512,128]{2,1,0:T(8,128)(2,1)} %get-tuple-element.24.hx.own, bf16[8,16,2048]{2,1,0:T(8,128)(2,1)} %get-tuple-element.31.w3, bf16[8,16,2048]{2,1,0:T(8,128)(2,1)} %get-tuple-element.34.w3x), custom_call_target="tpu_custom_call" | custom-call | flops 1000000000 | bytes 16777216 | tf_op jit(solution)/shard_map/pallas_call | solution.py:480
  108.6 0.0 copy-start.1
  108.6 28.1 %shard_map.117 = (bf16[16,512,128]{2,1,0:T(8,128)(2,1)}, bf16[8,16,16,512]{3,2,1,0:T(8,128)(2,1)}, bf16[2,16,8,16,512]{4,3,2,1,0:T(8,128)(2,1)}) custom-call(bf16[2,512,128]{2,1,0:T(8,128)(2,1)} %shard_map.116.mid.own, bf16[8,16,16,512]{3,2,1,0:T(8,128)(2,1)} %get-tuple-element.32.wk, bf16[8,16,16,512]{3,2,1,0:T(8,128)(2,1)} %get-tuple-element.35.wkg, ...), custom_call_target="tpu_custom_call" | custom-call | bytes 50331648 | tf_op jit(solution)/shard_map/pallas_call | solution.py:61
  136.6 0.0 copy-done.1
  136.6 0.8 collective-permute-start
  137.5 41.9 %shard_map.118.out = bf16[1024,128]{1,0:T(8,128)(2,1)} custom-call(bf16[16,512,128]{2,1,0:T(8,128)(2,1)} %get-tuple-element.38.midg, f32[16,6,128]{2,1,0:T(8,128)} %get-tuple-element.25.par, f32[9,2048]{1,0:T(8,128)} %shift.5, bf16[8,16,16,512]{3,2,1,0:T(8,128)(2,1)} %get-tuple-element.32.wk, bf16[8,16,16,512]{3,2,1,0:T(8,128)(2,1)} %get-tuple-element.35.wkg, ...), custom_call_target="tpu_custom_call" | custom-call | bytes 50331648 | tf_op jit(solution)/shard_map/pallas_call | solution.py:61
  179.4 43.2 %shard_map.119 = (bf16[16,512,128]{2,1,0:T(8,128)(2,1)}, bf16[16,8,3,16,256]{4,3,2,1,0:T(8,128)(2,1)}) custom-call(bf16[1024,128]{1,0:T(8,128)(2,1)} %shard_map.118.out, bf16[16,8,3,16,256]{4,3,2,1,0:T(8,128)(2,1)} %get-tuple-element.41.wn), custom_call_target="tpu_custom_call" | custom-call | bytes 50331648 | tf_op jit(solution)/shard_map/pallas_call | solution.py:61
  222.6 7.1 %shard_map.120 = bf16[3,512,256]{2,1,0:T(8,128)(2,1)} custom-call(bf16[16,512,128]{2,1,0:T(8,128)(2,1)} %get-tuple-element.42.nx, f32[16,6,128]{2,1,0:T(8,128)} %get-tuple-element.25.par, f32[9,2048]{1,0:T(8,128)} %shift.5, bf16[16,8,3,16,256]{4,3,2,1,0:T(8,128)(2,1)} %get-tuple-element.43.weight), custom_call_target="tpu_custom_call" | custom-call | flops 2000000000 | bytes 16777216 | tf_op jit(solution)/shard_map/pallas_call | solution.py:480
  229.7 0.0 copy-start
  229.7 0.0 collective-permute-done
  229.7 0.3 reshape.21
  230.1 0.9 reshape.18
  231.0 0.0 copy-done
  231.0 0.7 copy.14
  (1 shorter events, 0.0 us)
Async XLA Ops:
  108.6 28.1 %copy-start.1 = (bf16[4,2,64,128]{3,2,1,0:T(8,128)(2,1)S(1)}, bf16[4,2,64,128]{3,2,1,0:T(8,128)(2,1)}, u32[]{:S(2)}) copy-start(bf16[4,2,64,128]{3,2,1,0:T(8,128)(2,1)} %get-tuple-element.44) | copy-start | bytes 393220
  136.6 93.1 %collective-permute-start = (bf16[4,2,64,128]{3,2,1,0:T(8,128)(2,1)S(1)}, bf16[4,2,64,128]{3,2,1,0:T(8,128)(2,1)S(1)}, u32[]{:S(2)}, u32[]{:S(2)}) collective-permute-start(bf16[4,2,64,128]{3,2,1,0:T(8,128)(2,1)S(1)} %copy-done.1), channel_id=1, source_target_pairs={{0,0},{1,16},{2,32},{3,48},{4,64},{5,80},{6,96},{7,112},{8,8},{9,2... | collective-permute-start | bytes 393224 | tf_op jit(solution)/shard_map/ppermute | solution.py:895
  229.7 1.3 copy-start

commit v5 on v4

--- a/solution.py
+++ b/solution.py
@@ -1,3 +1,5 @@
+import functools
+
 import jax
 import jax.numpy as jnp
 from jax import lax
@@ -28,17 +30,25 @@
     pl.semaphore_wait(barrier, len(devices))
 
 
-def send(source, target, send_sem, recv_sem, device):
-    copy = pltpu.make_async_remote_copy(
-        src_ref=source,
-        dst_ref=target,
-        send_sem=send_sem,
-        recv_sem=recv_sem,
-        device_id=device,
-        device_id_type=MESH,
-    )
-    copy.start()
-    return copy
+class Copy:
+    def __init__(self, source, target, send_sem, recv_sem, slot, device):
+        self.made = lambda: pltpu.make_async_remote_copy(
+            src_ref=source() if callable(source) else source,
+            dst_ref=target() if callable(target) else target,
+            send_sem=send_sem.at[slot],
+            recv_sem=recv_sem.at[slot],
+            device_id=device,
+            device_id_type=MESH,
+        )
+
+    def start(self):
+        self.made().start()
+
+    def wait_recv(self):
+        self.made().wait_recv()
+
+    def wait_send(self):
+        self.made().wait_send()
 
 
 def keep(source, target, sem):
@@ -92,9 +102,8 @@
         self.open = []
 
     def go(self, source, target, device):
-        copy = send(
-            source, target, self.send_sem.at[self.slot], self.recv_sem.at[self.slot], device
-        )
+        copy = Copy(source, target, self.send_sem, self.recv_sem, self.slot, device)
+        copy.start()
         self.slot += 1
         self.copies.append(copy)
         self.open.append(copy)
@@ -147,15 +156,16 @@
         seen(chip, half)
 
     def forward(chip, half, side):
-        return links.go(slot(chip, half), slot(chip, half), to[side])
+        return links.go(lambda: slot(chip, half), lambda: slot(chip, half), to[side])
 
     first = {}
     for k in range(2):
         if ready is not None:
             ready(k)
-        source = own(k) if own is not None else slot(here, which[k])
+        target = functools.partial(slot, here, which[k])
+        source = functools.partial(own, k) if own is not None else target
         for side in "pmz":
-            first[side, k] = links.go(source, slot(here, which[k]), to[side])
+            first[side, k] = links.go(source, target, to[side])
     yield
     for k in range(2):
         take(first["p", k], chips["m"], which[k])
@@ -340,26 +350,6 @@
     return [keep(source.at[k], target.at[2 * q + k], local_sem.at[k]) for k in range(2)]
 
 
-def att_kernel(att, w3, wk, attg, w3x, wkg, send_sem, recv_sem, local_sem):
-    r, c, h, q, sibling = place()
-    local = own_block(att, attg, q, local_sem)
-    greet([(sibling, c)] + ring_peers("row") + ring_peers("col"))
-    links = Links(send_sem, recv_sem)
-    links.go(w3, w3x, (sibling, c))
-    together(
-        row_ring(links, att, attg),
-        ring(
-            links,
-            "col",
-            lambda chip, half: wkg.at[chip, pl.ds(8 * half, 8)],
-            own=lambda k: wk.at[c, pl.ds(8 * k, 8)],
-        ),
-    )
-    links.finish()
-    for copy in local:
-        copy.wait()
-
-
 def mid_kernel(mid, wk, wkg, wv, midg, wvg, theirs, send_sem, recv_sem, local_sem):
     r, c, h, q, sibling = place()
     local = own_block(mid, midg, q, local_sem)
@@ -546,9 +536,10 @@
                 low[j - 3, pl.ds(at, TILE), :] = dot(blend, down[j - 3], ((1,), (1,)))
 
 
-def core_kernel(lens, rkv, low, coef, up, att, final):
+def one_prompt(prompt, lens, rkv, low, coef, up, att, final):
     r, c, h, q, _ = place()
-    length = lens[c * 8 + h * 4 + pl.program_id(0)]
+    length = lens[c * 8 + h * 4 + prompt]
+    tokens = aligned(prompt, LMAX)
     wide = SLICE
     channels = aligned(q, SLICE)
     heads = wide // HEAD
@@ -569,13 +560,13 @@
     def only(x, k):
         return jnp.where(lane == k, x, jnp.zeros_like(x))
 
-    receptance, key, value = rkv[0], rkv[1], rkv[2]
+    receptance, key, value = rkv[0, tokens], rkv[1, tokens], rkv[2, tokens]
     decay = (
         -0.606531
-        * jax.nn.sigmoid(coef[0:1, channels] + dot(jnp.tanh(low[0]).astype(BF16), up[0, :, channels]))
+        * jax.nn.sigmoid(coef[0:1, channels] + dot(jnp.tanh(low[0, tokens]).astype(BF16), up[0, :, channels]))
         * live
     )
-    rate = jax.nn.sigmoid(coef[1:2, channels] + dot(low[1].astype(BF16), up[1, :, channels]))
+    rate = jax.nn.sigmoid(coef[1:2, channels] + dot(low[1, tokens].astype(BF16), up[1, :, channels]))
     kappa = key * coef[2:3, channels]
     kappa = kappa * lax.rsqrt(head_sum(kappa * kappa) + 1e-05)
     remove = -kappa * live
@@ -649,7 +640,7 @@
     even = lax.broadcasted_iota(jnp.int32, (HEAD, FEAT), 1) < HEAD
     for k in range(heads // 2):
         lanes = slice(k * FEAT, (k + 1) * FEAT)
-        final[0, k] = jnp.where(
+        final[prompt, k] = jnp.where(
             even,
             state[k * FEAT : k * FEAT + HEAD, lanes],
             state[k * FEAT + HEAD : (k + 1) * FEAT, lanes],
@@ -661,22 +652,135 @@
     spread = head_sum(out * out) * (1.0 / HEAD)
     out = (out * lax.rsqrt(spread + 0.00064) * coef[4:5, channels] + coef[5:6, channels]).astype(BF16)
     for side in range(2):
-        att[side] = out[:, side * FEAT : (side + 1) * FEAT]
-
-
-def project_kernel(attg, own, w3, w3x, mid):
-    r = lax.axis_index("row")
-    h = lax.rem(r, 2)
+        att[side, tokens] = out[:, side * FEAT : (side + 1) * FEAT]
+
+
+PROMPTS = MINE // LMAX
+HOPS = 9
+
+
+def attend_kernel(
+    lens,
+    rkv,
+    low,
+    coef,
+    up,
+    own,
+    w3,
+    wk,
+    mid,
+    final,
+    wkg,
+    send_sem,
+    recv_sem,
+    local_sem,
+    att,
+    attg,
+    w3x,
+):
+    r, c, h, q, sibling = place()
+    _, chips, to = ring_at("row")
+    greet([(sibling, c)] + ring_peers("row") + ring_peers("col"))
+    links = Links(send_sem, recv_sem, PROMPTS * HOPS)
+    links.go(w3, w3x, (sibling, c))
+    near = keep(own.at[pl.ds(pl.multiple_of(r - h, 2), 2)], attg.at[pl.ds(N_ROW, 2)], local_sem.at[0])
+    keys = ring(
+        links,
+        "col",
+        lambda chip, half: wkg.at[chip, pl.ds(8 * half, 8)],
+        own=lambda k: wk.at[c, pl.ds(8 * k, 8)],
+    )
+    next(keys)
+
+    def hop(prompt, slot, chip, side, half=None):
+        def block():
+            tokens = aligned(prompt, LMAX)
+            if half is None:
+                return attg.at[pl.ds(2 * chips.get(chip, q), 2), tokens]
+            return attg.at[2 * chips[chip] + half, tokens]
+
+        def source():
+            return att.at[:, aligned(prompt, LMAX)] if chip == "own" else block()
+
+        return Copy(source, block, send_sem, recv_sem, prompt * HOPS + slot, to[side])
+
+    def hops(prompt):
+        return [
+            hop(prompt, 0, "own", "p"),
+            hop(prompt, 1, "own", "m"),
+            hop(prompt, 2, "own", "z"),
+            hop(prompt, 3, "m", "p", 0),
+            hop(prompt, 4, "p", "m", 1),
+            hop(prompt, 5, "z", "p"),
+            hop(prompt, 6, "z", "m"),
+            hop(prompt, 7, "o", "z", 0),
+            hop(prompt, 8, "o", "z", 1),
+        ]
+
+    @pl.loop(0, PROMPTS + 2)
+    def _(step):
+        @pl.when(step < PROMPTS)
+        def _():
+            one_prompt(step, lens, rkv, low, coef, up, att, final)
+            copies = hops(step)
+            for k in range(3):
+                copies[k].start()
+            tokens = aligned(step, LMAX)
+            for side in range(2):
+                attg[2 * q + side, tokens] = att[side, tokens]
+
+        @pl.when((step >= 1) & (step <= PROMPTS))
+        def _():
+            copies = hops(step - 1)
+            copies[0].wait_recv()
+            copies[3].start()
+            copies[1].wait_recv()
+            copies[4].start()
+            copies[2].wait_recv()
+            copies[5].start()
+            copies[6].start()
+
+        @pl.when(step >= 2)
+        def _():
+            copies = hops(step - 2)
+            copies[3].wait_recv()
+            copies[7].start()
+            copies[4].wait_recv()
+            copies[8].start()
+
+        @pl.when(step == 1)
+        def _():
+            next(keys)
+
+        @pl.when(step == 2)
+        def _():
+            next(keys)
+
+        @pl.when(step == 3)
+        def _():
+            next(keys)
+
+    @pl.loop(0, PROMPTS)
+    def _(prompt):
+        copies = hops(prompt)
+        for k in (5, 6, 7, 8):
+            copies[k].wait_recv()
+        for copy in copies:
+            copy.wait_send()
+
+    together(keys)
+    links.finish()
+    near.wait()
 
     @pl.loop(0, MINE // TILE)
     def _(m):
-        rows = pl.ds(pl.multiple_of(m * TILE, TILE), TILE)
+        rows = aligned(m, TILE)
         wide = jnp.concatenate([attg[j, rows, :] for j in range(N_ROW)], axis=1)
         weight = jnp.concatenate([w[...].reshape(FEAT, WIDTH) for w in (w3, w3x)])
         total = dot(wide, weight, ((1,), (1,)))
         for k, side in enumerate((h, 1 - h)):
             mid[side, rows, :] = (
-                own[r - h + side, rows, :].astype(F32) + total[:, k * FEAT : (k + 1) * FEAT]
+                attg[N_ROW + side, rows, :].astype(F32) + total[:, k * FEAT : (k + 1) * FEAT]
             ).astype(BF16)
 
 
@@ -781,28 +885,6 @@
             out[j, pl.ds(at, TILE), :] = dot(
                 blend, weight[:, :, j].reshape(WIDTH, SLICE)
             ).astype(BF16)
-
-
-def time_core(lens, rkv, low, coef, up):
-    prompts = rkv.shape[1] // LMAX
-    return compute(
-        core_kernel,
-        [((2, prompts * LMAX, FEAT), BF16), ((prompts, 2, HEAD, FEAT), BF16)],
-        (lens, rkv, low, coef, up),
-        grid=(prompts,),
-        in_specs=[
-            pl.BlockSpec(memory_space=pltpu.SMEM),
-            pl.BlockSpec((3, LMAX, SLICE), lambda p: (0, p, 0)),
-            pl.BlockSpec((2, LMAX, low.shape[2]), lambda p: (0, p, 0)),
-            pl.BlockSpec(coef.shape, lambda p: (0, 0)),
-            pl.BlockSpec(up.shape, lambda p: (0, 0, 0)),
-        ],
-        out_specs=[
-            pl.BlockSpec((2, LMAX, FEAT), lambda p: (0, p, 0)),
-            pl.BlockSpec((1, 2, HEAD, FEAT), lambda p: (p, 0, 0, 0)),
-        ],
-        flops=4 * 10**9,
-    )
 
 
 def per_device(
@@ -847,22 +929,31 @@
         (hx, parg, token_shift_weights, wt, lowrank_down.transpose(0, 2, 1)),
         flops=4 * 10**9,
     )
-    att, final = time_core(
-        lengths, rkv, low, attention_coefficients, lowrank_up
-    )
-    attg, w3x, wkg = exchange(
-        att_kernel,
+    mid, final, wkg = exchange(
+        attend_kernel,
         [
-            ((N_ROW, MINE, FEAT), BF16),
-            ((N_COL, 16, WIDTH), BF16),
+            ((2, MINE, FEAT), BF16),
+            ((PROMPTS, 2, HEAD, FEAT), BF16),
             ((N_COL, N_ROW, 16, MINE), BF16),
         ],
-        1 + 2 * RING,
+        PROMPTS * HOPS + 1 + RING,
+        1,
         2,
-        2,
-        att,
+        lengths,
+        rkv,
+        low,
+        attention_coefficients,
+        lowrank_up,
+        hx,
         w3,
         wk,
+        scratch=[
+            pltpu.VMEM((2, MINE, FEAT), BF16),
+            pltpu.VMEM((N_ROW + 2, MINE, FEAT), BF16),
+            pltpu.VMEM((N_COL, 16, WIDTH), BF16),
+        ],
+        in_specs=[pl.BlockSpec(memory_space=pltpu.SMEM)] + [VMEM] * 4 + [ANY, VMEM, ANY],
+        out_specs=[VMEM, VMEM, ANY],
     )
     moves = [
         ((2 * a + b) * N_COL + d, (2 * d + b) * N_COL + a)
@@ -870,12 +961,6 @@
         for b in range(2)
         for d in range(N_COL)
     ]
-    (mid,) = compute(
-        project_kernel,
-        [((2, MINE, FEAT), BF16)],
-        (attg, hx, w3, w3x),
-        flops=10**9,
-    )
     midg, wvg, theirs = exchange(
         mid_kernel,
         [

time: 232 us -> 217 us (0.935)
  Pallas kernels: 228 us -> 214 us
    pallas_call x4 -> x2, Pallas kernels: 44.1 us -> 15.4 us  [compute(): pl.pallas_call(kernel, grid=grid if grid is not None else (), out_shape=[...]
    pallas_call x5, Pallas kernels: 184 us -> 198 us  [exchange(): pl.pallas_call(kernel, out_shape=[jax.ShapeDtypeStruct(*out) for out in o...]
  transfers between devices with their start and end apart: 1 -> 1, of which waited for: 0 -> 0; matrix products, arithmetic and copies ran while one was open for 0% -> 0% of each run, Pallas kernels for 40% -> 42%
where the time goes in v5:
time: 217 us
  Pallas kernels  214 us (99%)
    pallas_call x5, Pallas kernels, exchange(): pl.pallas_call(kernel, out_shape=[jax.ShapeDtypeStruct(*out) for out in o...  198 us
    pallas_call x2, Pallas kernels, compute(): pl.pallas_call(kernel, grid=grid if grid is not None else (), out_shape=[...  15.4 us
  transfers between devices with their start and end apart: 1, of which 0 were waited for; matrix products, arithmetic and copies ran while one was open for 0% of the time, Pallas kernels for 42%

profile of v5, /device:TPU:1, one launch (start us, length us, event | category | flops | bytes accessed | tf_op | source)
XLA Modules:
  0.0 217.1 jit_solution(994401722036302940)
XLA Ops:
  0.6 45.9 %shard_map.112 = (bf16[16,512,128]{2,1,0:T(8,128)(2,1)}, bf16[2,3,16,8,16,128]{5,4,3,2,1,0:T(8,128)(2,1)}, bf16[8,16,2048]{2,1,0:T(8,128)(2,1)}, bf16[8,16,16,51...) custom-call(f32[7,16,2048]{2,1,0:T(8,128)} %square_in.1, ...), custom_call_target="tpu_custom_call" | custom-call | bytes 50331648 | tf_op jit(solution)/shard_map/pallas_call | solution.py:71
  46.6 8.3 %shard_map.113 = (f32[3,512,256]{2,1,0:T(8,128)}, f32[2,512,96]{2,1,0:T(8,128)}) custom-call(bf16[16,512,128]{2,1,0:T(8,128)(2,1)} %get-tuple-element.22.hx.own, f32[16,6,128]{2,1,0:T(8,128)} %get-tuple-element.23.par, f32[9,2048]{1,0:T(8,128)} %shift.5, bf16[2,3,16,8,16,128]{5,4,3,2,1,0:T(8,128)(2,1)} %get-tuple-element.24.wt, bf16[2,96,2048]{2,1,0:T(8,128)(2,1)} %bitcast.7), custom_call_target="tpu_custom_call" | custom-call | flops 4000000000 | bytes 16777216 | tf_op jit(solution)/shard_map/pallas_call | solution.py:470
  54.8 38.2 %shard_map.114 = (bf16[2,512,128]{2,1,0:T(8,128)(2,1)}, bf16[4,2,64,128]{3,2,1,0:T(8,128)(2,1)}, bf16[8,16,16,512]{3,2,1,0:T(8,128)(2,1)}) custom-call(s32[64]{0:T(128)} %lens.1, f32[3,512,256]{2,1,0:T(8,128)} %get-tuple-element.25.rkv, f32[2,512,96]{2,1,0:T(8,128)} %get-tuple-element.26.low, f32[6,2048]{1,0:T(8,128)} %coef.1, bf16[2,96,2048]{2,1,0:T(8,128)(2,1)} %up.1, ...), custom_call_target="tpu_custom_call" | custom-call | bytes 50331648 | tf_op jit(solution)/shard_map/pallas_call | solution.py:71
  93.0 0.0 copy-start.1
  93.1 29.5 %shard_map.115 = (bf16[16,512,128]{2,1,0:T(8,128)(2,1)}, bf16[8,16,16,512]{3,2,1,0:T(8,128)(2,1)}, bf16[2,16,8,16,512]{4,3,2,1,0:T(8,128)(2,1)}) custom-call(bf16[2,512,128]{2,1,0:T(8,128)(2,1)} %get-tuple-element.30.mid.own, bf16[8,16,16,512]{3,2,1,0:T(8,128)(2,1)} %get-tuple-element.28.wk, bf16[8,16,16,512]{3,2,1,0:T(8,128)(2,1)} %get-tuple-element.31.wkg, ...), custom_call_target="tpu_custom_call" | custom-call | bytes 50331648 | tf_op jit(solution)/shard_map/pallas_call | solution.py:71
  122.5 0.0 copy-done.1
  122.5 0.8 collective-permute-start
  123.4 40.3 %shard_map.116.out = bf16[1024,128]{1,0:T(8,128)(2,1)} custom-call(bf16[16,512,128]{2,1,0:T(8,128)(2,1)} %get-tuple-element.34.midg, f32[16,6,128]{2,1,0:T(8,128)} %get-tuple-element.23.par, f32[9,2048]{1,0:T(8,128)} %shift.5, bf16[8,16,16,512]{3,2,1,0:T(8,128)(2,1)} %get-tuple-element.28.wk, bf16[8,16,16,512]{3,2,1,0:T(8,128)(2,1)} %get-tuple-element.31.wkg, ...), custom_call_target="tpu_custom_call" | custom-call | bytes 50331648 | tf_op jit(solution)/shard_map/pallas_call | solution.py:71
  163.7 44.2 %shard_map.117 = (bf16[16,512,128]{2,1,0:T(8,128)(2,1)}, bf16[16,8,3,16,256]{4,3,2,1,0:T(8,128)(2,1)}) custom-call(bf16[1024,128]{1,0:T(8,128)(2,1)} %shard_map.116.out, bf16[16,8,3,16,256]{4,3,2,1,0:T(8,128)(2,1)} %get-tuple-element.37.wn), custom_call_target="tpu_custom_call" | custom-call | bytes 50331648 | tf_op jit(solution)/shard_map/pallas_call | solution.py:71
  208.0 7.1 %shard_map.118 = bf16[3,512,256]{2,1,0:T(8,128)(2,1)} custom-call(bf16[16,512,128]{2,1,0:T(8,128)(2,1)} %get-tuple-element.38.nx, f32[16,6,128]{2,1,0:T(8,128)} %get-tuple-element.23.par, f32[9,2048]{1,0:T(8,128)} %shift.5, bf16[16,8,3,16,256]{4,3,2,1,0:T(8,128)(2,1)} %get-tuple-element.39.weight), custom_call_target="tpu_custom_call" | custom-call | flops 2000000000 | bytes 16777216 | tf_op jit(solution)/shard_map/pallas_call | solution.py:470
  215.1 0.0 copy-start
  215.1 0.0 collective-permute-done
  215.1 0.3 reshape.21
  215.4 0.9 reshape.18
  216.4 0.0 copy-done
  216.4 0.7 copy.14
  (1 shorter events, 0.0 us)
Async XLA Ops:
  93.0 29.5 %copy-start.1 = (bf16[4,2,64,128]{3,2,1,0:T(8,128)(2,1)S(1)}, bf16[4,2,64,128]{3,2,1,0:T(8,128)(2,1)}, u32[]{:S(2)}) copy-start(bf16[4,2,64,128]{3,2,1,0:T(8,128)(2,1)} %get-tuple-element.40) | copy-start | bytes 393220
  122.5 92.5 %collective-permute-start = (bf16[4,2,64,128]{3,2,1,0:T(8,128)(2,1)S(1)}, bf16[4,2,64,128]{3,2,1,0:T(8,128)(2,1)S(1)}, u32[]{:S(2)}, u32[]{:S(2)}) collective-permute-start(bf16[4,2,64,128]{3,2,1,0:T(8,128)(2,1)S(1)} %copy-done.1), channel_id=1, source_target_pairs={{0,0},{1,16},{2,32},{3,48},{4,64},{5,80},{6,96},{7,112},{8,8},{9,2... | collective-permute-start | bytes 393224 | tf_op jit(solution)/shard_map/ppermute | solution.py:980
  215.1 1.3 copy-start

commit v6 on v5

--- a/solution.py
+++ b/solution.py
@@ -146,9 +146,9 @@
     return list(ring_at(axis)[2].values())
 
 
-def ring(links, axis, slot, own=None, which=(0, 1), ready=None, seen=None):
+def ring(links, axis, slot, own=None, which=(0, 1), ready=None, seen=None, heavy=None):
     here, chips, to = ring_at(axis)
-    heavy = axis == "row"
+    heavy = axis == "row" if heavy is None else heavy
     seen = seen or (lambda chip, half: None)
 
     def take(copy, chip, half):
@@ -164,7 +164,7 @@
             ready(k)
         target = functools.partial(slot, here, which[k])
         source = functools.partial(own, k) if own is not None else target
-        for side in "pmz":
+        for side in "zpm":
             first[side, k] = links.go(source, target, to[side])
     yield
     for k in range(2):
@@ -261,6 +261,7 @@
     greet([(p, c) for p in rows] + [(r, p) for p in cols])
     links = Links(send_sem, recv_sem)
     times = []
+    own_time = []
     other = links.go(hid.at[aligned(1 - h, MINE)], hx.at[r], (sibling, c))
 
     def hid_own(k):
@@ -294,12 +295,15 @@
             square[j] = square_wide[j].astype(BF16)
         for p in rows:
             times.append(links.go(time_part(p), wt.at[lax.rem(p, 2), :, r, c], (p, c)))
-        own_time = keep(time_part(r), wt.at[h, :, r, c], local_sem.at[0])
+        own_time.append(keep(time_part(r), wt.at[h, :, r, c], local_sem.at[0]))
+        yield
+
+    def casts():
         for j in range(3, 7):
             square[j] = square_wide[j].astype(BF16)
         mlp_load.wait()
         mlp[...] = mlp_wide[...].astype(BF16)
-        own_time.wait()
+        own_time[0].wait()
         yield
 
     def rest():
@@ -322,6 +326,7 @@
             links.go(value_part(p), wv.at[c, r], (p, c))
 
     together(
+        feed(),
         ring(
             links,
             "row",
@@ -330,7 +335,7 @@
             which=(h, 1 - h),
             ready=hid_ready,
         ),
-        feed(),
+        casts(),
         ring(links, "col", time_slot, ready=time_ready, seen=time_seen),
         rest(),
         ring(links, "col", out_slot, own=out_own),
@@ -386,84 +391,6 @@
     links.finish()
     for copy in local:
         copy.wait()
-
-
-def next_kernel(out, wn, got, wng, send_sem, recv_sem, local_sem):
-    r, c, h, q, sibling = place()
-    barrier = pltpu.get_barrier_semaphore()
-
-    def target(i):
-        return (2 * c + lax.rem(h + i, 2), q)
-
-    peers = ring_peers("row") + ring_peers("col") + [(sibling, c)]
-
-    @pl.when(q != c)
-    def _():
-        for i in range(2):
-            pl.semaphore_signal(barrier, inc=1, device_id=target(i), device_id_type=MESH)
-
-    for device in peers:
-        pl.semaphore_signal(barrier, inc=1, device_id=device, device_id_type=MESH)
-    pl.semaphore_wait(barrier, len(peers) + 2 * (q != c).astype(jnp.int32))
-
-    def piece(i):
-        return out.at[aligned(lax.rem(h + i, 2), MINE)]
-
-    def move(i):
-        return pltpu.make_async_remote_copy(
-            src_ref=piece(i),
-            dst_ref=got.at[2 * q + h],
-            send_sem=send_sem.at[i],
-            recv_sem=recv_sem.at[h],
-            device_id=target(i),
-            device_id_type=MESH,
-        )
-
-    @pl.when(q == c)
-    def _():
-        keep(piece(0), got.at[r], recv_sem.at[h])
-
-    @pl.when(q != c)
-    def _():
-        move(0).start()
-
-    move(1).start()
-    local = keep(wn.at[r], wng.at[r], local_sem.at[0])
-    links = Links(send_sem, recv_sem, 2)
-
-    def out_ready(k):
-        block = got.at[2 * c + k]
-        pltpu.make_async_copy(block, block, recv_sem.at[k]).wait()
-
-    def weight_slot(chip, half):
-        return wng.at[2 * chip + h, pl.ds(4 * half, 4)]
-
-    def weight_seen(chip, half):
-        links.go(weight_slot(chip, half), weight_slot(chip, half), (sibling, c))
-
-    def across():
-        links.go(wn.at[r], wng.at[r], (sibling, c))
-        yield
-
-    together(
-        ring(links, "col", lambda chip, side: got.at[2 * chip + side], ready=out_ready),
-        across(),
-        ring(
-            links,
-            "row",
-            weight_slot,
-            own=lambda k: wn.at[r, pl.ds(4 * k, 4)],
-            seen=weight_seen,
-        ),
-    )
-    links.finish()
-    local.wait()
-
-    @pl.when(q != c)
-    def _():
-        move(0).wait_send()
-
-    move(1).wait_send()
 
 
 def compute(kernel, outs, operands, scratch=(), grid=None, in_specs=None, out_specs=None, flops=0):
@@ -668,9 +595,11 @@
     own,
     w3,
     wk,
+    wn,
     mid,
     final,
     wkg,
+    wng,
     send_sem,
     recv_sem,
     local_sem,
@@ -690,7 +619,30 @@
         lambda chip, half: wkg.at[chip, pl.ds(8 * half, 8)],
         own=lambda k: wk.at[c, pl.ds(8 * k, 8)],
     )
-    next(keys)
+    far = keep(wn.at[r], wng.at[r], local_sem.at[1])
+    links.go(wn.at[r], wng.at[r], (sibling, c))
+
+    def weight_slot(chip, half):
+        return wng.at[2 * chip + h, pl.ds(4 * half, 4)]
+
+    def weight_seen(chip, half):
+        links.go(
+            lambda: weight_slot(chip, half), lambda: weight_slot(chip, half), (sibling, c)
+        )
+
+    weights = ring(
+        links,
+        "row",
+        weight_slot,
+        own=lambda k: wn.at[r, pl.ds(4 * k, 4)],
+        seen=weight_seen,
+    )
+
+    def advance():
+        for steps in (keys, weights):
+            next(steps)
+
+    advance()
 
     def hop(prompt, slot, chip, side, half=None):
         def block():
@@ -750,15 +702,15 @@
 
         @pl.when(step == 1)
         def _():
-            next(keys)
+            advance()
 
         @pl.when(step == 2)
         def _():
-            next(keys)
+            advance()
 
         @pl.when(step == 3)
         def _():
-            next(keys)
+            advance()
 
     @pl.loop(0, PROMPTS)
     def _(prompt):
@@ -768,9 +720,10 @@
         for copy in copies:
             copy.wait_send()
 
-    together(keys)
+    together(keys, weights)
     links.finish()
     near.wait()
+    far.wait()
 
     @pl.loop(0, MINE // TILE)
     def _(m):
@@ -784,10 +737,7 @@
             ).astype(BF16)
 
 
-STEP = 128
-
-
-def mlp_kernel(
+def tail_kernel(
     midg,
     par,
     shift,
@@ -797,7 +747,11 @@
     wvg,
     theirs,
     own,
+    wng,
+    state,
     out,
+    rkv,
+    final,
     send_sem,
     recv_sem,
     local_sem,
@@ -805,41 +759,110 @@
     act_scr,
     part,
     got,
+    nx,
+    weight,
 ):
     r, c, h, q, sibling = place()
+    _, chips, to = ring_at("col")
     copies = []
     for m, (near, far) in enumerate(((wk, wkg), (wv, wvg))):
         copies.append(keep(near.at[c], held.at[m, :, c], local_sem.at[8 * m]))
         for d in range(1, N_COL):
             p = lax.rem(c + d, N_COL)
             copies.append(keep(far.at[p], held.at[m, :, p], local_sem.at[8 * m + d]))
+    load = keep(wng, weight, local_sem.at[16])
     rows = [lax.rem(r + d, N_ROW) for d in range(1, N_ROW)]
-    greet([(p, c) for p in rows])
+    n_sum = PROMPTS * (N_ROW - 1)
+    n_turn = n_sum + 2 * PROMPTS
+    n_ring = n_turn + PROMPTS * HOPS
+
+    def target(i):
+        return (2 * c + lax.rem(h + i, 2), q)
+
+    barrier = pltpu.get_barrier_semaphore()
+    peers = [(p, c) for p in rows] + ring_peers("col")
+
+    @pl.when(q != c)
+    def _():
+        for i in range(2):
+            pl.semaphore_signal(barrier, inc=1, device_id=target(i), device_id_type=MESH)
+
+    for device in peers:
+        pl.semaphore_signal(barrier, inc=1, device_id=device, device_id_type=MESH)
+    pl.semaphore_wait(barrier, len(peers) + 2 * (q != c).astype(jnp.int32))
+
+    move_state = Copy(state, final, send_sem, recv_sem, n_ring, target(0))
+
+    @pl.when(q == c)
+    def _():
+        keep(state, final, recv_sem.at[n_ring])
+
+    @pl.when(q != c)
+    def _():
+        move_state.start()
+
     for copy in copies:
         copy.wait()
 
-    def moves(m):
-        tokens = pl.ds(pl.multiple_of(m * STEP, STEP), STEP)
+    def sums(m):
+        def copy_of(i, p):
+            return Copy(
+                lambda: part.at[p, aligned(m, LMAX)],
+                lambda: got.at[r, aligned(m, LMAX)],
+                send_sem,
+                recv_sem,
+                m * (N_ROW - 1) + i,
+                (p, c),
+            )
+
+        return [copy_of(i, p) for i, p in enumerate(rows)]
+
+    def source_rows(m, i):
+        return pl.ds(pl.multiple_of(lax.rem(h + i, 2) * MINE + m * LMAX, LMAX), LMAX)
+
+    def turn(m, i):
+        return pltpu.make_async_remote_copy(
+            src_ref=out.at[source_rows(m, i)],
+            dst_ref=nx.at[2 * q + h, aligned(m, LMAX)],
+            send_sem=send_sem.at[n_sum + 2 * m + i],
+            recv_sem=recv_sem.at[n_sum + 2 * m + h],
+            device_id=target(i),
+            device_id_type=MESH,
+        )
+
+    def hop(m, slot, chip, side, half=None):
+        def block():
+            at = chips.get(chip, c)
+            if half is None:
+                return nx.at[pl.ds(2 * at, 2), aligned(m, LMAX)]
+            return nx.at[2 * at + half, aligned(m, LMAX)]
+
+        return Copy(block, block, send_sem, recv_sem, n_turn + m * HOPS + slot, to[side])
+
+    def hops(m):
         return [
-            pltpu.make_async_remote_copy(
-                src_ref=part.at[p, tokens],
-                dst_ref=got.at[r, tokens],
-                send_sem=send_sem.at[m * (N_ROW - 1) + i],
-                recv_sem=recv_sem.at[m * (N_ROW - 1) + i],
-                device_id=(p, c),
-                device_id_type=MESH,
-            )
-            for i, p in enumerate(rows)
+            hop(m, 0, "own", "p"),
+            hop(m, 1, "own", "m"),
+            hop(m, 2, "own", "z"),
+            hop(m, 3, "m", "p", 0),
+            hop(m, 4, "p", "m", 1),
+            hop(m, 5, "z", "p"),
+            hop(m, 6, "z", "m"),
+            hop(m, 7, "o", "z", 0),
+            hop(m, 8, "o", "z", 1),
         ]
 
-    @pl.loop(0, MINE // STEP)
-    def _(m):
-        tokens = pl.ds(pl.multiple_of(m * STEP, STEP), STEP)
-        z = norm(
-            jnp.concatenate([midg[j, tokens, :].astype(F32) for j in range(N_ROW)], axis=1),
-            row_of(par, 2),
-            row_of(par, 3),
+    def normed(ref, m, k):
+        tokens = aligned(m, LMAX)
+        return norm(
+            jnp.concatenate([ref[j, tokens, :].astype(F32) for j in range(N_ROW)], axis=1),
+            row_of(par, k),
+            row_of(par, k + 1),
         )
+
+    def channel(m):
+        tokens = aligned(m, LMAX)
+        z = normed(midg, m, 2)
         blend = (z + step_back(z) * shift[5:6, :]).astype(BF16)
         for side, weights in enumerate((held, theirs)):
             act = jnp.square(jnp.maximum(dot(blend, weights[0].reshape(WIDTH, MINE)), 0.0))
@@ -849,8 +872,8 @@
         def _(n):
             total = None
             for side, weights in enumerate((held, theirs)):
-                weight = weights[1, pl.ds(2 * n, 2)].reshape(SLICE, MINE)
-                term = dot(act_scr[side], weight, ((1,), (1,)))
+                rows_n = weights[1, pl.ds(2 * n, 2)].reshape(SLICE, MINE)
+                term = dot(act_scr[side], rows_n, ((1,), (1,)))
                 total = term if total is None else total + term
             for side in range(2):
                 added = jnp.where(n == q, own[side, tokens, :].astype(F32), 0.0)
@@ -858,33 +881,101 @@
                     total[:, side * FEAT : (side + 1) * FEAT] + added
                 ).astype(BF16)
 
-        for copy in moves(m):
+        for copy in sums(m):
             copy.start()
         got[r, tokens, :] = part[r, tokens, :]
 
-    @pl.loop(0, MINE // STEP)
-    def _(m):
-        for copy in moves(m):
-            copy.wait()
-
-    for side in range(2):
-        total = got[side].astype(F32)
-        for k in range(1, N_CHIP):
-            total += got[2 * k + side].astype(F32)
-        out[pl.ds(side * MINE, MINE), :] = total.astype(BF16)
-
-
-def last_kernel(nx, par, shift, weight, out):
-    @pl.loop(0, MINE // TILE)
-    def _(m):
-        at = pl.multiple_of(m * TILE, TILE)
-        z = norm(blocks_of(nx, at), row_of(par, 4), row_of(par, 5))
+    def add_up(m):
+        for copy in sums(m):
+            copy.wait_recv()
+        tokens = aligned(m, LMAX)
+        for side in range(2):
+            total = got[side, tokens, :].astype(F32)
+            for k in range(1, N_CHIP):
+                total += got[2 * k + side, tokens, :].astype(F32)
+            rows_m = pl.ds(pl.multiple_of(side * MINE + m * LMAX, LMAX), LMAX)
+            out[rows_m, :] = total.astype(BF16)
+
+        @pl.when(q == c)
+        def _():
+            keep(
+                out.at[source_rows(m, 0)],
+                nx.at[r, aligned(m, LMAX)],
+                recv_sem.at[n_sum + 2 * m + h],
+            )
+
+        @pl.when(q != c)
+        def _():
+            turn(m, 0).start()
+
+        turn(m, 1).start()
+
+    def spread(m):
+        for k in range(2):
+            block = nx.at[2 * c + k, aligned(m, LMAX)]
+            pltpu.make_async_copy(block, block, recv_sem.at[n_sum + 2 * m + k]).wait()
+        for k in (2, 0, 1):
+            hops(m)[k].start()
+
+    def forward(m):
+        ring_m = hops(m)
+        ring_m[0].wait_recv()
+        ring_m[3].start()
+        ring_m[1].wait_recv()
+        ring_m[4].start()
+        ring_m[2].wait_recv()
+        ring_m[5].start()
+        ring_m[6].start()
+
+    def close(m):
+        ring_m = hops(m)
+        ring_m[3].wait_recv()
+        ring_m[7].start()
+        ring_m[4].wait_recv()
+        ring_m[8].start()
+
+    def project(m):
+        ring_m = hops(m)
+        for k in (5, 6, 7, 8):
+            ring_m[k].wait_recv()
+        z = normed(nx, m, 4)
         dz = step_back(z)
         for j in range(3):
             blend = (z + dz * shift[6 + j : 7 + j, :]).astype(BF16)
-            out[j, pl.ds(at, TILE), :] = dot(
+            rkv[j, aligned(m, LMAX), :] = dot(
                 blend, weight[:, :, j].reshape(WIDTH, SLICE)
             ).astype(BF16)
+
+    stages = (channel, add_up, spread, forward, close, project)
+
+    @pl.loop(0, PROMPTS + len(stages) - 1)
+    def _(step):
+        @pl.when(step == len(stages) - 1)
+        def _():
+            load.wait()
+
+        for lag, stage in enumerate(stages):
+
+            @pl.when((step >= lag) & (step < PROMPTS + lag))
+            def _():
+                stage(step - lag)
+
+    @pl.loop(0, PROMPTS)
+    def _(m):
+        for copy in sums(m) + hops(m):
+            copy.wait_send()
+
+        @pl.when(q != c)
+        def _():
+            turn(m, 0).wait_send()
+
+        turn(m, 1).wait_send()
+
+    pltpu.make_async_copy(state, final, recv_sem.at[n_ring]).wait()
+
+    @pl.when(q != c)
+    def _():
+        move_state.wait_send()
 
 
 def per_device(
@@ -929,15 +1020,16 @@
         (hx, parg, token_shift_weights, wt, lowrank_down.transpose(0, 2, 1)),
         flops=4 * 10**9,
     )
-    mid, final, wkg = exchange(
+    mid, state, wkg, wng = exchange(
         attend_kernel,
         [
             ((2, MINE, FEAT), BF16),
             ((PROMPTS, 2, HEAD, FEAT), BF16),
             ((N_COL, N_ROW, 16, MINE), BF16),
+            ((N_ROW, N_COL, 3, 16, SLICE), BF16),
         ],
-        PROMPTS * HOPS + 1 + RING,
-        1,
+        PROMPTS * HOPS + 2 + 14 + 2 * RING,
+        2,
         2,
         lengths,
         rkv,
@@ -947,20 +1039,15 @@
         hx,
         w3,
         wk,
+        wn,
         scratch=[
             pltpu.VMEM((2, MINE, FEAT), BF16),
             pltpu.VMEM((N_ROW + 2, MINE, FEAT), BF16),
             pltpu.VMEM((N_COL, 16, WIDTH), BF16),
         ],
-        in_specs=[pl.BlockSpec(memory_space=pltpu.SMEM)] + [VMEM] * 4 + [ANY, VMEM, ANY],
-        out_specs=[VMEM, VMEM, ANY],
-    )
-    moves = [
-        ((2 * a + b) * N_COL + d, (2 * d + b) * N_COL + a)
-        for a in range(N_CHIP)
-        for b in range(2)
-        for d in range(N_COL)
-    ]
+        in_specs=[pl.BlockSpec(memory_space=pltpu.SMEM)] + [VMEM] * 4 + [ANY, VMEM, ANY, ANY],
+        out_specs=[VMEM, VMEM, ANY, ANY],
+    )
     midg, wvg, theirs = exchange(
         mid_kernel,
         [
@@ -976,15 +1063,15 @@
         wkg,
         wv,
     )
-    final, midg = lax.optimization_barrier((final, midg))
-    final = lax.ppermute(final, ("row", "col"), moves)
-    final = final.reshape(4, 2, HEAD, 2, HEAD).transpose(0, 1, 3, 2, 4).astype(F32)
-    final_state = final.reshape(4, 4, HEAD * HEAD)
-    (out_hidden,) = exchange(
-        mlp_kernel,
-        [((2 * MINE, FEAT), BF16)],
-        15 * MINE // STEP,
-        16,
+    out_hidden, next_rkv, final = exchange(
+        tail_kernel,
+        [
+            ((2 * MINE, FEAT), BF16),
+            ((3, MINE, SLICE), BF16),
+            ((PROMPTS, 2, HEAD, FEAT), BF16),
+        ],
+        PROMPTS * (N_ROW - 1) + 2 * PROMPTS + PROMPTS * HOPS + 1,
+        17,
         4,
         midg,
         parg,
@@ -995,30 +1082,21 @@
         wvg,
         theirs,
         mid,
+        wng,
+        state,
         scratch=[
             pltpu.VMEM((2, N_ROW, N_COL, 16, MINE), BF16),
-            pltpu.VMEM((2, STEP, MINE), BF16),
+            pltpu.VMEM((2, LMAX, MINE), BF16),
             pltpu.VMEM((N_ROW, MINE, FEAT), BF16),
             pltpu.VMEM((N_ROW, MINE, FEAT), BF16),
+            pltpu.VMEM((N_ROW, MINE, FEAT), BF16),
+            pltpu.VMEM((N_ROW, N_COL, 3, 16, SLICE), BF16),
         ],
-        in_specs=[VMEM] * 3 + [ANY] * 4 + [VMEM] * 2,
-        out_specs=[VMEM],
-    )
-    nx, weight_next = exchange(
-        next_kernel,
-        [((N_ROW, MINE, FEAT), BF16), ((N_ROW, N_COL, 3, 16, SLICE), BF16)],
-        2 + 1 + 14 + 2 * RING,
-        1,
-        5,
-        out_hidden,
-        wn,
-    )
-    (next_rkv,) = compute(
-        last_kernel,
-        [((3, MINE, SLICE), BF16)],
-        (nx, parg, token_shift_weights, weight_next),
-        flops=2 * 10**9,
-    )
+        in_specs=[VMEM] * 3 + [ANY] * 4 + [VMEM] * 2 + [ANY] * 2,
+        out_specs=[VMEM, VMEM, ANY],
+    )
+    final = final.reshape(4, 2, HEAD, 2, HEAD).transpose(0, 1, 3, 2, 4).astype(F32)
+    final_state = final.reshape(4, 4, HEAD * HEAD)
     return (out_hidden, next_rkv, final_state)
 
 

time: 217 us -> 196 us (0.903)
  Pallas kernels: 214 us -> 190 us
    pallas_call x5 -> x4, Pallas kernels: 198 us -> 182 us  [exchange(): pl.pallas_call(kernel, out_shape=[jax.ShapeDtypeStruct(*out) for out in o...]
    pallas_call x2 -> x1, Pallas kernels: 15.4 us -> 8.26 us  [compute(): pl.pallas_call(kernel, grid=grid if grid is not None else (), out_shape=[...]
  transfers between devices with their start and end apart: 1 -> 0, of which waited for: 0 -> 0; matrix products, arithmetic and copies ran while one was open for 0% -> 0% of each run, Pallas kernels for 42% -> 0%
where the time goes in v6:
time: 196 us; the launch traced here: 195 us
  Pallas kernels  190 us (97%)
  local copies, waits for them, and re-layouts  3.87 us (2%)
    pallas_call x4, Pallas kernels, exchange(): pl.pallas_call(kernel, out_shape=[jax.ShapeDtypeStruct(*out) for out in o...  182 us
    pallas_call x1, Pallas kernels, compute(): pl.pallas_call(kernel, grid=grid if grid is not None else (), out_shape=[...  8.26 us

profile of v6, /device:TPU:1, one launch (start us, length us, event | category | flops | bytes accessed | tf_op | source)
XLA Modules:
  0.0 195.0 jit_solution(5722552581556962194)
XLA Ops:
  0.6 41.0 %shard_map.112 = (bf16[16,512,128]{2,1,0:T(8,128)(2,1)}, bf16[2,3,16,8,16,128]{5,4,3,2,1,0:T(8,128)(2,1)}, bf16[8,16,2048]{2,1,0:T(8,128)(2,1)}, bf16[8,16,16,51...) custom-call(f32[7,16,2048]{2,1,0:T(8,128)} %square_in.1, ...), custom_call_target="tpu_custom_call" | custom-call | bytes 50331648 | tf_op jit(solution)/shard_map/pallas_call | solution.py:71
  41.7 8.3 %shard_map.113 = (f32[3,512,256]{2,1,0:T(8,128)}, f32[2,512,96]{2,1,0:T(8,128)}) custom-call(bf16[16,512,128]{2,1,0:T(8,128)(2,1)} %get-tuple-element.22.hx.own, f32[16,6,128]{2,1,0:T(8,128)} %get-tuple-element.23.par, f32[9,2048]{1,0:T(8,128)} %shift.3, bf16[2,3,16,8,16,128]{5,4,3,2,1,0:T(8,128)(2,1)} %get-tuple-element.24.wt, bf16[2,96,2048]{2,1,0:T(8,128)(2,1)} %bitcast.7), custom_call_target="tpu_custom_call" | custom-call | flops 4000000000 | bytes 16777216 | tf_op jit(solution)/shard_map/pallas_call | solution.py:397
  49.9 48.0 %shard_map.114 = (bf16[2,512,128]{2,1,0:T(8,128)(2,1)}, bf16[4,2,64,128]{3,2,1,0:T(8,128)(2,1)}, bf16[8,16,16,512]{3,2,1,0:T(8,128)(2,1)}, bf16[16,8,3,16,256]{4,3,2,1,0:T(8,128)(2,1)}) custom-call(s32[64]{0:T(128)} %lens.1, f32[3,512,256]{2,1,0:T(8,128)} %get-tuple-element.25.rkv, f32[2,512,96]{2,1,0:T(8,128)} %get-tuple-element.26.low, f32[6,2048]{1,0:T(8,128)} %coef.1, ...), custom_call_target="tpu_custom_call" | custom-call | bytes 50331648 | tf_op jit(solution)/shard_map/pallas_call | solution.py:71
  97.9 27.8 %shard_map.115 = (bf16[16,512,128]{2,1,0:T(8,128)(2,1)}, bf16[8,16,16,512]{3,2,1,0:T(8,128)(2,1)}, bf16[2,16,8,16,512]{4,3,2,1,0:T(8,128)(2,1)}) custom-call(bf16[2,512,128]{2,1,0:T(8,128)(2,1)} %get-tuple-element.30.mid.own, bf16[8,16,16,512]{3,2,1,0:T(8,128)(2,1)} %get-tuple-element.28.wk, bf16[8,16,16,512]{3,2,1,0:T(8,128)(2,1)} %get-tuple-element.31.wkg, ...), custom_call_target="tpu_custom_call" | custom-call | bytes 50331648 | tf_op jit(solution)/shard_map/pallas_call | solution.py:71
  125.7 65.4 %shard_map.116 = (bf16[1024,128]{1,0:T(8,128)(2,1)}, bf16[3,512,256]{2,1,0:T(8,128)(2,1)}, bf16[4,2,64,128]{3,2,1,0:T(8,128)(2,1)}) custom-call(bf16[16,512,128]{2,1,0:T(8,128)(2,1)} %get-tuple-element.33.midg, f32[16,6,128]{2,1,0:T(8,128)} %get-tuple-element.23.par, f32[9,2048]{1,0:T(8,128)} %shift.3, bf16[8,16,16,512]{3,2,1,0:T(8,128)(2,1)} %get-tuple-element.28.wk, ...), custom_call_target="tpu_custom_call" | custom-call | bytes 50331648 | tf_op jit(solution)/shard_map/pallas_call | solution.py:71
  191.1 0.0 copy-start.1
  191.1 0.0 copy-start
  191.1 1.3 reshape.21
  192.5 0.9 reshape.18
  193.4 0.0 copy-done.1
  193.4 0.7 copy.15
  194.1 0.0 copy-done
  194.1 0.9 copy.16
  (1 shorter events, 0.0 us)
Async XLA Ops:
  191.1 2.3 %copy-start.1 = (bf16[1024,128]{1,0:T(8,128)(2,1)S(1)}, bf16[1024,128]{1,0:T(8,128)(2,1)}, u32[]{:S(2)}) copy-start(bf16[1024,128]{1,0:T(8,128)(2,1)} %get-tuple-element.44) | copy-start | bytes 786436
  191.1 3.0 %copy-start = (bf16[3,512,256]{2,1,0:T(8,128)(2,1)S(1)}, bf16[3,512,256]{2,1,0:T(8,128)(2,1)}, u32[]{:S(2)}) copy-start(bf16[3,512,256]{2,1,0:T(8,128)(2,1)} %get-tuple-element.45) | copy-start | bytes 2359300

commit v7 on v6

--- a/solution.py
+++ b/solution.py
@@ -146,8 +146,8 @@
     return list(ring_at(axis)[2].values())
 
 
-def ring(links, axis, slot, own=None, which=(0, 1), ready=None, seen=None, heavy=None):
-    here, chips, to = ring_at(axis)
+def ring(links, axis, slot, own=None, which=(0, 1), ready=None, seen=None, heavy=None, at=None):
+    here, chips, to = at or ring_at(axis)
     heavy = axis == "row" if heavy is None else heavy
     seen = seen or (lambda chip, half: None)
 
@@ -345,67 +345,6 @@
         copy.wait()
 
 
-def row_ring(links, source, target):
-    return ring(
-        links, "row", lambda chip, side: target.at[2 * chip + side], own=lambda k: source.at[k]
-    )
-
-
-def own_block(source, target, q, local_sem):
-    return [keep(source.at[k], target.at[2 * q + k], local_sem.at[k]) for k in range(2)]
-
-
-def mid_kernel(mid, wk, wkg, wv, midg, wvg, theirs, send_sem, recv_sem, local_sem):
-    r, c, h, q, sibling = place()
-    local = own_block(mid, midg, q, local_sem)
-    greet([(sibling, c)] + ring_peers("row") + ring_peers("col"))
-    links = Links(send_sem, recv_sem)
-
-    def value_slot(chip, half):
-        return wvg.at[chip, pl.ds(8 * half, 8)]
-
-    def value_seen(chip, half):
-        links.go(
-            value_slot(chip, half), theirs.at[1, pl.ds(8 * half, 8), chip], (sibling, c)
-        )
-
-    def across():
-        links.go(wk.at[c], theirs.at[0, :, c], (sibling, c))
-        links.go(wv.at[c], theirs.at[1, :, c], (sibling, c))
-        for d in range(1, N_COL):
-            p = lax.rem(c + d, N_COL)
-            links.go(wkg.at[p], theirs.at[0, :, p], (sibling, c))
-        yield
-
-    together(
-        row_ring(links, mid, midg),
-        ring(
-            links,
-            "col",
-            value_slot,
-            own=lambda k: wv.at[c, pl.ds(8 * k, 8)],
-            seen=value_seen,
-        ),
-        across(),
-    )
-    links.finish()
-    for copy in local:
-        copy.wait()
-
-
-def compute(kernel, outs, operands, scratch=(), grid=None, in_specs=None, out_specs=None, flops=0):
-    return pl.pallas_call(
-        kernel,
-        grid=grid if grid is not None else (),
-        out_shape=[jax.ShapeDtypeStruct(*out) for out in outs],
-        in_specs=in_specs if in_specs is not None else [VMEM] * len(operands),
-        out_specs=out_specs if out_specs is not None else [VMEM] * len(outs),
-        scratch_shapes=list(scratch),
-        compiler_params=pltpu.CompilerParams(vmem_limit_bytes=56 * 2**20),
-        cost_estimate=pl.CostEstimate(flops=flops, bytes_accessed=16 * 2**20, transcendentals=0),
-    )(*operands)
-
-
 def dot(a, b, dims=((1,), (0,))):
     return lax.dot_general(a, b, (dims, ((), ())), preferred_element_type=F32)
 
@@ -435,32 +374,6 @@
 def step_back(z):
     position = lax.rem(lax.broadcasted_iota(jnp.int32, z.shape, 0), LMAX)
     return jnp.where(position == 0, 0.0, pltpu.roll(z, 1, 0)) - z
-
-
-TILE = 256
-
-
-def blocks_of(ref, at):
-    return jnp.concatenate(
-        [ref[j, pl.ds(at, TILE), :].astype(F32) for j in range(ref.shape[0])], axis=1
-    )
-
-
-def mix_kernel(hx, par, shift, wt, down, rkv, low):
-    @pl.loop(0, MINE // TILE)
-    def _(m):
-        at = pl.multiple_of(m * TILE, TILE)
-        z = norm(blocks_of(hx, at), row_of(par, 0), row_of(par, 1))
-        dz = step_back(z)
-        for j in range(5):
-            blend = (z + dz * shift[j : j + 1, :]).astype(BF16)
-            if j < 3:
-                weight = jnp.concatenate(
-                    [wt[side, j].reshape(WIDTH, FEAT) for side in range(2)], axis=1
-                )
-                rkv[j, pl.ds(at, TILE), :] = dot(blend, weight)
-            else:
-                low[j - 3, pl.ds(at, TILE), :] = dot(blend, down[j - 3], ((1,), (1,)))
 
 
 def one_prompt(prompt, lens, rkv, low, coef, up, att, final):
@@ -487,13 +400,13 @@
     def only(x, k):
         return jnp.where(lane == k, x, jnp.zeros_like(x))
 
-    receptance, key, value = rkv[0, tokens], rkv[1, tokens], rkv[2, tokens]
+    receptance, key, value = rkv[0], rkv[1], rkv[2]
     decay = (
         -0.606531
-        * jax.nn.sigmoid(coef[0:1, channels] + dot(jnp.tanh(low[0, tokens]).astype(BF16), up[0, :, channels]))
+        * jax.nn.sigmoid(coef[0:1, channels] + dot(jnp.tanh(low[0]).astype(BF16), up[0, :, channels]))
         * live
     )
-    rate = jax.nn.sigmoid(coef[1:2, channels] + dot(low[1, tokens].astype(BF16), up[1, :, channels]))
+    rate = jax.nn.sigmoid(coef[1:2, channels] + dot(low[1].astype(BF16), up[1, :, channels]))
     kappa = key * coef[2:3, channels]
     kappa = kappa * lax.rsqrt(head_sum(kappa * kappa) + 1e-05)
     remove = -kappa * live
@@ -586,195 +499,134 @@
 HOPS = 9
 
 
-def attend_kernel(
+class PromptRing:
+    def __init__(self, send_sem, recv_sem, base, axis, own, got):
+        self.send_sem = send_sem
+        self.recv_sem = recv_sem
+        self.base = base
+        self.here, self.chips, self.to = ring_at(axis)
+        self.own = own
+        self.got = got
+
+    def hop(self, m, slot, chip, side, half=None):
+        def block():
+            at = self.chips.get(chip, self.here)
+            if half is None:
+                return self.got.at[pl.ds(2 * at, 2), aligned(m, LMAX)]
+            return self.got.at[2 * at + half, aligned(m, LMAX)]
+
+        def source():
+            if chip == "own" and self.own is not None:
+                return self.own.at[:, aligned(m, LMAX)]
+            return block()
+
+        return Copy(
+            source,
+            block,
+            self.send_sem,
+            self.recv_sem,
+            self.base + m * HOPS + slot,
+            self.to[side],
+        )
+
+    def hops(self, m):
+        return [
+            self.hop(m, 0, "own", "p"),
+            self.hop(m, 1, "own", "m"),
+            self.hop(m, 2, "own", "z"),
+            self.hop(m, 3, "m", "p", 0),
+            self.hop(m, 4, "p", "m", 1),
+            self.hop(m, 5, "z", "p"),
+            self.hop(m, 6, "z", "m"),
+            self.hop(m, 7, "o", "z", 0),
+            self.hop(m, 8, "o", "z", 1),
+        ]
+
+    def begin(self, m):
+        copies = self.hops(m)
+        for k in (2, 0, 1):
+            copies[k].start()
+
+    def forward(self, m):
+        copies = self.hops(m)
+        copies[0].wait_recv()
+        copies[3].start()
+        copies[1].wait_recv()
+        copies[4].start()
+        copies[2].wait_recv()
+        copies[5].start()
+        copies[6].start()
+
+    def close(self, m):
+        copies = self.hops(m)
+        copies[3].wait_recv()
+        copies[7].start()
+        copies[4].wait_recv()
+        copies[8].start()
+
+    def last(self, m):
+        for k in (5, 6, 7, 8):
+            self.hops(m)[k].wait_recv()
+
+    def sent(self, m):
+        for copy in self.hops(m):
+            copy.wait_send()
+
+
+N_SUM = PROMPTS * (N_ROW - 1)
+N_TURN = N_SUM + 2 * PROMPTS
+N_STATE = N_TURN + 1
+N_WEIGHT = N_STATE + 3 * PROMPTS * HOPS
+N_ALL = N_WEIGHT + 1 + 2 * (1 + 14 + RING) + 1 + 14 + RING
+
+
+def body_kernel(
     lens,
-    rkv,
-    low,
+    hx,
+    par,
+    shift,
+    wt,
+    down,
     coef,
     up,
-    own,
     w3,
     wk,
+    wv,
     wn,
-    mid,
-    final,
-    wkg,
-    wng,
-    send_sem,
-    recv_sem,
-    local_sem,
-    att,
-    attg,
-    w3x,
-):
-    r, c, h, q, sibling = place()
-    _, chips, to = ring_at("row")
-    greet([(sibling, c)] + ring_peers("row") + ring_peers("col"))
-    links = Links(send_sem, recv_sem, PROMPTS * HOPS)
-    links.go(w3, w3x, (sibling, c))
-    near = keep(own.at[pl.ds(pl.multiple_of(r - h, 2), 2)], attg.at[pl.ds(N_ROW, 2)], local_sem.at[0])
-    keys = ring(
-        links,
-        "col",
-        lambda chip, half: wkg.at[chip, pl.ds(8 * half, 8)],
-        own=lambda k: wk.at[c, pl.ds(8 * k, 8)],
-    )
-    far = keep(wn.at[r], wng.at[r], local_sem.at[1])
-    links.go(wn.at[r], wng.at[r], (sibling, c))
-
-    def weight_slot(chip, half):
-        return wng.at[2 * chip + h, pl.ds(4 * half, 4)]
-
-    def weight_seen(chip, half):
-        links.go(
-            lambda: weight_slot(chip, half), lambda: weight_slot(chip, half), (sibling, c)
-        )
-
-    weights = ring(
-        links,
-        "row",
-        weight_slot,
-        own=lambda k: wn.at[r, pl.ds(4 * k, 4)],
-        seen=weight_seen,
-    )
-
-    def advance():
-        for steps in (keys, weights):
-            next(steps)
-
-    advance()
-
-    def hop(prompt, slot, chip, side, half=None):
-        def block():
-            tokens = aligned(prompt, LMAX)
-            if half is None:
-                return attg.at[pl.ds(2 * chips.get(chip, q), 2), tokens]
-            return attg.at[2 * chips[chip] + half, tokens]
-
-        def source():
-            return att.at[:, aligned(prompt, LMAX)] if chip == "own" else block()
-
-        return Copy(source, block, send_sem, recv_sem, prompt * HOPS + slot, to[side])
-
-    def hops(prompt):
-        return [
-            hop(prompt, 0, "own", "p"),
-            hop(prompt, 1, "own", "m"),
-            hop(prompt, 2, "own", "z"),
-            hop(prompt, 3, "m", "p", 0),
-            hop(prompt, 4, "p", "m", 1),
-            hop(prompt, 5, "z", "p"),
-            hop(prompt, 6, "z", "m"),
-            hop(prompt, 7, "o", "z", 0),
-            hop(prompt, 8, "o", "z", 1),
-        ]
-
-    @pl.loop(0, PROMPTS + 2)
-    def _(step):
-        @pl.when(step < PROMPTS)
-        def _():
-            one_prompt(step, lens, rkv, low, coef, up, att, final)
-            copies = hops(step)
-            for k in range(3):
-                copies[k].start()
-            tokens = aligned(step, LMAX)
-            for side in range(2):
-                attg[2 * q + side, tokens] = att[side, tokens]
-
-        @pl.when((step >= 1) & (step <= PROMPTS))
-        def _():
-            copies = hops(step - 1)
-            copies[0].wait_recv()
-            copies[3].start()
-            copies[1].wait_recv()
-            copies[4].start()
-            copies[2].wait_recv()
-            copies[5].start()
-            copies[6].start()
-
-        @pl.when(step >= 2)
-        def _():
-            copies = hops(step - 2)
-            copies[3].wait_recv()
-            copies[7].start()
-            copies[4].wait_recv()
-            copies[8].start()
-
-        @pl.when(step == 1)
-        def _():
-            advance()
-
-        @pl.when(step == 2)
-        def _():
-            advance()
-
-        @pl.when(step == 3)
-        def _():
-            advance()
-
-    @pl.loop(0, PROMPTS)
-    def _(prompt):
-        copies = hops(prompt)
-        for k in (5, 6, 7, 8):
-            copies[k].wait_recv()
-        for copy in copies:
-            copy.wait_send()
-
-    together(keys, weights)
-    links.finish()
-    near.wait()
-    far.wait()
-
-    @pl.loop(0, MINE // TILE)
-    def _(m):
-        rows = aligned(m, TILE)
-        wide = jnp.concatenate([attg[j, rows, :] for j in range(N_ROW)], axis=1)
-        weight = jnp.concatenate([w[...].reshape(FEAT, WIDTH) for w in (w3, w3x)])
-        total = dot(wide, weight, ((1,), (1,)))
-        for k, side in enumerate((h, 1 - h)):
-            mid[side, rows, :] = (
-                attg[N_ROW + side, rows, :].astype(F32) + total[:, k * FEAT : (k + 1) * FEAT]
-            ).astype(BF16)
-
-
-def tail_kernel(
-    midg,
-    par,
-    shift,
-    wk,
-    wkg,
-    wv,
-    wvg,
-    theirs,
-    own,
-    wng,
-    state,
     out,
-    rkv,
+    next_rkv,
     final,
     send_sem,
     recv_sem,
     local_sem,
+    rkv,
+    low,
+    state,
+    att,
+    attg,
+    w3x,
+    mid,
+    midg,
     held,
+    theirs,
     act_scr,
     part,
     got,
     nx,
-    weight,
+    wng,
 ):
     r, c, h, q, sibling = place()
-    _, chips, to = ring_at("col")
-    copies = []
-    for m, (near, far) in enumerate(((wk, wkg), (wv, wvg))):
-        copies.append(keep(near.at[c], held.at[m, :, c], local_sem.at[8 * m]))
-        for d in range(1, N_COL):
-            p = lax.rem(c + d, N_COL)
-            copies.append(keep(far.at[p], held.at[m, :, p], local_sem.at[8 * m + d]))
-    load = keep(wng, weight, local_sem.at[16])
     rows = [lax.rem(r + d, N_ROW) for d in range(1, N_ROW)]
-    n_sum = PROMPTS * (N_ROW - 1)
-    n_turn = n_sum + 2 * PROMPTS
-    n_ring = n_turn + PROMPTS * HOPS
+
+    def local():
+        return [
+            pltpu.make_async_copy(wk.at[c], held.at[0, :, c], local_sem.at[0]),
+            pltpu.make_async_copy(wv.at[c], held.at[1, :, c], local_sem.at[1]),
+            pltpu.make_async_copy(wn.at[r], wng.at[r], local_sem.at[2]),
+        ]
+
+    for copy in local():
+        copy.start()
 
     def target(i):
         return (2 * c + lax.rem(h + i, 2), q)
@@ -791,18 +643,102 @@
         pl.semaphore_signal(barrier, inc=1, device_id=device, device_id_type=MESH)
     pl.semaphore_wait(barrier, len(peers) + 2 * (q != c).astype(jnp.int32))
 
-    move_state = Copy(state, final, send_sem, recv_sem, n_ring, target(0))
-
-    @pl.when(q == c)
-    def _():
-        keep(state, final, recv_sem.at[n_ring])
-
-    @pl.when(q != c)
-    def _():
-        move_state.start()
-
-    for copy in copies:
-        copy.wait()
+    links = Links(send_sem, recv_sem, N_WEIGHT)
+    links.go(w3, w3x, (sibling, c))
+
+    col_place = ring_at("col")
+
+    def mlp_ring(which, source):
+        def slot(chip, half):
+            return held.at[which, pl.ds(8 * half, 8), chip]
+
+        def over(chip, half):
+            return theirs.at[which, pl.ds(8 * half, 8), chip]
+
+        def seen(chip, half):
+            links.go(lambda: slot(chip, half), lambda: over(chip, half), (sibling, c))
+
+        def begin():
+            links.go(lambda: source.at[c], lambda: theirs.at[which, :, c], (sibling, c))
+            yield from ring(
+                links,
+                "col",
+                slot,
+                own=lambda k: source.at[c, pl.ds(8 * k, 8)],
+                seen=seen,
+                at=col_place,
+            )
+
+        return begin()
+
+    def weight_slot(chip, half):
+        return wng.at[2 * chip + h, pl.ds(4 * half, 4)]
+
+    far_links = Links(send_sem, recv_sem, N_ALL - 1 - 14 - RING)
+
+    def weight_seen(chip, half):
+        far_links.go(
+            lambda: weight_slot(chip, half), lambda: weight_slot(chip, half), (sibling, c)
+        )
+
+    def weight_ring():
+        far_links.go(lambda: wn.at[r], lambda: wng.at[r], (sibling, c))
+        yield from ring(
+            far_links,
+            "row",
+            weight_slot,
+            own=lambda k: wn.at[r, pl.ds(4 * k, 4)],
+            seen=weight_seen,
+        )
+
+    keys = mlp_ring(0, wk)
+    values = mlp_ring(1, wv)
+    weights = weight_ring()
+    next(weights)
+    next(keys)
+
+    att_ring = PromptRing(send_sem, recv_sem, N_STATE, "row", att, attg)
+    mid_ring = PromptRing(send_sem, recv_sem, N_STATE + PROMPTS * HOPS, "row", mid, midg)
+    out_ring = PromptRing(send_sem, recv_sem, N_STATE + 2 * PROMPTS * HOPS, "col", None, nx)
+    move_state = Copy(state, final, send_sem, recv_sem, N_TURN, target(0))
+
+    def wide(ref, m):
+        return jnp.concatenate([ref[j, aligned(m, LMAX), :] for j in range(N_ROW)], axis=1)
+
+    def normed(ref, m, k):
+        return norm(wide(ref, m).astype(F32), row_of(par, k), row_of(par, k + 1))
+
+    def blends(m):
+        z = normed(hx, m, 0)
+        dz = step_back(z)
+        for j in range(5):
+            blend = (z + dz * shift[j : j + 1, :]).astype(BF16)
+            if j < 3:
+                weight = jnp.concatenate(
+                    [wt[side, j].reshape(WIDTH, FEAT) for side in range(2)], axis=1
+                )
+                rkv[j] = dot(blend, weight)
+            else:
+                low[j - 3] = dot(blend, down[j - 3], ((1,), (1,)))
+
+    def core(m):
+        one_prompt(m, lens, rkv, low, coef, up, att, state)
+        att_ring.begin(m)
+        for side in range(2):
+            attg[2 * q + side, aligned(m, LMAX)] = att[side, aligned(m, LMAX)]
+
+    def project(m):
+        att_ring.last(m)
+        tokens = aligned(m, LMAX)
+        weight = jnp.concatenate([w[...].reshape(FEAT, WIDTH) for w in (w3, w3x)])
+        total = dot(wide(attg, m), weight, ((1,), (1,)))
+        for k, side in enumerate((h, 1 - h)):
+            block = (
+                hx[r - h + side, tokens, :].astype(F32) + total[:, k * FEAT : (k + 1) * FEAT]
+            ).astype(BF16)
+            mid[side, tokens, :] = block
+            midg[r - h + side, tokens, :] = block
+        mid_ring.begin(m)
 
     def sums(m):
         def copy_of(i, p):
@@ -817,6 +753,32 @@
 
         return [copy_of(i, p) for i, p in enumerate(rows)]
 
+    def channel(m):
+        mid_ring.last(m)
+        tokens = aligned(m, LMAX)
+        z = normed(midg, m, 2)
+        blend = (z + step_back(z) * shift[5:6, :]).astype(BF16)
+        for side, weight in enumerate((held, theirs)):
+            act = jnp.square(jnp.maximum(dot(blend, weight[0].reshape(WIDTH, MINE)), 0.0))
+            act_scr[side] = act.astype(BF16)
+
+        @pl.loop(0, N_CHIP)
+        def _(n):
+            total = None
+            for side, weight in enumerate((held, theirs)):
+                rows_n = weight[1, pl.ds(2 * n, 2)].reshape(SLICE, MINE)
+                term = dot(act_scr[side], rows_n, ((1,), (1,)))
+                total = term if total is None else total + term
+            for side in range(2):
+                added = jnp.where(n == q, mid[side, tokens, :].astype(F32), 0.0)
+                part[2 * n + side, tokens, :] = (
+                    total[:, side * FEAT : (side + 1) * FEAT] + added
+                ).astype(BF16)
+
+        for copy in sums(m):
+            copy.start()
+        got[r, tokens, :] = part[r, tokens, :]
+
     def source_rows(m, i):
         return pl.ds(pl.multiple_of(lax.rem(h + i, 2) * MINE + m * LMAX, LMAX), LMAX)
 
@@ -824,66 +786,11 @@
         return pltpu.make_async_remote_copy(
             src_ref=out.at[source_rows(m, i)],
             dst_ref=nx.at[2 * q + h, aligned(m, LMAX)],
-            send_sem=send_sem.at[n_sum + 2 * m + i],
-            recv_sem=recv_sem.at[n_sum + 2 * m + h],
+            send_sem=send_sem.at[N_SUM + 2 * m + i],
+            recv_sem=recv_sem.at[N_SUM + 2 * m + h],
             device_id=target(i),
             device_id_type=MESH,
         )
-
-    def hop(m, slot, chip, side, half=None):
-        def block():
-            at = chips.get(chip, c)
-            if half is None:
-                return nx.at[pl.ds(2 * at, 2), aligned(m, LMAX)]
-            return nx.at[2 * at + half, aligned(m, LMAX)]
-
-        return Copy(block, block, send_sem, recv_sem, n_turn + m * HOPS + slot, to[side])
-
-    def hops(m):
-        return [
-            hop(m, 0, "own", "p"),
-            hop(m, 1, "own", "m"),
-            hop(m, 2, "own", "z"),
-            hop(m, 3, "m", "p", 0),
-            hop(m, 4, "p", "m", 1),
-            hop(m, 5, "z", "p"),
-            hop(m, 6, "z", "m"),
-            hop(m, 7, "o", "z", 0),
-            hop(m, 8, "o", "z", 1),
-        ]
-
-    def normed(ref, m, k):
-        tokens = aligned(m, LMAX)
-        return norm(
-            jnp.concatenate([ref[j, tokens, :].astype(F32) for j in range(N_ROW)], axis=1),
-            row_of(par, k),
-            row_of(par, k + 1),
-        )
-
-    def channel(m):
-        tokens = aligned(m, LMAX)
-        z = normed(midg, m, 2)
-        blend = (z + step_back(z) * shift[5:6, :]).astype(BF16)
-        for side, weights in enumerate((held, theirs)):
-            act = jnp.square(jnp.maximum(dot(blend, weights[0].reshape(WIDTH, MINE)), 0.0))
-            act_scr[side] = act.astype(BF16)
-
-        @pl.loop(0, N_CHIP)
-        def _(n):
-            total = None
-            for side, weights in enumerate((held, theirs)):
-                rows_n = weights[1, pl.ds(2 * n, 2)].reshape(SLICE, MINE)
-                term = dot(act_scr[side], rows_n, ((1,), (1,)))
-                total = term if total is None else total + term
-            for side in range(2):
-                added = jnp.where(n == q, own[side, tokens, :].astype(F32), 0.0)
-                part[2 * n + side, tokens, :] = (
-                    total[:, side * FEAT : (side + 1) * FEAT] + added
-                ).astype(BF16)
-
-        for copy in sums(m):
-            copy.start()
-        got[r, tokens, :] = part[r, tokens, :]
 
     def add_up(m):
         for copy in sums(m):
@@ -901,7 +808,7 @@
             keep(
                 out.at[source_rows(m, 0)],
                 nx.at[r, aligned(m, LMAX)],
-                recv_sem.at[n_sum + 2 * m + h],
+                recv_sem.at[N_SUM + 2 * m + h],
             )
 
         @pl.when(q != c)
@@ -913,57 +820,99 @@
     def spread(m):
         for k in range(2):
             block = nx.at[2 * c + k, aligned(m, LMAX)]
-            pltpu.make_async_copy(block, block, recv_sem.at[n_sum + 2 * m + k]).wait()
-        for k in (2, 0, 1):
-            hops(m)[k].start()
-
-    def forward(m):
-        ring_m = hops(m)
-        ring_m[0].wait_recv()
-        ring_m[3].start()
-        ring_m[1].wait_recv()
-        ring_m[4].start()
-        ring_m[2].wait_recv()
-        ring_m[5].start()
-        ring_m[6].start()
-
-    def close(m):
-        ring_m = hops(m)
-        ring_m[3].wait_recv()
-        ring_m[7].start()
-        ring_m[4].wait_recv()
-        ring_m[8].start()
-
-    def project(m):
-        ring_m = hops(m)
-        for k in (5, 6, 7, 8):
-            ring_m[k].wait_recv()
+            pltpu.make_async_copy(block, block, recv_sem.at[N_SUM + 2 * m + k]).wait()
+        out_ring.begin(m)
+
+    def project_next(m):
+        out_ring.last(m)
         z = normed(nx, m, 4)
         dz = step_back(z)
         for j in range(3):
             blend = (z + dz * shift[6 + j : 7 + j, :]).astype(BF16)
-            rkv[j, aligned(m, LMAX), :] = dot(
-                blend, weight[:, :, j].reshape(WIDTH, SLICE)
+            next_rkv[j, aligned(m, LMAX), :] = dot(
+                blend, wng[:, :, j].reshape(WIDTH, SLICE)
             ).astype(BF16)
 
-    stages = (channel, add_up, spread, forward, close, project)
-
-    @pl.loop(0, PROMPTS + len(stages) - 1)
-    def _(step):
-        @pl.when(step == len(stages) - 1)
+    stages = (
+        blends,
+        core,
+        att_ring.forward,
+        att_ring.close,
+        project,
+        mid_ring.forward,
+        mid_ring.close,
+        channel,
+        add_up,
+        spread,
+        out_ring.forward,
+        out_ring.close,
+        project_next,
+    )
+    end = object()
+
+    def wait_mlp():
+        for copy in local():
+            copy.wait()
+        for copy in links.open:
+            copy.wait_recv()
+        links.open = []
+
+    def send_state():
+        @pl.when(q == c)
         def _():
-            load.wait()
-
-        for lag, stage in enumerate(stages):
-
-            @pl.when((step >= lag) & (step < PROMPTS + lag))
+            keep(state, final, recv_sem.at[N_TURN])
+
+        @pl.when(q != c)
+        def _():
+            move_state.start()
+
+    def wait_far():
+        for copy in far_links.open:
+            copy.wait_recv()
+        far_links.open = []
+
+    beside = {
+        1: [weights, keys],
+        2: [keys, values],
+        3: [weights, keys, values, lambda: links.arrive(links.copies[0])],
+        4: [keys, values],
+        5: [weights, values],
+        6: [values],
+        7: [send_state, wait_mlp],
+        8: [weights],
+        12: [wait_far],
+    }
+    middle = stages.index(channel)
+
+    def run(t, first, end_at):
+        for lag in range(first, end_at):
+            since = t - lag
+
+            @pl.when((since >= 0) & (since < 2 * PROMPTS) & (lax.rem(t + lag, 2) == 0))
             def _():
-                stage(step - lag)
+                stages[lag](lax.div(since, 2))
+
+    @pl.loop(0, 2 * PROMPTS + len(stages) - 2)
+    def _(t):
+        run(t, 0, middle)
+        for at, works in beside.items():
+
+            @pl.when(t == at)
+            def _():
+                for work in works:
+                    if callable(work):
+                        work()
+                    else:
+                        next(work, end)
+
+        run(t, middle, len(stages))
 
     @pl.loop(0, PROMPTS)
     def _(m):
-        for copy in sums(m) + hops(m):
+        for copy in sums(m):
             copy.wait_send()
+        for prompt_ring in (att_ring, mid_ring, out_ring):
+            prompt_ring.sent(m)
 
         @pl.when(q != c)
         def _():
@@ -971,11 +920,14 @@
 
         turn(m, 1).wait_send()
 
-    pltpu.make_async_copy(state, final, recv_sem.at[n_ring]).wait()
+    pltpu.make_async_copy(state, final, recv_sem.at[N_TURN]).wait()
 
     @pl.when(q != c)
     def _():
         move_state.wait_send()
+
+    for copy in links.copies + far_links.copies:
+        copy.wait_send()
 
 
 def per_device(
@@ -1014,77 +966,39 @@
             pltpu.VMEM(channel_mix_shards.shape, BF16),
         ],
     )
-    rkv, low = compute(
-        mix_kernel,
-        [((3, MINE, SLICE), F32), ((2, MINE, lowrank_down.shape[2]), F32)],
-        (hx, parg, token_shift_weights, wt, lowrank_down.transpose(0, 2, 1)),
-        flops=4 * 10**9,
-    )
-    mid, state, wkg, wng = exchange(
-        attend_kernel,
-        [
-            ((2, MINE, FEAT), BF16),
-            ((PROMPTS, 2, HEAD, FEAT), BF16),
-            ((N_COL, N_ROW, 16, MINE), BF16),
-            ((N_ROW, N_COL, 3, 16, SLICE), BF16),
-        ],
-        PROMPTS * HOPS + 2 + 14 + 2 * RING,
-        2,
-        2,
-        lengths,
-        rkv,
-        low,
-        attention_coefficients,
-        lowrank_up,
-        hx,
-        w3,
-        wk,
-        wn,
-        scratch=[
-            pltpu.VMEM((2, MINE, FEAT), BF16),
-            pltpu.VMEM((N_ROW + 2, MINE, FEAT), BF16),
-            pltpu.VMEM((N_COL, 16, WIDTH), BF16),
-        ],
-        in_specs=[pl.BlockSpec(memory_space=pltpu.SMEM)] + [VMEM] * 4 + [ANY, VMEM, ANY, ANY],
-        out_specs=[VMEM, VMEM, ANY, ANY],
-    )
-    midg, wvg, theirs = exchange(
-        mid_kernel,
-        [
-            ((N_ROW, MINE, FEAT), BF16),
-            ((N_COL, N_ROW, 16, MINE), BF16),
-            ((2, N_ROW, N_COL, 16, MINE), BF16),
-        ],
-        9 + 14 + 2 * RING,
-        2,
-        3,
-        mid,
-        wk,
-        wkg,
-        wv,
-    )
+    lowrank = lowrank_down.shape[2]
     out_hidden, next_rkv, final = exchange(
-        tail_kernel,
+        body_kernel,
         [
             ((2 * MINE, FEAT), BF16),
             ((3, MINE, SLICE), BF16),
             ((PROMPTS, 2, HEAD, FEAT), BF16),
         ],
-        PROMPTS * (N_ROW - 1) + 2 * PROMPTS + PROMPTS * HOPS + 1,
-        17,
-        4,
-        midg,
+        N_ALL,
+        3,
+        2,
+        lengths,
+        hx,
         parg,
         token_shift_weights,
+        wt,
+        lowrank_down.transpose(0, 2, 1),
+        attention_coefficients,
+        lowrank_up,
+        w3,
         wk,
-        wkg,
         wv,
-        wvg,
-        theirs,
-        mid,
-        wng,
-        state,
+        wn,
         scratch=[
+            pltpu.VMEM((3, LMAX, SLICE), F32),
+            pltpu.VMEM((2, LMAX, lowrank), F32),
+            pltpu.VMEM((PROMPTS, 2, HEAD, FEAT), BF16),
+            pltpu.VMEM((2, MINE, FEAT), BF16),
+            pltpu.VMEM((N_ROW, MINE, FEAT), BF16),
+            pltpu.VMEM((N_COL, 16, WIDTH), BF16),
+            pltpu.VMEM((2, MINE, FEAT), BF16),
+            pltpu.VMEM((N_ROW, MINE, FEAT), BF16),
+            pltpu.VMEM((2, N_ROW, N_COL, 16, MINE), BF16),
             pltpu.VMEM((2, N_ROW, N_COL, 16, MINE), BF16),
             pltpu.VMEM((2, LMAX, MINE), BF16),
             pltpu.VMEM((N_ROW, MINE, FEAT), BF16),
@@ -1092,7 +1006,7 @@
             pltpu.VMEM((N_ROW, MINE, FEAT), BF16),
             pltpu.VMEM((N_ROW, N_COL, 3, 16, SLICE), BF16),
         ],
-        in_specs=[VMEM] * 3 + [ANY] * 4 + [VMEM] * 2 + [ANY] * 2,
+        in_specs=[pl.BlockSpec(memory_space=pltpu.SMEM)] + [VMEM] * 8 + [ANY] * 3,
         out_specs=[VMEM, VMEM, ANY],
     )
     final = final.reshape(4, 2, HEAD, 2, HEAD).transpose(0, 1, 3, 2, 4).astype(F32)

time: 196 us -> 185 us (0.944)
  Pallas kernels: 190 us -> 179 us
    pallas_call x1 -> x0, Pallas kernels: 8.26 us -> none  [compute(): pl.pallas_call(kernel, grid=grid if grid is not None else (), out_shape=[...]
    pallas_call x4 -> x2, Pallas kernels: 182 us -> 179 us  [exchange(): pl.pallas_call(kernel, out_shape=[jax.ShapeDtypeStruct(*out) for out in o...]
where the time goes in v7:
time: 185 us; the launch traced here: 183 us
  Pallas kernels  179 us (97%)
  local copies, waits for them, and re-layouts  3.87 us (2%)
    pallas_call x2, Pallas kernels, exchange(): pl.pallas_call(kernel, out_shape=[jax.ShapeDtypeStruct(*out) for out in o...  179 us

profile of v7, /device:TPU:1, one launch (start us, length us, event | category | flops | bytes accessed | tf_op | source)
XLA Modules:
  0.0 183.4 jit_solution(6617934451209555004)
XLA Ops:
  0.6 41.0 %shard_map.112 = (bf16[16,512,128]{2,1,0:T(8,128)(2,1)}, bf16[2,3,16,8,16,128]{5,4,3,2,1,0:T(8,128)(2,1)}, bf16[8,16,2048]{2,1,0:T(8,128)(2,1)}, bf16[8,16,16,51...) custom-call(f32[7,16,2048]{2,1,0:T(8,128)} %square_in.1, ...), custom_call_target="tpu_custom_call" | custom-call | bytes 50331648 | tf_op jit(solution)/shard_map/pallas_call | solution.py:71
  41.7 137.8 %shard_map.113 = (bf16[1024,128]{1,0:T(8,128)(2,1)}, bf16[3,512,256]{2,1,0:T(8,128)(2,1)}, bf16[4,2,64,128]{3,2,1,0:T(8,128)(2,1)}) custom-call(s32[64]{0:T(128)} %lens.1, bf16[16,512,128]{2,1,0:T(8,128)(2,1)} %get-tuple-element.13.hx, f32[16,6,128]{2,1,0:T(8,128)} %get-tuple-element.14.par, f32[9,2048]{1,0:T(8,128)} %shift.1, ...), custom_call_target="tpu_custom_call" | custom-call | bytes 50331648 | tf_op jit(solution)/shard_map/pallas_call | solution.py:71
  179.5 0.0 copy-start.1
  179.5 0.0 copy-start
  179.5 1.3 reshape.21
  180.9 0.9 reshape.18
  181.8 0.0 copy-done.1
  181.8 0.7 copy.15
  182.5 0.0 copy-done
  182.5 0.9 copy.16
  (1 shorter events, 0.0 us)
Async XLA Ops:
  179.5 2.3 %copy-start.1 = (bf16[1024,128]{1,0:T(8,128)(2,1)S(1)}, bf16[1024,128]{1,0:T(8,128)(2,1)}, u32[]{:S(2)}) copy-start(bf16[1024,128]{1,0:T(8,128)(2,1)} %get-tuple-element.26) | copy-start | bytes 786436
  179.5 3.0 %copy-start = (bf16[3,512,256]{2,1,0:T(8,128)(2,1)S(1)}, bf16[3,512,256]{2,1,0:T(8,128)(2,1)}, u32[]{:S(2)}) copy-start(bf16[3,512,256]{2,1,0:T(8,128)(2,1)} %get-tuple-element.27) | copy-start | bytes 2359300

commit v8 on v7

--- a/solution.py
+++ b/solution.py
@@ -306,22 +306,39 @@
         own_time[0].wait()
         yield
 
+    nexts = []
+
+    def next_slot(chip, half):
+        return wn.at[2 * chip + h, pl.ds(4 * half, 4)]
+
+    def next_seen(chip, half):
+        links.go(lambda: next_slot(chip, half), lambda: next_slot(chip, half), (sibling, c))
+
+    def next_ready(k):
+        if k == 0:
+            for copy in nexts:
+                links.arrive(copy)
+            own_next[0].wait()
+            links.go(wn.at[r], wn.at[r], (sibling, c))
+
+    own_next = []
+
     def rest():
         local.extend(
             [
                 keep(square.at[3], w3.at[c], local_sem.at[3]),
                 keep(key_part(r), wk.at[c, r], local_sem.at[4]),
                 keep(value_part(r), wv.at[c, r], local_sem.at[5]),
-                keep(next_part(c), wn.at[r, c], local_sem.at[6]),
             ]
         )
+        own_next.append(keep(next_part(c), wn.at[r, c], local_sem.at[6]))
+        for p in cols:
+            nexts.append(links.go(next_part(p), wn.at[r, c], (r, p)))
         for p in rows:
             links.go(par, parg.at[r], (p, c))
         yield
         for p in rows:
             links.go(key_part(p), wk.at[c, r], (p, c))
-        for p in cols:
-            links.go(next_part(p), wn.at[r, c], (r, p))
         for p in rows:
             links.go(value_part(p), wv.at[c, r], (p, c))
 
@@ -339,6 +356,7 @@
         ring(links, "col", time_slot, ready=time_ready, seen=time_seen),
         rest(),
         ring(links, "col", out_slot, own=out_own),
+        ring(links, "row", next_slot, ready=next_ready, seen=next_seen),
     )
     links.finish()
     for copy in local:
@@ -507,6 +525,7 @@
         self.here, self.chips, self.to = ring_at(axis)
         self.own = own
         self.got = got
+        self.heavy = axis == "row"
 
     def hop(self, m, slot, chip, side, half=None):
         def block():
@@ -538,8 +557,8 @@
             self.hop(m, 4, "p", "m", 1),
             self.hop(m, 5, "z", "p"),
             self.hop(m, 6, "z", "m"),
-            self.hop(m, 7, "o", "z", 0),
-            self.hop(m, 8, "o", "z", 1),
+            self.hop(m, 7, "o", "z", 0) if self.heavy else self.hop(m, 7, "mz", "p", 0),
+            self.hop(m, 8, "o", "z", 1) if self.heavy else self.hop(m, 8, "pz", "m", 1),
         ]
 
     def begin(self, m):
@@ -559,13 +578,12 @@
 
     def close(self, m):
         copies = self.hops(m)
-        copies[3].wait_recv()
-        copies[7].start()
-        copies[4].wait_recv()
-        copies[8].start()
+        for early, late in ((3, 7), (4, 8)) if self.heavy else ((6, 8), (5, 7)):
+            copies[early].wait_recv()
+            copies[late].start()
 
     def last(self, m):
-        for k in (5, 6, 7, 8):
+        for k in (5, 6, 7, 8) if self.heavy else (3, 4, 7, 8):
             self.hops(m)[k].wait_recv()
 
     def sent(self, m):
@@ -573,11 +591,11 @@
             copy.wait_send()
 
 
-N_SUM = PROMPTS * (N_ROW - 1)
+N_SUM = PROMPTS * 6
 N_TURN = N_SUM + 2 * PROMPTS
 N_STATE = N_TURN + 1
 N_WEIGHT = N_STATE + 3 * PROMPTS * HOPS
-N_ALL = N_WEIGHT + 1 + 2 * (1 + 14 + RING) + 1 + 14 + RING
+N_ALL = N_WEIGHT + 1 + 2 * (1 + 14 + RING)
 
 
 def body_kernel(
@@ -612,17 +630,20 @@
     act_scr,
     part,
     got,
+    summed,
+    fin,
     nx,
     wng,
 ):
     r, c, h, q, sibling = place()
-    rows = [lax.rem(r + d, N_ROW) for d in range(1, N_ROW)]
+    x_here = lax.div(r, 4)
+    z_row = 4 * x_here + 2 * (1 - lax.rem(q, 2))
 
     def local():
         return [
             pltpu.make_async_copy(wk.at[c], held.at[0, :, c], local_sem.at[0]),
             pltpu.make_async_copy(wv.at[c], held.at[1, :, c], local_sem.at[1]),
-            pltpu.make_async_copy(wn.at[r], wng.at[r], local_sem.at[2]),
+            pltpu.make_async_copy(wn, wng, local_sem.at[2]),
         ]
 
     for copy in local():
@@ -632,7 +653,8 @@
         return (2 * c + lax.rem(h + i, 2), q)
 
     barrier = pltpu.get_barrier_semaphore()
-    peers = [(p, c) for p in rows] + ring_peers("col")
+    peers = [(lax.rem(r + 4 * d, N_ROW), c) for d in range(1, 4)] + ring_peers("col")
+    peers += [(sibling, c), (z_row, c), (z_row + 1, c)]
 
     @pl.when(q != c)
     def _():
@@ -671,30 +693,8 @@
 
         return begin()
 
-    def weight_slot(chip, half):
-        return wng.at[2 * chip + h, pl.ds(4 * half, 4)]
-
-    far_links = Links(send_sem, recv_sem, N_ALL - 1 - 14 - RING)
-
-    def weight_seen(chip, half):
-        far_links.go(
-            lambda: weight_slot(chip, half), lambda: weight_slot(chip, half), (sibling, c)
-        )
-
-    def weight_ring():
-        far_links.go(lambda: wn.at[r], lambda: wng.at[r], (sibling, c))
-        yield from ring(
-            far_links,
-            "row",
-            weight_slot,
-            own=lambda k: wn.at[r, pl.ds(4 * k, 4)],
-            seen=weight_seen,
-        )
-
     keys = mlp_ring(0, wk)
     values = mlp_ring(1, wv)
-    weights = weight_ring()
-    next(weights)
     next(keys)
 
     att_ring = PromptRing(send_sem, recv_sem, N_STATE, "row", att, attg)
@@ -740,18 +740,31 @@
             midg[r - h + side, tokens, :] = block
         mid_ring.begin(m)
 
-    def sums(m):
-        def copy_of(i, p):
+    def first_sums(m):
+        def copy_of(d):
+            x_there = lax.rem(x_here + d, 4)
             return Copy(
-                lambda: part.at[p, aligned(m, LMAX)],
-                lambda: got.at[r, aligned(m, LMAX)],
+                lambda: part.at[pl.ds(4 * x_there, 4), aligned(m, LMAX)],
+                lambda: got.at[pl.ds(4 * x_here, 4), aligned(m, LMAX)],
                 send_sem,
                 recv_sem,
-                m * (N_ROW - 1) + i,
-                (p, c),
+                6 * m + d - 1,
+                (lax.rem(r + 4 * d, N_ROW), c),
             )
 
-        return [copy_of(i, p) for i, p in enumerate(rows)]
+        return [copy_of(d) for d in range(1, 4)]
+
+    def plane_move(m, k):
+        there = sibling if k == 0 else z_row + k - 1
+        own_k = 0 if k == 0 else 1 + h
+        return pltpu.make_async_remote_copy(
+            src_ref=summed.at[there - 4 * x_here, aligned(m, LMAX)],
+            dst_ref=fin.at[(0 if k == 0 else 2) + h, aligned(m, LMAX)],
+            send_sem=send_sem.at[6 * m + 3 + k],
+            recv_sem=recv_sem.at[6 * m + 3 + own_k],
+            device_id=(there, c),
+            device_id_type=MESH,
+        )
 
     def channel(m):
         mid_ring.last(m)
@@ -775,9 +788,23 @@
                     total[:, side * FEAT : (side + 1) * FEAT] + added
                 ).astype(BF16)
 
-        for copy in sums(m):
+        for copy in first_sums(m):
             copy.start()
-        got[r, tokens, :] = part[r, tokens, :]
+        for k in range(4):
+            got[4 * x_here + k, tokens, :] = part[4 * x_here + k, tokens, :]
+
+    def plane_sum(m):
+        for copy in first_sums(m):
+            copy.wait_recv()
+        tokens = aligned(m, LMAX)
+        for k in range(4):
+            total = got[k, tokens, :].astype(F32)
+            for x in range(1, 4):
+                total += got[4 * x + k, tokens, :].astype(F32)
+            summed[k, tokens, :] = total.astype(BF16)
+        for k in (1, 2, 0):
+            plane_move(m, k).start()
+        fin[h, tokens, :] = summed[r - 4 * x_here, tokens, :]
 
     def source_rows(m, i):
         return pl.ds(pl.multiple_of(lax.rem(h + i, 2) * MINE + m * LMAX, LMAX), LMAX)
@@ -793,13 +820,12 @@
         )
 
     def add_up(m):
-        for copy in sums(m):
-            copy.wait_recv()
         tokens = aligned(m, LMAX)
+        for k in range(3):
+            block = fin.at[0, tokens]
+            pltpu.make_async_copy(block, block, recv_sem.at[6 * m + 3 + k]).wait()
         for side in range(2):
-            total = got[side, tokens, :].astype(F32)
-            for k in range(1, N_CHIP):
-                total += got[2 * k + side, tokens, :].astype(F32)
+            total = fin[side, tokens, :].astype(F32) + fin[2 + side, tokens, :].astype(F32)
             rows_m = pl.ds(pl.multiple_of(side * MINE + m * LMAX, LMAX), LMAX)
             out[rows_m, :] = total.astype(BF16)
 
@@ -842,6 +868,7 @@
         mid_ring.forward,
         mid_ring.close,
         channel,
+        plane_sum,
         add_up,
         spread,
         out_ring.forward,
@@ -851,7 +878,7 @@
     end = object()
 
     def wait_mlp():
-        for copy in local():
+        for copy in local()[:2]:
             copy.wait()
         for copy in links.open:
             copy.wait_recv()
@@ -867,20 +894,17 @@
             move_state.start()
 
     def wait_far():
-        for copy in far_links.open:
-            copy.wait_recv()
-        far_links.open = []
+        local()[2].wait()
 
     beside = {
-        1: [weights, keys],
+        1: [keys],
         2: [keys, values],
-        3: [weights, keys, values, lambda: links.arrive(links.copies[0])],
+        3: [keys, values, lambda: links.arrive(links.copies[0])],
         4: [keys, values],
-        5: [weights, values],
+        5: [values],
         6: [values],
         7: [send_state, wait_mlp],
-        8: [weights],
-        12: [wait_far],
+        13: [wait_far],
     }
     middle = stages.index(channel)
 
@@ -909,8 +933,10 @@
 
     @pl.loop(0, PROMPTS)
     def _(m):
-        for copy in sums(m):
+        for copy in first_sums(m):
             copy.wait_send()
+        for k in range(3):
+            plane_move(m, k).wait_send()
         for prompt_ring in (att_ring, mid_ring, out_ring):
             prompt_ring.sent(m)
 
@@ -926,7 +952,7 @@
     def _():
         move_state.wait_send()
 
-    for copy in links.copies + far_links.copies:
+    for copy in links.copies:
         copy.wait_send()
 
 
@@ -952,7 +978,7 @@
             ((N_ROW, N_COL, 3, 16, SLICE), BF16),
             ((N_ROW, 6, FEAT), F32),
         ],
-        15 + 1 + 3 * RING + 1 + 14 + 15 + 15 + 7 + 15,
+        15 + 1 + 4 * RING + 2 * (1 + 14) + 15 + 15 + 7 + 15,
         9,
         1,
         square_matrix_shards,
@@ -1003,6 +1029,8 @@
             pltpu.VMEM((2, LMAX, MINE), BF16),
             pltpu.VMEM((N_ROW, MINE, FEAT), BF16),
             pltpu.VMEM((N_ROW, MINE, FEAT), BF16),
+            pltpu.VMEM((4, MINE, FEAT), BF16),
+            pltpu.VMEM((4, MINE, FEAT), BF16),
             pltpu.VMEM((N_ROW, MINE, FEAT), BF16),
             pltpu.VMEM((N_ROW, N_COL, 3, 16, SLICE), BF16),
         ],

time: 185 us -> 198 us (1.070)
  Pallas kernels: 179 us -> 191 us
    pallas_call x2, Pallas kernels: 179 us -> 191 us  [exchange(): pl.pallas_call(kernel, out_shape=[jax.ShapeDtypeStruct(*out) for out in o...]
where the time goes in v8:
time: 198 us; the launch traced here: 196 us
  Pallas kernels  191 us (96%)
  local copies, waits for them, and re-layouts  3.87 us (2%)
    pallas_call x2, Pallas kernels, exchange(): pl.pallas_call(kernel, out_shape=[jax.ShapeDtypeStruct(*out) for out in o...  191 us

profile of v8, /device:TPU:1, one launch (start us, length us, event | category | flops | bytes accessed | tf_op | source)
XLA Modules:
  0.0 195.8 jit_solution(7875973347754126685)
XLA Ops:
  0.6 56.6 %shard_map.112 = (bf16[16,512,128]{2,1,0:T(8,128)(2,1)}, bf16[2,3,16,8,16,128]{5,4,3,2,1,0:T(8,128)(2,1)}, bf16[8,16,2048]{2,1,0:T(8,128)(2,1)}, bf16[8,16,16,51...) custom-call(f32[7,16,2048]{2,1,0:T(8,128)} %square_in.1, ...), custom_call_target="tpu_custom_call" | custom-call | bytes 50331648 | tf_op jit(solution)/shard_map/pallas_call | solution.py:71
  57.2 134.6 %shard_map.113 = (bf16[1024,128]{1,0:T(8,128)(2,1)}, bf16[3,512,256]{2,1,0:T(8,128)(2,1)}, bf16[4,2,64,128]{3,2,1,0:T(8,128)(2,1)}) custom-call(s32[64]{0:T(128)} %lens.1, bf16[16,512,128]{2,1,0:T(8,128)(2,1)} %get-tuple-element.13.hx, f32[16,6,128]{2,1,0:T(8,128)} %get-tuple-element.14.par, f32[9,2048]{1,0:T(8,128)} %shift.1, ...), custom_call_target="tpu_custom_call" | custom-call | bytes 50331648 | tf_op jit(solution)/shard_map/pallas_call | solution.py:71
  191.9 0.0 copy-start.1
  191.9 0.0 copy-start
  191.9 1.3 reshape.21
  193.2 0.9 reshape.18
  194.2 0.0 copy-done.1
  194.2 0.7 copy.15
  194.9 0.0 copy-done
  194.9 0.9 copy.16
  (1 shorter events, 0.0 us)
Async XLA Ops:
  191.9 2.3 %copy-start.1 = (bf16[1024,128]{1,0:T(8,128)(2,1)S(1)}, bf16[1024,128]{1,0:T(8,128)(2,1)}, u32[]{:S(2)}) copy-start(bf16[1024,128]{1,0:T(8,128)(2,1)} %get-tuple-element.26) | copy-start | bytes 786436
  191.9 3.0 %copy-start = (bf16[3,512,256]{2,1,0:T(8,128)(2,1)S(1)}, bf16[3,512,256]{2,1,0:T(8,128)(2,1)}, u32[]{:S(2)}) copy-start(bf16[3,512,256]{2,1,0:T(8,128)(2,1)} %get-tuple-element.27) | copy-start | bytes 2359300

commit v9 on v7

--- a/solution.py
+++ b/solution.py
@@ -632,7 +632,7 @@
         return (2 * c + lax.rem(h + i, 2), q)
 
     barrier = pltpu.get_barrier_semaphore()
-    peers = [(p, c) for p in rows] + ring_peers("col")
+    peers = [(p, c) for p in rows] + [(r, lax.rem(c + d, N_COL)) for d in range(1, N_COL)]
 
     @pl.when(q != c)
     def _():
@@ -694,12 +694,23 @@
     keys = mlp_ring(0, wk)
     values = mlp_ring(1, wv)
     weights = weight_ring()
-    next(weights)
-    next(keys)
+    for steps in (weights, keys, values):
+        next(steps)
 
     att_ring = PromptRing(send_sem, recv_sem, N_STATE, "row", att, attg)
     mid_ring = PromptRing(send_sem, recv_sem, N_STATE + PROMPTS * HOPS, "row", mid, midg)
-    out_ring = PromptRing(send_sem, recv_sem, N_STATE + 2 * PROMPTS * HOPS, "col", None, nx)
+    cols = [lax.rem(c + d, N_COL) for d in range(1, N_COL)]
+
+    def out_sends(m):
+        def copy_of(k, p):
+            def block():
+                return nx.at[pl.ds(2 * c, 2), aligned(m, LMAX)]
+
+            at = N_STATE + (2 * PROMPTS + m) * HOPS + k
+            return Copy(block, block, send_sem, recv_sem, at, (r, p))
+
+        return [copy_of(k, p) for k, p in enumerate(cols)]
+
     move_state = Copy(state, final, send_sem, recv_sem, N_TURN, target(0))
 
     def wide(ref, m):
@@ -722,6 +733,7 @@
                 low[j - 3] = dot(blend, down[j - 3], ((1,), (1,)))
 
     def core(m):
+        blends(m)
         one_prompt(m, lens, rkv, low, coef, up, att, state)
         att_ring.begin(m)
         for side in range(2):
@@ -821,10 +833,12 @@
         for k in range(2):
             block = nx.at[2 * c + k, aligned(m, LMAX)]
             pltpu.make_async_copy(block, block, recv_sem.at[N_SUM + 2 * m + k]).wait()
-        out_ring.begin(m)
+        for copy in out_sends(m):
+            copy.start()
 
     def project_next(m):
-        out_ring.last(m)
+        for copy in out_sends(m):
+            copy.wait_recv()
         z = normed(nx, m, 4)
         dz = step_back(z)
         for j in range(3):
@@ -834,7 +848,6 @@
             ).astype(BF16)
 
     stages = (
-        blends,
         core,
         att_ring.forward,
         att_ring.close,
@@ -844,8 +857,6 @@
         channel,
         add_up,
         spread,
-        out_ring.forward,
-        out_ring.close,
         project_next,
     )
     end = object()
@@ -872,29 +883,22 @@
         far_links.open = []
 
     beside = {
-        1: [weights, keys],
-        2: [keys, values],
-        3: [weights, keys, values, lambda: links.arrive(links.copies[0])],
-        4: [keys, values],
-        5: [weights, values],
-        6: [values],
-        7: [send_state, wait_mlp],
-        8: [weights],
-        12: [wait_far],
+        0: [weights, keys, values, weights, keys, values],
+        2: [weights, keys, values, lambda: links.arrive(links.copies[0])],
+        3: [send_state],
+        4: [weights, keys, values],
+        5: [wait_mlp],
+        8: [wait_far],
     }
-    middle = stages.index(channel)
-
-    def run(t, first, end_at):
-        for lag in range(first, end_at):
-            since = t - lag
-
-            @pl.when((since >= 0) & (since < 2 * PROMPTS) & (lax.rem(t + lag, 2) == 0))
+
+    @pl.loop(0, PROMPTS + len(stages) - 1)
+    def _(t):
+        for lag, stage in enumerate(stages):
+
+            @pl.when((t >= lag) & (t < PROMPTS + lag))
             def _():
-                stages[lag](lax.div(since, 2))
-
-    @pl.loop(0, 2 * PROMPTS + len(stages) - 2)
-    def _(t):
-        run(t, 0, middle)
+                stage(t - lag)
+
         for at, works in beside.items():
 
             @pl.when(t == at)
@@ -905,13 +909,11 @@
                     else:
                         next(work, end)
 
-        run(t, middle, len(stages))
-
     @pl.loop(0, PROMPTS)
     def _(m):
-        for copy in sums(m):
+        for copy in sums(m) + out_sends(m):
             copy.wait_send()
-        for prompt_ring in (att_ring, mid_ring, out_ring):
+        for prompt_ring in (att_ring, mid_ring):
             prompt_ring.sent(m)
 
         @pl.when(q != c)

time: 185 us -> 180 us (0.973)
  Pallas kernels: 179 us -> 173 us
    pallas_call x2, Pallas kernels: 179 us -> 173 us  [exchange(): pl.pallas_call(kernel, out_shape=[jax.ShapeDtypeStruct(*out) for out in o...]
where the time goes in v9:
time: 180 us; the launch traced here: 178 us
  Pallas kernels  173 us (96%)
  local copies, waits for them, and re-layouts  3.87 us (2%)
    pallas_call x2, Pallas kernels, exchange(): pl.pallas_call(kernel, out_shape=[jax.ShapeDtypeStruct(*out) for out in o...  173 us

profile of v9, /device:TPU:1, one launch (start us, length us, event | category | flops | bytes accessed | tf_op | source)
XLA Modules:
  0.0 178.0 jit_solution(17162421934269760161)
XLA Ops:
  0.6 41.0 %shard_map.112 = (bf16[16,512,128]{2,1,0:T(8,128)(2,1)}, bf16[2,3,16,8,16,128]{5,4,3,2,1,0:T(8,128)(2,1)}, bf16[8,16,2048]{2,1,0:T(8,128)(2,1)}, bf16[8,16,16,51...) custom-call(f32[7,16,2048]{2,1,0:T(8,128)} %square_in.1, ...), custom_call_target="tpu_custom_call" | custom-call | bytes 50331648 | tf_op jit(solution)/shard_map/pallas_call | solution.py:71
  41.7 132.4 %shard_map.113 = (bf16[1024,128]{1,0:T(8,128)(2,1)}, bf16[3,512,256]{2,1,0:T(8,128)(2,1)}, bf16[4,2,64,128]{3,2,1,0:T(8,128)(2,1)}) custom-call(s32[64]{0:T(128)} %lens.1, bf16[16,512,128]{2,1,0:T(8,128)(2,1)} %get-tuple-element.13.hx, f32[16,6,128]{2,1,0:T(8,128)} %get-tuple-element.14.par, f32[9,2048]{1,0:T(8,128)} %shift.1, ...), custom_call_target="tpu_custom_call" | custom-call | bytes 50331648 | tf_op jit(solution)/shard_map/pallas_call | solution.py:71
  174.1 0.0 copy-start.1
  174.1 0.0 copy-start
  174.1 1.3 reshape.21
  175.4 0.9 reshape.18
  176.4 0.0 copy-done.1
  176.4 0.7 copy.15
  177.1 0.0 copy-done
  177.1 0.9 copy.16
  (1 shorter events, 0.0 us)
Async XLA Ops:
  174.1 2.3 %copy-start.1 = (bf16[1024,128]{1,0:T(8,128)(2,1)S(1)}, bf16[1024,128]{1,0:T(8,128)(2,1)}, u32[]{:S(2)}) copy-start(bf16[1024,128]{1,0:T(8,128)(2,1)} %get-tuple-element.26) | copy-start | bytes 786436
  174.1 3.0 %copy-start = (bf16[3,512,256]{2,1,0:T(8,128)(2,1)S(1)}, bf16[3,512,256]{2,1,0:T(8,128)(2,1)}, u32[]{:S(2)}) copy-start(bf16[3,512,256]{2,1,0:T(8,128)(2,1)} %get-tuple-element.27) | copy-start | bytes 2359300

commit v10 on v9

--- a/solution.py
+++ b/solution.py
@@ -507,6 +507,7 @@
         self.here, self.chips, self.to = ring_at(axis)
         self.own = own
         self.got = got
+        self.heavy = axis == "row"
 
     def hop(self, m, slot, chip, side, half=None):
         def block():
@@ -538,8 +539,8 @@
             self.hop(m, 4, "p", "m", 1),
             self.hop(m, 5, "z", "p"),
             self.hop(m, 6, "z", "m"),
-            self.hop(m, 7, "o", "z", 0),
-            self.hop(m, 8, "o", "z", 1),
+            self.hop(m, 7, "o", "z", 0) if self.heavy else self.hop(m, 7, "mz", "p", 0),
+            self.hop(m, 8, "o", "z", 1) if self.heavy else self.hop(m, 8, "pz", "m", 1),
         ]
 
     def begin(self, m):
@@ -559,13 +560,12 @@
 
     def close(self, m):
         copies = self.hops(m)
-        copies[3].wait_recv()
-        copies[7].start()
-        copies[4].wait_recv()
-        copies[8].start()
+        for early, late in ((3, 7), (4, 8)) if self.heavy else ((6, 8), (5, 7)):
+            copies[early].wait_recv()
+            copies[late].start()
 
     def last(self, m):
-        for k in (5, 6, 7, 8):
+        for k in (5, 6, 7, 8) if self.heavy else (3, 4, 7, 8):
             self.hops(m)[k].wait_recv()
 
     def sent(self, m):
@@ -573,7 +573,7 @@
             copy.wait_send()
 
 
-N_SUM = PROMPTS * (N_ROW - 1)
+N_SUM = PROMPTS * 9
 N_TURN = N_SUM + 2 * PROMPTS
 N_STATE = N_TURN + 1
 N_WEIGHT = N_STATE + 3 * PROMPTS * HOPS
@@ -612,11 +612,15 @@
     act_scr,
     part,
     got,
+    summed,
+    fin,
     nx,
     wng,
 ):
     r, c, h, q, sibling = place()
-    rows = [lax.rem(r + d, N_ROW) for d in range(1, N_ROW)]
+    x_here = lax.div(r, 4)
+    x_plus, x_over, x_minus = (lax.rem(x_here + d, 4) for d in range(1, 4))
+    z_row = 4 * x_here + 2 * (1 - lax.rem(q, 2))
 
     def local():
         return [
@@ -632,7 +636,8 @@
         return (2 * c + lax.rem(h + i, 2), q)
 
     barrier = pltpu.get_barrier_semaphore()
-    peers = [(p, c) for p in rows] + [(r, lax.rem(c + d, N_COL)) for d in range(1, N_COL)]
+    peers = [(lax.rem(r + 4, N_ROW), c), (lax.rem(r + 12, N_ROW), c)] + ring_peers("col")
+    peers += [(sibling, c), (z_row, c), (z_row + 1, c)]
 
     @pl.when(q != c)
     def _():
@@ -689,6 +694,7 @@
             weight_slot,
             own=lambda k: wn.at[r, pl.ds(4 * k, 4)],
             seen=weight_seen,
+            heavy=False,
         )
 
     keys = mlp_ring(0, wk)
@@ -699,18 +705,7 @@
 
     att_ring = PromptRing(send_sem, recv_sem, N_STATE, "row", att, attg)
     mid_ring = PromptRing(send_sem, recv_sem, N_STATE + PROMPTS * HOPS, "row", mid, midg)
-    cols = [lax.rem(c + d, N_COL) for d in range(1, N_COL)]
-
-    def out_sends(m):
-        def copy_of(k, p):
-            def block():
-                return nx.at[pl.ds(2 * c, 2), aligned(m, LMAX)]
-
-            at = N_STATE + (2 * PROMPTS + m) * HOPS + k
-            return Copy(block, block, send_sem, recv_sem, at, (r, p))
-
-        return [copy_of(k, p) for k, p in enumerate(cols)]
-
+    out_ring = PromptRing(send_sem, recv_sem, N_STATE + 2 * PROMPTS * HOPS, "col", None, nx)
     move_state = Copy(state, final, send_sem, recv_sem, N_TURN, target(0))
 
     def wide(ref, m):
@@ -752,18 +747,36 @@
             midg[r - h + side, tokens, :] = block
         mid_ring.begin(m)
 
-    def sums(m):
-        def copy_of(i, p):
-            return Copy(
-                lambda: part.at[p, aligned(m, LMAX)],
-                lambda: got.at[r, aligned(m, LMAX)],
-                send_sem,
-                recv_sem,
-                m * (N_ROW - 1) + i,
-                (p, c),
-            )
-
-        return [copy_of(i, p) for i, p in enumerate(rows)]
+    def x_move(m, k):
+        tokens = aligned(m, LMAX)
+        source, first, target_at, step = (
+            (part, 4 * x_over, 0, 4),
+            (part, 4 * x_over + 2, 2, 12),
+            (part, 4 * x_plus + 2, 6, 4),
+            (part, 4 * x_minus, 8, 12),
+            (got, 12, 4, 4),
+            (got, 14, 10, 12),
+        )[k]
+        return pltpu.make_async_remote_copy(
+            src_ref=source.at[pl.ds(first, 2), tokens],
+            dst_ref=got.at[pl.ds(target_at, 2), tokens],
+            send_sem=send_sem.at[9 * m + k],
+            recv_sem=recv_sem.at[9 * m + k],
+            device_id=(lax.rem(r + step, N_ROW), c),
+            device_id_type=MESH,
+        )
+
+    def plane_move(m, k):
+        there = sibling if k == 0 else z_row + k - 1
+        own_k = 0 if k == 0 else 1 + h
+        return pltpu.make_async_remote_copy(
+            src_ref=summed.at[there - 4 * x_here, aligned(m, LMAX)],
+            dst_ref=fin.at[(0 if k == 0 else 2) + h, aligned(m, LMAX)],
+            send_sem=send_sem.at[9 * m + 6 + k],
+            recv_sem=recv_sem.at[9 * m + 6 + own_k],
+            device_id=(there, c),
+            device_id_type=MESH,
+        )
 
     def channel(m):
         mid_ring.last(m)
@@ -787,9 +800,32 @@
                     total[:, side * FEAT : (side + 1) * FEAT] + added
                 ).astype(BF16)
 
-        for copy in sums(m):
-            copy.start()
-        got[r, tokens, :] = part[r, tokens, :]
+        for k in range(4):
+            x_move(m, k).start()
+
+    def relay(m):
+        tokens = aligned(m, LMAX)
+        for k, other in enumerate((x_plus, x_minus)):
+            x_move(m, k).wait_recv()
+            for j in range(2):
+                added = part[4 * other + 2 * k + j, tokens, :].astype(F32)
+                got[12 + 2 * k + j, tokens, :] = (
+                    got[2 * k + j, tokens, :].astype(F32) + added
+                ).astype(BF16)
+            x_move(m, 4 + k).start()
+
+    def plane_sum(m):
+        tokens = aligned(m, LMAX)
+        for k in range(2, 6):
+            x_move(m, k).wait_recv()
+        for k, places in enumerate(((4, 8), (5, 9), (10, 6), (11, 7))):
+            total = part[4 * x_here + k, tokens, :].astype(F32)
+            for j in places:
+                total += got[j, tokens, :].astype(F32)
+            summed[k, tokens, :] = total.astype(BF16)
+        for k in (1, 2, 0):
+            plane_move(m, k).start()
+        fin[h, tokens, :] = summed[r - 4 * x_here, tokens, :]
 
     def source_rows(m, i):
         return pl.ds(pl.multiple_of(lax.rem(h + i, 2) * MINE + m * LMAX, LMAX), LMAX)
@@ -805,13 +841,12 @@
         )
 
     def add_up(m):
-        for copy in sums(m):
-            copy.wait_recv()
         tokens = aligned(m, LMAX)
+        for k in range(3):
+            block = fin.at[0, tokens]
+            pltpu.make_async_copy(block, block, recv_sem.at[9 * m + 6 + k]).wait()
         for side in range(2):
-            total = got[side, tokens, :].astype(F32)
-            for k in range(1, N_CHIP):
-                total += got[2 * k + side, tokens, :].astype(F32)
+            total = fin[side, tokens, :].astype(F32) + fin[2 + side, tokens, :].astype(F32)
             rows_m = pl.ds(pl.multiple_of(side * MINE + m * LMAX, LMAX), LMAX)
             out[rows_m, :] = total.astype(BF16)
 
@@ -833,12 +868,10 @@
         for k in range(2):
             block = nx.at[2 * c + k, aligned(m, LMAX)]
             pltpu.make_async_copy(block, block, recv_sem.at[N_SUM + 2 * m + k]).wait()
-        for copy in out_sends(m):
-            copy.start()
+        out_ring.begin(m)
 
     def project_next(m):
-        for copy in out_sends(m):
-            copy.wait_recv()
+        out_ring.last(m)
         z = normed(nx, m, 4)
         dz = step_back(z)
         for j in range(3):
@@ -855,8 +888,12 @@
         mid_ring.forward,
         mid_ring.close,
         channel,
+        relay,
+        plane_sum,
         add_up,
         spread,
+        out_ring.forward,
+        out_ring.close,
         project_next,
     )
     end = object()
@@ -888,7 +925,7 @@
         3: [send_state],
         4: [weights, keys, values],
         5: [wait_mlp],
-        8: [wait_far],
+        12: [wait_far],
     }
 
     @pl.loop(0, PROMPTS + len(stages) - 1)
@@ -911,9 +948,11 @@
 
     @pl.loop(0, PROMPTS)
     def _(m):
-        for copy in sums(m) + out_sends(m):
-            copy.wait_send()
-        for prompt_ring in (att_ring, mid_ring):
+        for k in range(6):
+            x_move(m, k).wait_send()
+        for k in range(3):
+            plane_move(m, k).wait_send()
+        for prompt_ring in (att_ring, mid_ring, out_ring):
             prompt_ring.sent(m)
 
         @pl.when(q != c)
@@ -1005,6 +1044,8 @@
             pltpu.VMEM((2, LMAX, MINE), BF16),
             pltpu.VMEM((N_ROW, MINE, FEAT), BF16),
             pltpu.VMEM((N_ROW, MINE, FEAT), BF16),
+            pltpu.VMEM((4, MINE, FEAT), BF16),
+            pltpu.VMEM((4, MINE, FEAT), BF16),
             pltpu.VMEM((N_ROW, MINE, FEAT), BF16),
             pltpu.VMEM((N_ROW, N_COL, 3, 16, SLICE), BF16),
         ],

time: 180 us -> 175 us (0.972)
  Pallas kernels: 173 us -> 170 us
    pallas_call x2, Pallas kernels: 173 us -> 170 us  [exchange(): pl.pallas_call(kernel, out_shape=[jax.ShapeDtypeStruct(*out) for out in o...]
where the time goes in v10:
time: 175 us; the launch traced here: 174 us
  Pallas kernels  170 us (97%)
  local copies, waits for them, and re-layouts  3.87 us (2%)
    pallas_call x2, Pallas kernels, exchange(): pl.pallas_call(kernel, out_shape=[jax.ShapeDtypeStruct(*out) for out in o...  170 us

profile of v10, /device:TPU:1, one launch (start us, length us, event | category | flops | bytes accessed | tf_op | source)
XLA Modules:
  0.0 174.4 jit_solution(5046654567565033904)
XLA Ops:
  0.6 41.0 %shard_map.112 = (bf16[16,512,128]{2,1,0:T(8,128)(2,1)}, bf16[2,3,16,8,16,128]{5,4,3,2,1,0:T(8,128)(2,1)}, bf16[8,16,2048]{2,1,0:T(8,128)(2,1)}, bf16[8,16,16,51...) custom-call(f32[7,16,2048]{2,1,0:T(8,128)} %square_in.1, ...), custom_call_target="tpu_custom_call" | custom-call | bytes 50331648 | tf_op jit(solution)/shard_map/pallas_call | solution.py:71
  41.7 128.8 %shard_map.113 = (bf16[1024,128]{1,0:T(8,128)(2,1)}, bf16[3,512,256]{2,1,0:T(8,128)(2,1)}, bf16[4,2,64,128]{3,2,1,0:T(8,128)(2,1)}) custom-call(s32[64]{0:T(128)} %lens.1, bf16[16,512,128]{2,1,0:T(8,128)(2,1)} %get-tuple-element.13.hx, f32[16,6,128]{2,1,0:T(8,128)} %get-tuple-element.14.par, f32[9,2048]{1,0:T(8,128)} %shift.1, ...), custom_call_target="tpu_custom_call" | custom-call | bytes 50331648 | tf_op jit(solution)/shard_map/pallas_call | solution.py:71
  170.5 0.0 copy-start.1
  170.5 0.0 copy-start
  170.5 1.3 reshape.21
  171.9 0.9 reshape.18
  172.8 0.0 copy-done.1
  172.8 0.7 copy.15
  173.5 0.0 copy-done
  173.5 0.9 copy.16
  (1 shorter events, 0.0 us)
Async XLA Ops:
  170.5 2.3 %copy-start.1 = (bf16[1024,128]{1,0:T(8,128)(2,1)S(1)}, bf16[1024,128]{1,0:T(8,128)(2,1)}, u32[]{:S(2)}) copy-start(bf16[1024,128]{1,0:T(8,128)(2,1)} %get-tuple-element.26) | copy-start | bytes 786436
  170.5 3.0 %copy-start = (bf16[3,512,256]{2,1,0:T(8,128)(2,1)S(1)}, bf16[3,512,256]{2,1,0:T(8,128)(2,1)}, u32[]{:S(2)}) copy-start(bf16[3,512,256]{2,1,0:T(8,128)(2,1)} %get-tuple-element.27) | copy-start | bytes 2359300

commit v11 on v10

--- a/solution.py
+++ b/solution.py
@@ -357,7 +357,9 @@
 def dot3(a, b, dims=((1,), (0,))):
     a_high, a_low = a
     b_high, b_low = b
-    return dot(a_high, b_high, dims) + (dot(a_high, b_low, dims) + dot(a_low, b_high, dims))
+    left = jnp.concatenate([a_high, a_high, a_low], axis=dims[0][0])
+    right = jnp.concatenate([b_high, b_low, b_high], axis=dims[1][0])
+    return dot(left, right, dims)
 
 
 def norm(source, gain, bias):
@@ -920,11 +922,13 @@
         far_links.open = []
 
     beside = {
-        0: [weights, keys, values, weights, keys, values],
-        2: [weights, keys, values, lambda: links.arrive(links.copies[0])],
-        3: [send_state],
-        4: [weights, keys, values],
-        5: [wait_mlp],
+        0: [keys, values],
+        1: [keys, values, weights, weights],
+        2: [lambda: links.arrive(links.copies[0])],
+        3: [keys, values, send_state],
+        4: [weights],
+        5: [keys, values, wait_mlp],
+        6: [weights],
         12: [wait_far],
     }
 

time: 175 us -> 176 us (level)
  no operation moved by 1% of the time
where the time goes in v11:
time: 176 us; the launch traced here: 175 us
  Pallas kernels  170 us (97%)
  local copies, waits for them, and re-layouts  3.87 us (2%)
    pallas_call x2, Pallas kernels, exchange(): pl.pallas_call(kernel, out_shape=[jax.ShapeDtypeStruct(*out) for out in o...  170 us

profile of v11, /device:TPU:1, one launch (start us, length us, event | category | flops | bytes accessed | tf_op | source)
XLA Modules:
  0.0 174.6 jit_solution(17632460601072779303)
XLA Ops:
  0.6 41.0 %shard_map.112 = (bf16[16,512,128]{2,1,0:T(8,128)(2,1)}, bf16[2,3,16,8,16,128]{5,4,3,2,1,0:T(8,128)(2,1)}, bf16[8,16,2048]{2,1,0:T(8,128)(2,1)}, bf16[8,16,16,51...) custom-call(f32[7,16,2048]{2,1,0:T(8,128)} %square_in.1, ...), custom_call_target="tpu_custom_call" | custom-call | bytes 50331648 | tf_op jit(solution)/shard_map/pallas_call | solution.py:71
  41.7 129.0 %shard_map.113 = (bf16[1024,128]{1,0:T(8,128)(2,1)}, bf16[3,512,256]{2,1,0:T(8,128)(2,1)}, bf16[4,2,64,128]{3,2,1,0:T(8,128)(2,1)}) custom-call(s32[64]{0:T(128)} %lens.1, bf16[16,512,128]{2,1,0:T(8,128)(2,1)} %get-tuple-element.13.hx, f32[16,6,128]{2,1,0:T(8,128)} %get-tuple-element.14.par, f32[9,2048]{1,0:T(8,128)} %shift.1, ...), custom_call_target="tpu_custom_call" | custom-call | bytes 50331648 | tf_op jit(solution)/shard_map/pallas_call | solution.py:71
  170.7 0.0 copy-start.1
  170.7 0.0 copy-start
  170.7 1.3 reshape.21
  172.1 0.9 reshape.18
  173.0 0.0 copy-done.1
  173.0 0.7 copy.15
  173.7 0.0 copy-done
  173.7 0.9 copy.16
  (1 shorter events, 0.0 us)
Async XLA Ops:
  170.7 2.3 %copy-start.1 = (bf16[1024,128]{1,0:T(8,128)(2,1)S(1)}, bf16[1024,128]{1,0:T(8,128)(2,1)}, u32[]{:S(2)}) copy-start(bf16[1024,128]{1,0:T(8,128)(2,1)} %get-tuple-element.26) | copy-start | bytes 786436
  170.7 3.0 %copy-start = (bf16[3,512,256]{2,1,0:T(8,128)(2,1)S(1)}, bf16[3,512,256]{2,1,0:T(8,128)(2,1)}, u32[]{:S(2)}) copy-start(bf16[3,512,256]{2,1,0:T(8,128)(2,1)} %get-tuple-element.27) | copy-start | bytes 2359300

commit v12 on v11

--- a/solution.py
+++ b/solution.py
@@ -357,9 +357,7 @@
 def dot3(a, b, dims=((1,), (0,))):
     a_high, a_low = a
     b_high, b_low = b
-    left = jnp.concatenate([a_high, a_high, a_low], axis=dims[0][0])
-    right = jnp.concatenate([b_high, b_low, b_high], axis=dims[1][0])
-    return dot(left, right, dims)
+    return dot(a_high, b_high, dims) + (dot(a_high, b_low, dims) + dot(a_low, b_high, dims))
 
 
 def norm(source, gain, bias):

time: 176 us -> 172 us (0.977)
  Pallas kernels: 170 us -> 166 us
    pallas_call x2, Pallas kernels: 170 us -> 166 us  [exchange(): pl.pallas_call(kernel, out_shape=[jax.ShapeDtypeStruct(*out) for out in o...]
where the time goes in v12:
time: 172 us; the launch traced here: 170 us
  Pallas kernels  166 us (97%)
  local copies, waits for them, and re-layouts  3.87 us (2%)
    pallas_call x2, Pallas kernels, exchange(): pl.pallas_call(kernel, out_shape=[jax.ShapeDtypeStruct(*out) for out in o...  166 us

profile of v12, /device:TPU:1, one launch (start us, length us, event | category | flops | bytes accessed | tf_op | source)
XLA Modules:
  0.0 170.5 jit_solution(17714055052906467021)
XLA Ops:
  0.6 41.0 %shard_map.112 = (bf16[16,512,128]{2,1,0:T(8,128)(2,1)}, bf16[2,3,16,8,16,128]{5,4,3,2,1,0:T(8,128)(2,1)}, bf16[8,16,2048]{2,1,0:T(8,128)(2,1)}, bf16[8,16,16,51...) custom-call(f32[7,16,2048]{2,1,0:T(8,128)} %square_in.1, ...), custom_call_target="tpu_custom_call" | custom-call | bytes 50331648 | tf_op jit(solution)/shard_map/pallas_call | solution.py:71
  41.7 124.9 %shard_map.113 = (bf16[1024,128]{1,0:T(8,128)(2,1)}, bf16[3,512,256]{2,1,0:T(8,128)(2,1)}, bf16[4,2,64,128]{3,2,1,0:T(8,128)(2,1)}) custom-call(s32[64]{0:T(128)} %lens.1, bf16[16,512,128]{2,1,0:T(8,128)(2,1)} %get-tuple-element.13.hx, f32[16,6,128]{2,1,0:T(8,128)} %get-tuple-element.14.par, f32[9,2048]{1,0:T(8,128)} %shift.1, ...), custom_call_target="tpu_custom_call" | custom-call | bytes 50331648 | tf_op jit(solution)/shard_map/pallas_call | solution.py:71
  166.6 0.0 copy-start.1
  166.6 0.0 copy-start
  166.6 1.3 reshape.21
  167.9 0.9 reshape.18
  168.9 0.0 copy-done.1
  168.9 0.7 copy.15
  169.6 0.0 copy-done
  169.6 0.9 copy.16
  (1 shorter events, 0.0 us)
Async XLA Ops:
  166.6 2.3 %copy-start.1 = (bf16[1024,128]{1,0:T(8,128)(2,1)S(1)}, bf16[1024,128]{1,0:T(8,128)(2,1)}, u32[]{:S(2)}) copy-start(bf16[1024,128]{1,0:T(8,128)(2,1)} %get-tuple-element.26) | copy-start | bytes 786436
  166.6 3.0 %copy-start = (bf16[3,512,256]{2,1,0:T(8,128)(2,1)S(1)}, bf16[3,512,256]{2,1,0:T(8,128)(2,1)}, u32[]{:S(2)}) copy-start(bf16[3,512,256]{2,1,0:T(8,128)(2,1)} %get-tuple-element.27) | copy-start | bytes 2359300
